TPU v7x, 32 devices: a whole 2x2x4 slice. The times are simulated.
32 devices in a mesh: group: 2 (over x), replica: 16 (over z, y, core).
Axes of the slice: x: 2, y: 2, z: 4, core: 2. Of those that a mesh axis runs over, the one named last changes fastest.
Arguments:
- images: bfloat16 [4, 64, 197, 384], P(None, ('group', 'replica')), may hold values from -6 to 6
- image_count: int32 [4, 32], P(None, ('group', 'replica')), may hold values from 1 to 2, as said below
- cotangent: bfloat16 [4, 64, 197, 384], P(None, ('group', 'replica')), may hold values from -6 to 6
- w_qkv: bfloat16 [384, 1152], P('group'), may hold values from -0.3125 to 0.3125
- b_qv: bfloat16 [768], P('group'), may hold values from -3 to 3
- w_out: bfloat16 [384, 384], P('group'), may hold values from -0.875 to 0.875
- b_out: bfloat16 [384], P('group'), may hold values from -3 to 3
- w_fc1: bfloat16 [384, 1536], P('group'), may hold values from -0.3125 to 0.3125
- b_fc1: bfloat16 [1536], P('group'), may hold values from -3 to 3
- w_fc2: bfloat16 [1536, 384], P('group'), may hold values from -0.15625 to 0.15625
- b_fc2: bfloat16 [384], P('group'), may hold values from -3 to 3
- gain_one: bfloat16 [384], P('group'), may hold values from 0.25 to 1.75
- shift_one: bfloat16 [384], P('group'), may hold values from -3 to 3
- gain_two: bfloat16 [384], P('group'), may hold values from 0.25 to 1.75
- shift_two: bfloat16 [384], P('group'), may hold values from -3 to 3
Outputs:
- outputs: bfloat16 [4, 64, 197, 384], P(None, ('group', 'replica'))
- input_grad: bfloat16 [4, 64, 197, 384], P(None, ('group', 'replica'))
- grad_w_qkv: float32 [384, 1152], P('group')
- grad_b_qv: float32 [768], P('group')
- grad_w_out: float32 [384, 384], P('group')
- grad_b_out: float32 [384], P('group')
- grad_w_fc1: float32 [384, 1536], P('group')
- grad_b_fc1: float32 [1536], P('group')
- grad_w_fc2: float32 [1536, 384], P('group')
- grad_b_fc2: float32 [384], P('group')
- grad_gain_one: float32 [384], P('group')
- grad_shift_one: float32 [384], P('group')
- grad_gain_two: float32 [384], P('group')
- grad_shift_two: float32 [384], P('group')
Inputs may be any that keep to these rules, and one draw needn't show every extreme that they name: image_count[m, d] is the number of images in slots 2 d and 2 d + 1 of micro-batch m; slot 2 d always holds one, slot 2 d + 1 only where the entry is 2; each micro-batch has devices with 1 and with 2.
All inputs are finite; a program needn't handle non-finite values.
Results may differ from a plain program's by a relative error of at most 0.012.
Values may be sent and summed in bfloat16 or wider, within the bound.
No kernel may reach another device: no remote copies, remote signals or barrier semaphores. Data moves between devices by JAX's collectives and lax.ppermute only.
A program may use at most 128 MiB of HBM per device.

v0:
```python
from functools import partial

import jax
import jax.numpy as jnp
from jax import lax
from jax.sharding import PartitionSpec as P

HEADS = 6


def layer_norm(values, gain, shift):
    center = values - jnp.mean(values, axis=-1, keepdims=True)
    spread = jnp.mean(center * center, axis=-1, keepdims=True)
    return center * lax.rsqrt(spread + 1e-06) * gain + shift


def forward(params, tokens, valid_row, lse_kept):
    (
        w_qkv,
        b_qv,
        w_out,
        b_out,
        w_fc1,
        b_fc1,
        w_fc2,
        b_fc2,
        gain_one,
        shift_one,
        gain_two,
        shift_two,
    ) = params
    count, length, width = tokens.shape
    head_size = width // HEADS
    normed = layer_norm(tokens, gain_one.astype(jnp.float32), shift_one.astype(jnp.float32)).astype(
        jnp.bfloat16
    )
    joined = jnp.einsum("bsd,de->bse", normed, w_qkv, preferred_element_type=jnp.float32)
    bias_half = b_qv.astype(jnp.float32)
    bias = jnp.concatenate([bias_half[:width], jnp.zeros((width,), jnp.float32), bias_half[width:]])
    joined_low = (joined + bias).astype(jnp.bfloat16)
    query = joined_low[..., :width].reshape(count, length, HEADS, head_size)
    keys = joined_low[..., width : 2 * width].reshape(count, length, HEADS, head_size)
    values = joined_low[..., 2 * width :].reshape(count, length, HEADS, head_size)
    scores = jnp.einsum(
        "bqhe,bkhe->bhqk", query, keys, preferred_element_type=jnp.float32
    ) * head_size ** (-0.5)
    if lse_kept is None:
        lse = jax.nn.logsumexp(scores, axis=-1)
    else:
        lse = lse_kept
    prob = jnp.exp(scores - lse[..., None])
    prob_low = prob.astype(jnp.bfloat16)
    attended = jnp.einsum("bhqk,bkhe->bqhe", prob_low, values, preferred_element_type=jnp.float32)
    attended = attended.reshape(count, length, width).astype(jnp.bfloat16)
    middle = (
        tokens
        + jnp.einsum("bsd,de->bse", attended, w_out, preferred_element_type=jnp.float32)
        + b_out.astype(jnp.float32)
    )
    normed_two = layer_norm(
        middle, gain_two.astype(jnp.float32), shift_two.astype(jnp.float32)
    ).astype(jnp.bfloat16)
    pre = jnp.einsum(
        "bsd,df->bsf", normed_two, w_fc1, preferred_element_type=jnp.float32
    ) + b_fc1.astype(jnp.float32)
    act = jax.nn.gelu(pre, approximate=False).astype(jnp.bfloat16)
    mlp = jnp.einsum("bsf,fd->bsd", act, w_fc2, preferred_element_type=jnp.float32) + b_fc2.astype(
        jnp.float32
    )
    result = (middle + mlp) * valid_row[:, None, None]
    kept = (normed, joined_low, prob, prob_low, attended, middle, normed_two, pre, act)
    return (result, lse, kept)


def backward(params, tokens, cot_slot, valid_row, lse_kept):
    (
        w_qkv,
        b_qv,
        w_out,
        b_out,
        w_fc1,
        b_fc1,
        w_fc2,
        b_fc2,
        gain_one,
        shift_one,
        gain_two,
        shift_two,
    ) = params
    count, length, width = tokens.shape
    head_size = width // HEADS
    unused, unused_lse, kept = forward(params, tokens, valid_row, lse_kept)
    normed, joined_low, prob, prob_low, attended, middle, normed_two, pre, act = kept
    d_out = cot_slot.astype(jnp.float32) * valid_row[:, None, None]
    d_mlp = d_out.astype(jnp.bfloat16)
    grad_b_fc2 = jnp.sum(d_mlp.astype(jnp.float32), axis=(0, 1))
    grad_w_fc2 = jnp.einsum("bsf,bsd->fd", act, d_mlp, preferred_element_type=jnp.float32)
    d_act = jnp.einsum("bsd,fd->bsf", d_mlp, w_fc2, preferred_element_type=jnp.float32)
    unused_gelu, gelu_back = jax.vjp(partial(jax.nn.gelu, approximate=False), pre)
    d_pre = gelu_back(d_act)[0].astype(jnp.bfloat16)
    grad_b_fc1 = jnp.sum(d_pre.astype(jnp.float32), axis=(0, 1))
    grad_w_fc1 = jnp.einsum("bsd,bsf->df", normed_two, d_pre, preferred_element_type=jnp.float32)
    d_normed_two = jnp.einsum("bsf,df->bsd", d_pre, w_fc1, preferred_element_type=jnp.float32)
    unused_two, norm_two_back = jax.vjp(
        layer_norm, middle, gain_two.astype(jnp.float32), shift_two.astype(jnp.float32)
    )
    d_middle_norm, grad_gain_two, grad_shift_two = norm_two_back(d_normed_two)
    d_middle = d_out + d_middle_norm
    d_attn = d_middle.astype(jnp.bfloat16)
    grad_b_out = jnp.sum(d_attn.astype(jnp.float32), axis=(0, 1))
    grad_w_out = jnp.einsum("bsd,bse->de", attended, d_attn, preferred_element_type=jnp.float32)
    d_attended = jnp.einsum(
        "bse,de->bsd", d_attn, w_out, preferred_element_type=jnp.float32
    ).astype(jnp.bfloat16)
    d_heads = d_attended.reshape(count, length, HEADS, head_size)
    query = joined_low[..., :width].reshape(count, length, HEADS, head_size)
    keys = joined_low[..., width : 2 * width].reshape(count, length, HEADS, head_size)
    values = joined_low[..., 2 * width :].reshape(count, length, HEADS, head_size)
    d_values = jnp.einsum("bhqk,bqhe->bkhe", prob_low, d_heads, preferred_element_type=jnp.float32)
    d_prob = jnp.einsum("bqhe,bkhe->bhqk", d_heads, values, preferred_element_type=jnp.float32)
    d_scores = prob * (d_prob - jnp.sum(prob * d_prob, axis=-1, keepdims=True))
    d_scores = d_scores.astype(jnp.bfloat16)
    scale = head_size ** (-0.5)
    d_query = (
        jnp.einsum("bhqk,bkhe->bqhe", d_scores, keys, preferred_element_type=jnp.float32) * scale
    )
    d_keys = (
        jnp.einsum("bhqk,bqhe->bkhe", d_scores, query, preferred_element_type=jnp.float32) * scale
    )
    d_joined = jnp.concatenate(
        [
            d_query.reshape(count, length, width),
            d_keys.reshape(count, length, width),
            d_values.reshape(count, length, width),
        ],
        axis=-1,
    ).astype(jnp.bfloat16)
    joined_sums = jnp.sum(d_joined.astype(jnp.float32), axis=(0, 1))
    grad_b_qv = jnp.concatenate([joined_sums[:width], joined_sums[2 * width :]])
    grad_w_qkv = jnp.einsum("bsd,bse->de", normed, d_joined, preferred_element_type=jnp.float32)
    d_normed = jnp.einsum("bse,de->bsd", d_joined, w_qkv, preferred_element_type=jnp.float32)
    unused_one, norm_one_back = jax.vjp(
        layer_norm, tokens, gain_one.astype(jnp.float32), shift_one.astype(jnp.float32)
    )
    d_tokens_norm, grad_gain_one, grad_shift_one = norm_one_back(d_normed)
    d_tokens = (d_middle + d_tokens_norm).astype(jnp.bfloat16)
    grads = (
        grad_w_qkv,
        grad_b_qv,
        grad_w_out,
        grad_b_out,
        grad_w_fc1,
        grad_b_fc1,
        grad_w_fc2,
        grad_b_fc2,
        grad_gain_one,
        grad_shift_one,
        grad_gain_two,
        grad_shift_two,
    )
    return (d_tokens, grads)


def local(
    images,
    image_count,
    cotangent,
    w_qkv,
    b_qv,
    w_out,
    b_out,
    w_fc1,
    b_fc1,
    w_fc2,
    b_fc2,
    gain_one,
    shift_one,
    gain_two,
    shift_two,
):
    gathered = (
        lax.all_gather(w_qkv, "group", axis=0, tiled=True),
        lax.all_gather(b_qv, "group", axis=0, tiled=True),
        lax.all_gather(w_out, "group", axis=0, tiled=True),
        lax.all_gather(b_out, "group", axis=0, tiled=True),
        lax.all_gather(w_fc1, "group", axis=0, tiled=True),
        lax.all_gather(b_fc1, "group", axis=0, tiled=True),
        lax.all_gather(w_fc2, "group", axis=0, tiled=True),
        lax.all_gather(b_fc2, "group", axis=0, tiled=True),
        lax.all_gather(gain_one, "group", axis=0, tiled=True),
        lax.all_gather(shift_one, "group", axis=0, tiled=True),
        lax.all_gather(gain_two, "group", axis=0, tiled=True),
        lax.all_gather(shift_two, "group", axis=0, tiled=True),
    )
    valid = (jnp.arange(2, dtype=jnp.int32)[None, :] < image_count).astype(jnp.float32)

    def forward_step(carry, item):
        result, lse, unused = forward(gathered, item[0].astype(jnp.float32), item[1], None)
        return (carry, (result.astype(jnp.bfloat16), lse))

    unused_carry, (outputs, lse_all) = lax.scan(
        forward_step, jnp.zeros((), jnp.float32), (images, valid)
    )
    back_params = (
        lax.all_gather(w_qkv, "group", axis=0, tiled=True),
        lax.all_gather(b_qv, "group", axis=0, tiled=True),
        lax.all_gather(w_out, "group", axis=0, tiled=True),
        lax.all_gather(b_out, "group", axis=0, tiled=True),
        lax.all_gather(w_fc1, "group", axis=0, tiled=True),
        lax.all_gather(b_fc1, "group", axis=0, tiled=True),
        lax.all_gather(w_fc2, "group", axis=0, tiled=True),
        lax.all_gather(b_fc2, "group", axis=0, tiled=True),
        lax.all_gather(gain_one, "group", axis=0, tiled=True),
        lax.all_gather(shift_one, "group", axis=0, tiled=True),
        lax.all_gather(gain_two, "group", axis=0, tiled=True),
        lax.all_gather(shift_two, "group", axis=0, tiled=True),
    )
    totals_init = jax.tree.map(
        lambda whole: jnp.zeros(whole.shape, jnp.float32), tuple(back_params)
    )

    def backward_step(totals, item):
        d_tokens, grads = backward(
            back_params, item[0].astype(jnp.float32), item[1], item[2], item[3]
        )
        return (jax.tree.map(lambda left, right: left + right, totals, grads), d_tokens)

    totals, input_grad = lax.scan(backward_step, totals_init, (images, cotangent, valid, lse_all))
    g_qkv, g_bqv, g_out, g_bout, g_fc1, g_bfc1, g_fc2, g_bfc2, g_gone, g_sone, g_gtwo, g_stwo = (
        totals
    )
    shares = (
        lax.psum_scatter(
            g_qkv.astype(jnp.bfloat16), "group", scatter_dimension=0, tiled=True
        ).astype(jnp.float32),
        lax.psum_scatter(
            g_bqv.astype(jnp.bfloat16), "group", scatter_dimension=0, tiled=True
        ).astype(jnp.float32),
        lax.psum_scatter(
            g_out.astype(jnp.bfloat16), "group", scatter_dimension=0, tiled=True
        ).astype(jnp.float32),
        lax.psum_scatter(
            g_bout.astype(jnp.bfloat16), "group", scatter_dimension=0, tiled=True
        ).astype(jnp.float32),
        lax.psum_scatter(
            g_fc1.astype(jnp.bfloat16), "group", scatter_dimension=0, tiled=True
        ).astype(jnp.float32),
        lax.psum_scatter(
            g_bfc1.astype(jnp.bfloat16), "group", scatter_dimension=0, tiled=True
        ).astype(jnp.float32),
        lax.psum_scatter(
            g_fc2.astype(jnp.bfloat16), "group", scatter_dimension=0, tiled=True
        ).astype(jnp.float32),
        lax.psum_scatter(
            g_bfc2.astype(jnp.bfloat16), "group", scatter_dimension=0, tiled=True
        ).astype(jnp.float32),
        lax.psum_scatter(
            g_gone.astype(jnp.bfloat16), "group", scatter_dimension=0, tiled=True
        ).astype(jnp.float32),
        lax.psum_scatter(
            g_sone.astype(jnp.bfloat16), "group", scatter_dimension=0, tiled=True
        ).astype(jnp.float32),
        lax.psum_scatter(
            g_gtwo.astype(jnp.bfloat16), "group", scatter_dimension=0, tiled=True
        ).astype(jnp.float32),
        lax.psum_scatter(
            g_stwo.astype(jnp.bfloat16), "group", scatter_dimension=0, tiled=True
        ).astype(jnp.float32),
    )
    final = lax.psum(tuple(shares), "replica")
    return (
        outputs,
        input_grad,
        final[0],
        final[1],
        final[2],
        final[3],
        final[4],
        final[5],
        final[6],
        final[7],
        final[8],
        final[9],
        final[10],
        final[11],
    )


def solution(mesh):
    return jax.shard_map(
        local,
        mesh=mesh,
        in_specs=(
            P(None, ("group", "replica"), None, None),
            P(None, ("group", "replica")),
            P(None, ("group", "replica"), None, None),
            P("group", None),
            P("group"),
            P("group", None),
            P("group"),
            P("group", None),
            P("group"),
            P("group", None),
            P("group"),
            P("group"),
            P("group"),
            P("group"),
            P("group"),
        ),
        out_specs=(
            P(None, ("group", "replica"), None, None),
            P(None, ("group", "replica"), None, None),
            P("group", None),
            P("group"),
            P("group", None),
            P("group"),
            P("group", None),
            P("group"),
            P("group", None),
            P("group"),
            P("group"),
            P("group"),
            P("group"),
            P("group"),
        ),
        check_vma=False,
    )
```

profile of v0, /device:TPU:1, one launch (start us, length us, event | category | flops | bytes accessed | tf_op | source)
XLA Modules:
  0.0 485.4 jit_solution(1518654650898223087)
XLA Ops:
  9.6 3.7 all-gather
  21.7 4.5 all-reduce.16
  26.2 8.7 %all_gather.51 = bf16[384,384]{1,0:T(8,128)(2,1)S(1)} all-gather(bf16[192,384]{1,0:T(8,128)(2,1)S(1)} %copy-done.21), channel_id=1, replica_groups=mesh['group'=2,'replica'=16] {'group'}, dimensions={0}, use_global_device_ids=true | all-gather | bytes 442368 | tf_op jit(solution)/shard_map/all_gather | solution.py:184
  34.8 9.5 %all_gather.49 = bf16[384,1152]{1,0:T(8,128)(2,1)} all-gather(bf16[192,1152]{1,0:T(8,128)(2,1)S(1)} %copy-done.20), channel_id=1, replica_groups=mesh['group'=2,'replica'=16] {'group'}, dimensions={0}, use_global_device_ids=true | all-gather | bytes 1327104 | tf_op jit(solution)/shard_map/all_gather | solution.py:182
  44.4 17.1 %all-gather.7.cloned.1.call-done = bf16[1536,384]{1,0:T(8,128)(2,1)} async-done(((bf16[768,384]{1,0:T(8,128)(2,1)}), bf16[1536,384]{1,0:T(8,128)(2,1)}) %all-gather.7.cloned.1.call-update) | async-done | bytes 1179664 | tf_op jit(solution)/shard_map/all_gather | solution.py:188
  63.1 58.6 %while.47 = (s32[]{:T(128)}, bf16[4,2,197,384]{3,1,2,0:T(2,128)(2,1)}, f32[4,2,6,197]{3,2,1,0:T(8,128)S(1)}, bf16[4,2,197,384]{3,2,1,0:T(8,128)(2,1)S(1)}, bf16[...) while((s32[]{:T(128)}, ...), condition=%wide.region_7.8_spmd, body=%wide.region_0.7_spmd.sunk | while | flops 1572842240 | bytes 35440164 | solution.py:201
  70.1 6.7 %fusion.250 = bf16[1,2,197,384]{3,2,1,0:T(8,128)(2,1)S(1)} fusion(f32[2,197,384]{2,1,0:T(8,128)S(1)} %get-tuple-element.1026, f32[2,197,1536]{2,1,0:T(8,128)S(1)} %get-tuple-element.1028, bf16[1536,384]{1,0:T(8,128)(2,1)S(1)} %copy-done.33, u8[197,1536]{1,0:T(8,128)(4,1)S(1)} %get-tuple-element.1029, u8[197,1536]{1,0:T(8,128)(4,1)S(1)} %get-tuple-element.1030, ...), kind=kOutput, calls=%fused_computation.37.clone.1 | convolution fusion | flops 507749376 | bytes 5114888 | tf_op jit(solution)/shard_map/while/body/eval_jaxpr/bsf,fd->bsd/dot_general | solution.py:67
  84.8 6.7 %fusion.250 = bf16[1,2,197,384]{3,2,1,0:T(8,128)(2,1)S(1)} fusion(f32[2,197,384]{2,1,0:T(8,128)S(1)} %get-tuple-element.1026, f32[2,197,1536]{2,1,0:T(8,128)S(1)} %get-tuple-element.1028, bf16[1536,384]{1,0:T(8,128)(2,1)S(1)} %copy-done.33, u8[197,1536]{1,0:T(8,128)(4,1)S(1)} %get-tuple-element.1029, u8[197,1536]{1,0:T(8,128)(4,1)S(1)} %get-tuple-element.1030, ...), kind=kOutput, calls=%fused_computation.37.clone.1 | convolution fusion | flops 507749376 | bytes 5114888 | tf_op jit(solution)/shard_map/while/body/eval_jaxpr/bsf,fd->bsd/dot_general | solution.py:67
  99.4 6.7 %fusion.250 = bf16[1,2,197,384]{3,2,1,0:T(8,128)(2,1)S(1)} fusion(f32[2,197,384]{2,1,0:T(8,128)S(1)} %get-tuple-element.1026, f32[2,197,1536]{2,1,0:T(8,128)S(1)} %get-tuple-element.1028, bf16[1536,384]{1,0:T(8,128)(2,1)S(1)} %copy-done.33, u8[197,1536]{1,0:T(8,128)(4,1)S(1)} %get-tuple-element.1029, u8[197,1536]{1,0:T(8,128)(4,1)S(1)} %get-tuple-element.1030, ...), kind=kOutput, calls=%fused_computation.37.clone.1 | convolution fusion | flops 507749376 | bytes 5114888 | tf_op jit(solution)/shard_map/while/body/eval_jaxpr/bsf,fd->bsd/dot_general | solution.py:67
  114.1 6.7 %fusion.250 = bf16[1,2,197,384]{3,2,1,0:T(8,128)(2,1)S(1)} fusion(f32[2,197,384]{2,1,0:T(8,128)S(1)} %get-tuple-element.1026, f32[2,197,1536]{2,1,0:T(8,128)S(1)} %get-tuple-element.1028, bf16[1536,384]{1,0:T(8,128)(2,1)S(1)} %copy-done.33, u8[197,1536]{1,0:T(8,128)(4,1)S(1)} %get-tuple-element.1029, u8[197,1536]{1,0:T(8,128)(4,1)S(1)} %get-tuple-element.1030, ...), kind=kOutput, calls=%fused_computation.37.clone.1 | convolution fusion | flops 507749376 | bytes 5114888 | tf_op jit(solution)/shard_map/while/body/eval_jaxpr/bsf,fd->bsd/dot_general | solution.py:67
  123.4 182.7 %while.48 = (s32[]{:T(128)}, f32[384,1152]{1,0:T(8,128)}, f32[768]{0:T(1024)S(1)}, f32[384,384]{1,0:T(8,128)}, f32[384]{0:T(512)}, /*index=5*/f32[384,1536]{1,0:...) while((s32[]{:T(128)}, f32[384,1152]{1,0:T(8,128)}, ...), condition=%wide.region_26.27_spmd.clone, body=%wide.region_8.26_spmd.clone.sunk | while | flops 4168837632 | bytes 162929808 | solution.py:228
  134.6 5.4 %fusion.283 = f32[2,197,1536]{2,1,0:T(8,128)S(1)} fusion(f32[2,197,1536]{2,1,0:T(8,128)S(1)} %get-tuple-element.1067, u8[197,1536]{1,0:T(8,128)(4,1)S(1)} %get-tuple-element.1068, u8[197,1536]{1,0:T(8,128)(4,1)S(1)} %get-tuple-element.1069), kind=kLoop, calls=%fused_computation.123.clone.1 | loop fusion | flops 40547328 | bytes 5446656 | tf_op jit(solution)/shard_map/while/body/eval_jaxpr/jvp()/erfc | solution.py:99
  155.4 3.7 fusion.294
  179.8 5.4 %fusion.283 = f32[2,197,1536]{2,1,0:T(8,128)S(1)} fusion(f32[2,197,1536]{2,1,0:T(8,128)S(1)} %get-tuple-element.1067, u8[197,1536]{1,0:T(8,128)(4,1)S(1)} %get-tuple-element.1068, u8[197,1536]{1,0:T(8,128)(4,1)S(1)} %get-tuple-element.1069), kind=kLoop, calls=%fused_computation.123.clone.1 | loop fusion | flops 40547328 | bytes 5446656 | tf_op jit(solution)/shard_map/while/body/eval_jaxpr/jvp()/erfc | solution.py:99
  200.6 4.5 fusion.294
  225.6 5.4 %fusion.283 = f32[2,197,1536]{2,1,0:T(8,128)S(1)} fusion(f32[2,197,1536]{2,1,0:T(8,128)S(1)} %get-tuple-element.1067, u8[197,1536]{1,0:T(8,128)(4,1)S(1)} %get-tuple-element.1068, u8[197,1536]{1,0:T(8,128)(4,1)S(1)} %get-tuple-element.1069), kind=kLoop, calls=%fused_computation.123.clone.1 | loop fusion | flops 40547328 | bytes 5446656 | tf_op jit(solution)/shard_map/while/body/eval_jaxpr/jvp()/erfc | solution.py:99
  246.4 4.5 fusion.294
  271.5 5.4 %fusion.283 = f32[2,197,1536]{2,1,0:T(8,128)S(1)} fusion(f32[2,197,1536]{2,1,0:T(8,128)S(1)} %get-tuple-element.1067, u8[197,1536]{1,0:T(8,128)(4,1)S(1)} %get-tuple-element.1068, u8[197,1536]{1,0:T(8,128)(4,1)S(1)} %get-tuple-element.1069), kind=kLoop, calls=%fused_computation.123.clone.1 | loop fusion | flops 40547328 | bytes 5446656 | tf_op jit(solution)/shard_map/while/body/eval_jaxpr/jvp()/erfc | solution.py:99
  292.3 4.5 fusion.294
  316.8 5.6 %all-reduce.15 = (bf16[768]{0:T(1024)(128)(2,1)S(1)}, bf16[384]{0:T(512)(128)(2,1)S(1)}, bf16[1536]{0:T(1024)(128)(2,1)S(1)}, bf16[384]{0:T(512)(128)(2,1)S(1)},...) all-reduce(bf16[768]{0:T(1024)(128)(2,1)S(1)} %convert_element_type, ...), channel_id=3, replica_groups=mesh['group'=2,'replica'=16] {'group'}, use_global_device_ids=true, to_apply=%region_29.30.clone | all-reduce | flops 4608 | bytes 18432
  322.7 19.1 %reduce-scatter.5.cloned.1.call-done = bf16[192,1152]{1,0:T(8,128)(2,1)} async-done(((bf16[384,1152]{1,0:T(8,128)(2,1)}), bf16[192,1152]{1,0:T(8,128)(2,1)}) %reduce-scatter.5.cloned.1.call-update) | async-done | bytes 442384 | tf_op jit(solution)/shard_map/reduce_scatter | solution.py:233
  341.8 24.5 %reduce-scatter.9.cloned.1.call-done = bf16[192,1536]{1,0:T(8,128)(2,1)} async-done(((bf16[384,1536]{1,0:T(8,128)(2,1)}), bf16[192,1536]{1,0:T(8,128)(2,1)}) %reduce-scatter.9.cloned.1.call-update) | async-done | bytes 589840 | tf_op jit(solution)/shard_map/reduce_scatter | solution.py:245
  366.3 24.5 %reduce-scatter.11.cloned.1.call-done = bf16[768,384]{1,0:T(8,128)(2,1)} async-done(((bf16[1536,384]{1,0:T(8,128)(2,1)}), bf16[768,384]{1,0:T(8,128)(2,1)}) %reduce-scatter.11.cloned.1.call-update) | async-done | bytes 589840 | tf_op jit(solution)/shard_map/reduce_scatter | solution.py:251
  390.8 87.7 %all-reduce.18 = (f32[192,1152]{1,0:T(8,128)}, f32[384]{0:T(512)}, f32[192,384]{1,0:T(8,128)}, f32[192]{0:T(256)}, f32[192,1536]{1,0:T(8,128)}, /*index=5*/f32[7...) all-reduce(bf16[192,1152]{1,0:T(8,128)(2,1)} %reduce-scatter.5.clon, ...), channel_id=1, replica_groups=mesh['group'=2,'replica'=16] {'replica'}, use_global_device_ids=true, to_apply=%region_28.29 | all-reduce | flops 887040 | bytes 5326848 | tf_op jit(solution)/shard_map/psum | solution.py:270
  (692 shorter events, 195.2 us)
Async XLA Ops:
  7.2 11.7 %copy-start.27 = (u32[32]{0:T(128)S(1)}, u32[32]{0:T(128)}, u32[]{:S(2)}) copy-start(u32[32]{0:T(128)} %constant.199) | copy-start | bytes 388
  7.2 13.0 %copy-start.35 = (bf16[192]{0:T(256)(128)(2,1)S(1)}, bf16[192]{0:T(256)(128)(2,1)}, u32[]{:S(2)}) copy-start(bf16[192]{0:T(256)(128)(2,1)} %param.33) | copy-start | bytes 1156
  7.2 13.2 %copy-start.36 = (bf16[192]{0:T(256)(128)(2,1)S(1)}, bf16[192]{0:T(256)(128)(2,1)}, u32[]{:S(2)}) copy-start(bf16[192]{0:T(256)(128)(2,1)} %param.32) | copy-start | bytes 1156
  7.2 13.4 %copy-start.37 = (bf16[192]{0:T(256)(128)(2,1)S(1)}, bf16[192]{0:T(256)(128)(2,1)}, u32[]{:S(2)}) copy-start(bf16[192]{0:T(256)(128)(2,1)} %param.25) | copy-start | bytes 1156
  7.2 13.7 %copy-start.38 = (bf16[192]{0:T(256)(128)(2,1)S(1)}, bf16[192]{0:T(256)(128)(2,1)}, u32[]{:S(2)}) copy-start(bf16[192]{0:T(256)(128)(2,1)} %param.31) | copy-start | bytes 1156
  7.2 13.9 %copy-start.39 = (bf16[192]{0:T(256)(128)(2,1)S(1)}, bf16[192]{0:T(256)(128)(2,1)}, u32[]{:S(2)}) copy-start(bf16[192]{0:T(256)(128)(2,1)} %param.30) | copy-start | bytes 1156
  7.2 14.2 %copy-start.40 = (bf16[192]{0:T(256)(128)(2,1)S(1)}, bf16[192]{0:T(256)(128)(2,1)}, u32[]{:S(2)}) copy-start(bf16[192]{0:T(256)(128)(2,1)} %param.29) | copy-start | bytes 1156
  7.3 18.9 %copy-start.21 = (bf16[192,384]{1,0:T(8,128)(2,1)S(1)}, bf16[192,384]{1,0:T(8,128)(2,1)}, u32[]{:S(2)}) copy-start(bf16[192,384]{1,0:T(8,128)(2,1)} %param.24) | copy-start | bytes 442372
  7.3 27.6 %copy-start.20 = (bf16[192,1152]{1,0:T(8,128)(2,1)S(1)}, bf16[192,1152]{1,0:T(8,128)(2,1)}, u32[]{:S(2)}) copy-start(bf16[192,1152]{1,0:T(8,128)(2,1)} %param.22) | copy-start | bytes 1327108
  7.3 37.1 %all-gather.5.cloned.1.call-start = ((), (), s32[]{:S(2)}) async-start(), calls=%async_computation.4 | async-start | bytes 1769472 | tf_op jit(solution)/shard_map/all_gather | solution.py:186
  8.0 36.3 %copy-start.30 = (s32[4,1]{0,1:T(1,128)S(1)}, s32[4,1]{0,1:T(1,128)}, u32[]{:S(2)}) copy-start(s32[4,1]{0,1:T(1,128)} %param.20) | copy-start | bytes 52
  8.0 53.4 %all-gather.7.cloned.1.call-start = ((), (), s32[]{:S(2)}) async-start(), calls=%async_computation.5 | async-start | bytes 1769472 | tf_op jit(solution)/shard_map/all_gather | solution.py:188
  8.8 313.9 %reduce-scatter.7.cloned.1.call-start = ((), (), s32[]{:S(2)}) async-start(), calls=%async_computation.7 | async-start | bytes 442368 | tf_op jit(solution)/shard_map/reduce_scatter | solution.py:239
  134.6 5.4 %copy-start.34 = (bf16[1536,384]{1,0:T(8,128)(2,1)S(1)}, bf16[1536,384]{1,0:T(8,128)(2,1)}, u32[]{:S(2)}) copy-start(bf16[1536,384]{1,0:T(8,128)(2,1)} %get-tuple-element.1246) | copy-start | bytes 3538948 | tf_op jit(solution)/shard_map/while
  179.8 5.4 %copy-start.34 = (bf16[1536,384]{1,0:T(8,128)(2,1)S(1)}, bf16[1536,384]{1,0:T(8,128)(2,1)}, u32[]{:S(2)}) copy-start(bf16[1536,384]{1,0:T(8,128)(2,1)} %get-tuple-element.1246) | copy-start | bytes 3538948 | tf_op jit(solution)/shard_map/while
  200.6 4.5 copy-start.6
  225.6 5.4 %copy-start.34 = (bf16[1536,384]{1,0:T(8,128)(2,1)S(1)}, bf16[1536,384]{1,0:T(8,128)(2,1)}, u32[]{:S(2)}) copy-start(bf16[1536,384]{1,0:T(8,128)(2,1)} %get-tuple-element.1246) | copy-start | bytes 3538948 | tf_op jit(solution)/shard_map/while
  246.4 4.5 copy-start.6
  271.5 5.4 %copy-start.34 = (bf16[1536,384]{1,0:T(8,128)(2,1)S(1)}, bf16[1536,384]{1,0:T(8,128)(2,1)}, u32[]{:S(2)}) copy-start(bf16[1536,384]{1,0:T(8,128)(2,1)} %get-tuple-element.1246) | copy-start | bytes 3538948 | tf_op jit(solution)/shard_map/while
  306.1 4.6 copy-start.9
  308.0 33.7 %reduce-scatter.5.cloned.1.call-start = ((), (), s32[]{:S(2)}) async-start(), calls=%async_computation.6 | async-start | bytes 1327104 | tf_op jit(solution)/shard_map/reduce_scatter | solution.py:233
  310.6 55.7 %reduce-scatter.9.cloned.1.call-start = ((), (), s32[]{:S(2)}) async-start(), calls=%async_computation.8 | async-start | bytes 1769472 | tf_op jit(solution)/shard_map/reduce_scatter | solution.py:245
  311.8 4.8 copy-start.24
  311.8 79.0 %reduce-scatter.11.cloned.1.call-start = ((), (), s32[]{:S(2)}) async-start(), calls=%async_computation.9 | async-start | bytes 1769472 | tf_op jit(solution)/shard_map/reduce_scatter | solution.py:251
  (110 other events, 232.6 us)
Sparse Core Ops, SparseCore 0:
  9.6 27.4 all-gather.4
  38.7 22.7 all-gather.6
  308.2 12.2 reduce-scatter.6
  323.1 18.5 reduce-scatter.4
  344.4 21.8 reduce-scatter.8
  369.0 21.8 reduce-scatter.10
where the time goes:
time: 488 us; the launch traced here: 485 us
  matrix products  146 us (30%)
  blocking collectives  123 us (25%)
  waiting for transfers between devices  86.6 us (18%)
  local copies, waits for them, and re-layouts  62.8 us (13%)
  other arithmetic  46.7 us (10%)
  between operations  17.1 us (4%)
    psum x1, blocking collectives, local(): final = lax.psum(tuple(shares), 'replica')  87.7 us
    dot_general x4, matrix products, forward(): jnp.einsum('bsf,fd->bsd', act, w_fc2, preferred_element_type=jnp.float32)  26.7 us
    reduce_scatter x1, waiting for transfers between devices, local(): lax.psum_scatter(g_fc1.astype(jnp.bfloat16), 'group', scatter_dimension=0...  24.5 us
    reduce_scatter x1, waiting for transfers between devices, local(): lax.psum_scatter(g_fc2.astype(jnp.bfloat16), 'group', scatter_dimension=0...  24.5 us
    another operation x4, other arithmetic, backward(): jax.vjp(partial(jax.nn.gelu, approximate=False), pre)  21.6 us
    reduce_scatter x1, waiting for transfers between devices, local(): lax.psum_scatter(g_qkv.astype(jnp.bfloat16), 'group', scatter_dimension=0...  19.1 us
    dot_general x4, matrix products, backward(): jnp.einsum('bsd,bsf->df', normed_two, d_pre, preferred_element_type=jnp.f...  17.1 us
    all_gather x1, waiting for transfers between devices, local(): lax.all_gather(w_fc2, 'group', axis=0, tiled=True)  17.1 us
  transfers between devices with their start and end apart: 6, of which 4 were waited for; matrix products, arithmetic and copies ran while one was open for 2% of the time, Pallas kernels for 0%

commit v1 on v0

v1 whole, which is shorter than its diff:
```python
from functools import partial

import jax
import jax.numpy as jnp
from jax import lax
from jax.experimental import pallas as pl
from jax.experimental.pallas import tpu as pltpu
from jax.sharding import PartitionSpec as P

HEADS = 6
ROWS = 208
KEYS = 256
F32 = jnp.float32
BF16 = jnp.bfloat16
NT = (((1,), (1,)), ((), ()))
TN = (((0,), (0,)), ((), ()))


def mm(a, b):
    return jnp.dot(a, b, preferred_element_type=F32)


def mm_nt(a, b):
    return lax.dot_general(a, b, NT, preferred_element_type=F32)


def mm_tn(a, b):
    return lax.dot_general(a, b, TN, preferred_element_type=F32)


def normalize(values):
    center = values - jnp.mean(values, axis=-1, keepdims=True)
    spread = jnp.mean(center * center, axis=-1, keepdims=True)
    rstd = lax.rsqrt(spread + 1e-06)
    return center * rstd, rstd


def norm_back(grad_normed, hat, rstd, gain):
    grad_hat = grad_normed * gain
    first = jnp.mean(grad_hat, axis=-1, keepdims=True)
    second = jnp.mean(grad_hat * hat, axis=-1, keepdims=True)
    return rstd * (grad_hat - first - hat * second)


def gelu_both(pre):
    density = jnp.exp(-0.5 * pre * pre)
    t = 1.0 / (1.0 + (0.3275911 * 0.7071067811865476) * jnp.abs(pre))
    poly = t * (
        0.254829592
        + t * (-0.284496736 + t * (1.421413741 + t * (-1.453152027 + t * 1.061405429)))
    )
    tail = 0.5 * poly * density
    cumulative = jnp.where(pre < 0.0, tail, 1.0 - tail)
    return cumulative, density * 0.3989422804014327


def rows_of(ref):
    return ref[0, 0].astype(F32)


def attention_kernel(x_ref, w_ref, b_ref, g_ref, s_ref, qkv_ref, prob_ref, att_ref, xs, kv):
    seq = x_ref.shape[2]
    width = x_ref.shape[3]

    @pl.when(pl.program_id(0) == 0)
    def _():
        xs[...] = jnp.zeros_like(xs)
        kv[...] = jnp.zeros_like(kv)

    xs[:seq, :] = rows_of(x_ref)
    hat, _ = normalize(xs[...])
    normed = (hat * g_ref[...] + s_ref[...]).astype(BF16)
    qkv = (mm(normed, w_ref[...]) + b_ref[...]).astype(BF16)
    qkv_ref[0] = qkv
    kv[:ROWS, :] = qkv[:, width:]
    low_half = lax.broadcasted_iota(jnp.int32, (1, 128), 1) < 64
    column = lax.broadcasted_iota(jnp.int32, (1, KEYS), 1)
    for pair in range(HEADS // 2):
        lanes = slice(pair * 128, pair * 128 + 128)
        query = qkv[:, lanes] * jnp.array(0.125, BF16)
        keys = kv[:, lanes]
        values = kv[:, width + pair * 128 : width + pair * 128 + 128]
        total = None
        for half in range(2):
            mask = low_half if half == 0 else jnp.logical_not(low_half)
            scores = mm_nt(query, jnp.where(mask, keys, jnp.zeros_like(keys)))
            scores = jnp.where(column < seq, scores, -1e30)
            top = jnp.max(scores, axis=-1, keepdims=True)
            grown = jnp.exp(scores - top)
            prob = (grown * (1.0 / jnp.sum(grown, axis=-1, keepdims=True))).astype(BF16)
            prob_ref[0, 2 * pair + half] = prob
            part = mm(prob, jnp.where(mask, values, jnp.zeros_like(values)))
            total = part if total is None else total + part
        att_ref[0, :, lanes] = total.astype(BF16)


def mlp_kernel(
    count_ref, x_ref, cot_ref, att_ref, wo_ref, bo_ref, w1_ref, b1_ref, w2_ref, b2_ref, g_ref, s_ref,
    out_ref, dx_ref, datt_ref, grads_ref,
    xs, dys, acts, dpres, gw1, gw2, gwo, gb1, gsmall,
):
    step = pl.program_id(0)
    seq = x_ref.shape[2]
    width = x_ref.shape[3]
    hidden = w1_ref.shape[1]

    @pl.when(step == 0)
    def _():
        for ref in (xs, dys, gw1, gw2, gwo, gb1, gsmall):
            ref[...] = jnp.zeros_like(ref)

    valid = (lax.rem(step, 2) < count_ref[lax.div(step, 2), 0]).astype(F32)
    xs[:seq, :] = rows_of(x_ref)
    dys[:seq, :] = rows_of(cot_ref) * valid
    att = att_ref[0]
    middle = xs[...] + mm(att, wo_ref[...]) + bo_ref[...]
    hat, rstd = normalize(middle)
    normed = (hat * g_ref[...] + s_ref[...]).astype(BF16)
    d_out = dys[...]
    d_mlp = d_out.astype(BF16)
    for chunk in range(hidden // 256):
        cols = slice(chunk * 256, chunk * 256 + 256)
        pre = mm(normed, w1_ref[:, cols]) + b1_ref[:, cols]
        d_act = mm_nt(d_mlp, w2_ref[cols, :])
        cumulative, density = gelu_both(pre)
        act = (pre * cumulative).astype(BF16)
        d_pre = (d_act * (cumulative + pre * density)).astype(BF16)
        acts[:, cols] = act
        dpres[:, cols] = d_pre
        gb1[:, cols] += jnp.sum(d_pre.astype(F32).reshape(ROWS // 8, 8, 256), axis=0)
        gw1[:, cols] += mm_tn(normed, d_pre)
        gw2[:, cols] += mm_tn(d_mlp, act)
    result = (middle + mm(acts[...], w2_ref[...]) + b2_ref[...]) * valid
    out_ref[0, 0] = result[:seq].astype(BF16)
    d_normed = mm_nt(dpres[...], w1_ref[...])
    dx = d_out + norm_back(d_normed, hat, rstd, g_ref[...])
    dx_ref[0] = dx
    d_attn = dx.astype(BF16)
    datt_ref[0] = mm_nt(d_attn, wo_ref[...]).astype(BF16)
    gwo[...] += mm_tn(att, d_attn)

    def fold(values):
        return jnp.sum(values.reshape(ROWS // 8, 8, width), axis=0)

    gsmall[0] += fold(d_mlp.astype(F32))
    gsmall[1] += fold(d_attn.astype(F32))
    gsmall[2] += fold(d_normed * hat)
    gsmall[3] += fold(d_normed)

    @pl.when(step == pl.num_programs(0) - 1)
    def _():
        half = width // 2
        quarter = half // 4
        wide = hidden // 2 // 4
        gw2_t = gw2[...].T
        for group in range(2):
            for part in range(4):
                base = group * half + part * quarter
                for col in range(hidden // width):
                    grads_ref[group, part, col * quarter : (col + 1) * quarter, :] = gw1[
                        base : base + quarter, col * width : (col + 1) * width
                    ].astype(BF16)
                top = hidden // width * quarter
                start = group * (hidden // 2) + part * wide
                grads_ref[group, part, top : top + wide, :] = gw2_t[start : start + wide].astype(BF16)
                top += wide
                grads_ref[group, part, top : top + quarter, :] = gwo[base : base + quarter, :].astype(BF16)
                top += quarter
                if part < 2:
                    start = group * (hidden // 2) + part * width
                    row = jnp.sum(gb1[:, start : start + width], axis=0, keepdims=True)
                else:
                    own = slice(group * half, group * half + half)
                    row = jnp.concatenate(
                        [
                            jnp.sum(gsmall[2 * part - 4][:, own], axis=0, keepdims=True),
                            jnp.sum(gsmall[2 * part - 3][:, own], axis=0, keepdims=True),
                        ],
                        axis=1,
                    )
                grads_ref[group, part, top : top + 16, :] = jnp.broadcast_to(row, (16, width)).astype(BF16)


def attention_back_kernel(
    x_ref, qkv_ref, prob_ref, att_ref, datt_ref, dx_ref, w_ref, g_ref, s_ref,
    din_ref, grads_ref,
    xs, kv, dqkv, gw, gb, gsmall,
):
    step = pl.program_id(0)
    seq = x_ref.shape[2]
    width = x_ref.shape[3]

    @pl.when(step == 0)
    def _():
        for ref in (xs, kv, gw, gb, gsmall):
            ref[...] = jnp.zeros_like(ref)

    xs[:seq, :] = rows_of(x_ref)
    hat, rstd = normalize(xs[...])
    normed = (hat * g_ref[...] + s_ref[...]).astype(BF16)
    kv[:ROWS, :] = qkv_ref[0, :, width:]
    low_half = lax.broadcasted_iota(jnp.int32, (1, 128), 1) < 64
    for pair in range(HEADS // 2):
        lanes = slice(pair * 128, pair * 128 + 128)
        query = qkv_ref[0, :, lanes] * jnp.array(0.125, BF16)
        keys = kv[:, lanes] * jnp.array(0.125, BF16)
        values = kv[:, width + pair * 128 : width + pair * 128 + 128]
        d_att = datt_ref[0, :, lanes]
        product = d_att.astype(F32) * att_ref[0, :, lanes].astype(F32)
        dq = dk = dv = None
        for half in range(2):
            mask = low_half if half == 0 else jnp.logical_not(low_half)
            prob = prob_ref[0, 2 * pair + half]
            delta = jnp.sum(jnp.where(mask, product, 0.0), axis=-1, keepdims=True)
            d_prob = mm_nt(d_att, jnp.where(mask, values, jnp.zeros_like(values)))
            d_scores = (prob.astype(F32) * (d_prob - delta)).astype(BF16)
            d_att_h = jnp.where(mask, d_att, jnp.zeros_like(d_att))
            query_h = jnp.where(mask, query, jnp.zeros_like(query))
            keys_h = jnp.where(mask, keys, jnp.zeros_like(keys))
            dv_h = mm_tn(prob, d_att_h)
            dk_h = mm_tn(d_scores, query_h)
            dq_h = mm(d_scores, keys_h)
            dq = dq_h if dq is None else dq + dq_h
            dk = dk_h if dk is None else dk + dk_h
            dv = dv_h if dv is None else dv + dv_h
        dqkv[:, lanes] = dq.astype(BF16)
        dqkv[:, width + pair * 128 : width + pair * 128 + 128] = dk[:ROWS].astype(BF16)
        dqkv[:, 2 * width + pair * 128 : 2 * width + pair * 128 + 128] = dv[:ROWS].astype(BF16)
    d_joined = dqkv[...]
    d_normed = mm_nt(d_joined, w_ref[...])
    gw[...] += mm_tn(normed, d_joined)
    gb[...] += jnp.sum(d_joined.astype(F32).reshape(ROWS // 8, 8, 3 * width), axis=0)
    d_in = dx_ref[0] + norm_back(d_normed, hat, rstd, g_ref[...])
    din_ref[0, 0] = d_in[:seq].astype(BF16)

    def fold(values):
        return jnp.sum(values.reshape(ROWS // 8, 8, width), axis=0)

    gsmall[0] += fold(d_normed * hat)
    gsmall[1] += fold(d_normed)

    @pl.when(step == pl.num_programs(0) - 1)
    def _():
        half = width // 2
        quarter = half // 4
        for group in range(2):
            for part in range(4):
                base = group * half + part * quarter
                for col in range(3):
                    grads_ref[group, part, col * quarter : (col + 1) * quarter, :] = gw[
                        base : base + quarter, col * width : (col + 1) * width
                    ].astype(BF16)
                top = 3 * quarter
                if part == 0:
                    row = jnp.sum(gb[:, 2 * group * width : (2 * group + 1) * width], axis=0, keepdims=True)
                else:
                    own = slice(group * half, group * half + half)
                    row = jnp.concatenate(
                        [
                            jnp.sum(gsmall[0][:, own], axis=0, keepdims=True),
                            jnp.sum(gsmall[1][:, own], axis=0, keepdims=True),
                        ],
                        axis=1,
                    )
                grads_ref[group, part, top : top + 16, :] = jnp.broadcast_to(row, (16, width)).astype(BF16)


def whole(array):
    return pl.BlockSpec(array.shape, lambda i: (0,) * len(array.shape))


def per_image(*shape):
    return pl.BlockSpec((1, *shape), lambda i: (i,) + (0,) * len(shape))


def slot_block(seq, width):
    return pl.BlockSpec((1, 1, seq, width), lambda i: (i // 2, i % 2, 0, 0))


def run_attention(images, w_qkv, bias, gain, shift):
    micro, slots, seq, width = images.shape
    count = micro * slots
    return pl.pallas_call(
        attention_kernel,
        grid=(count,),
        in_specs=[slot_block(seq, width), whole(w_qkv), whole(bias), whole(gain), whole(shift)],
        out_specs=[per_image(ROWS, 3 * width), per_image(HEADS, ROWS, KEYS), per_image(ROWS, width)],
        out_shape=[
            jax.ShapeDtypeStruct((count, ROWS, 3 * width), BF16),
            jax.ShapeDtypeStruct((count, HEADS, ROWS, KEYS), BF16),
            jax.ShapeDtypeStruct((count, ROWS, width), BF16),
        ],
        scratch_shapes=[pltpu.VMEM((ROWS, width), F32), pltpu.VMEM((KEYS, 2 * width), BF16)],
        compiler_params=pltpu.CompilerParams(vmem_limit_bytes=40 << 20),
        cost_estimate=pl.CostEstimate(flops=3 << 30, bytes_accessed=20 << 20, transcendentals=0),
        name="attention_fwd",
    )(images, w_qkv, bias, gain, shift)


def run_mlp(counts, images, cotangent, att, wo, bo, w1, b1, w2, b2, gain, shift):
    micro, slots, seq, width = images.shape
    hidden = w1.shape[1]
    count = micro * slots
    rows = width // 8 * (hidden // width) + hidden // 8 + width // 8 + 16
    return pl.pallas_call(
        mlp_kernel,
        grid=(count,),
        in_specs=[
            pl.BlockSpec(memory_space=pltpu.SMEM),
            slot_block(seq, width),
            slot_block(seq, width),
            per_image(ROWS, width),
        ]
        + [whole(v) for v in (wo, bo, w1, b1, w2, b2, gain, shift)],
        out_specs=[
            slot_block(seq, width),
            per_image(ROWS, width),
            per_image(ROWS, width),
            pl.BlockSpec((2, 4, rows, width), lambda i: (0, 0, 0, 0)),
        ],
        out_shape=[
            jax.ShapeDtypeStruct(images.shape, BF16),
            jax.ShapeDtypeStruct((count, ROWS, width), F32),
            jax.ShapeDtypeStruct((count, ROWS, width), BF16),
            jax.ShapeDtypeStruct((2, 4, rows, width), BF16),
        ],
        scratch_shapes=[
            pltpu.VMEM((ROWS, width), F32),
            pltpu.VMEM((ROWS, width), F32),
            pltpu.VMEM((ROWS, hidden), BF16),
            pltpu.VMEM((ROWS, hidden), BF16),
            pltpu.VMEM((width, hidden), F32),
            pltpu.VMEM((width, hidden), F32),
            pltpu.VMEM((width, width), F32),
            pltpu.VMEM((8, hidden), F32),
            pltpu.VMEM((4, 8, width), F32),
        ],
        compiler_params=pltpu.CompilerParams(vmem_limit_bytes=60 << 20),
        cost_estimate=pl.CostEstimate(flops=12 << 30, bytes_accessed=20 << 20, transcendentals=0),
        name="mlp_fwd_bwd",
    )(counts, images, cotangent, att, wo, bo, w1, b1, w2, b2, gain, shift)


def run_attention_back(images, qkv, prob, att, datt, dx, w_qkv, gain, shift):
    micro, slots, seq, width = images.shape
    count = micro * slots
    rows = width // 8 * 3 + 16
    return pl.pallas_call(
        attention_back_kernel,
        grid=(count,),
        in_specs=[
            slot_block(seq, width),
            per_image(ROWS, 3 * width),
            per_image(HEADS, ROWS, KEYS),
            per_image(ROWS, width),
            per_image(ROWS, width),
            per_image(ROWS, width),
        ]
        + [whole(v) for v in (w_qkv, gain, shift)],
        out_specs=[slot_block(seq, width), pl.BlockSpec((2, 4, rows, width), lambda i: (0, 0, 0, 0))],
        out_shape=[
            jax.ShapeDtypeStruct(images.shape, BF16),
            jax.ShapeDtypeStruct((2, 4, rows, width), BF16),
        ],
        scratch_shapes=[
            pltpu.VMEM((ROWS, width), F32),
            pltpu.VMEM((KEYS, 2 * width), BF16),
            pltpu.VMEM((ROWS, 3 * width), BF16),
            pltpu.VMEM((width, 3 * width), F32),
            pltpu.VMEM((8, 3 * width), F32),
            pltpu.VMEM((2, 8, width), F32),
        ],
        compiler_params=pltpu.CompilerParams(vmem_limit_bytes=60 << 20),
        cost_estimate=pl.CostEstimate(flops=8 << 30, bytes_accessed=20 << 20, transcendentals=0),
        name="attention_bwd",
    )(images, qkv, prob, att, datt, dx, w_qkv, gain, shift)


def flip(value, axis, size, bit):
    return lax.ppermute(value, axis, [(i, i ^ bit) for i in range(size)])


def reduce_grads(grads, replicas):
    group = lax.axis_index("group")
    replica = lax.axis_index("replica")
    core = replica & 1
    side = (replica >> 1) & 1
    take = lambda value, index, size, dim: lax.dynamic_slice_in_dim(value, index * size, size, dim)
    other = flip(take(grads, 1 - core, 2, 1), "replica", replicas, 1)
    grads = take(grads, core, 2, 1) + other
    other = flip(take(grads, 1 - group, 1, 0), "group", 2, 1)
    grads = (take(grads, group, 1, 0) + other)[0]
    other = flip(take(grads, 1 - side, 1, 0), "replica", replicas, 2)
    grads = take(grads, side, 1, 0) + other
    bit = 4
    while bit < replicas:
        grads = grads + flip(grads, "replica", replicas, bit)
        bit *= 2
    other = flip(grads, "replica", replicas, 2)
    grads = jnp.where(side == 0, jnp.concatenate([grads, other]), jnp.concatenate([other, grads]))
    other = flip(grads, "replica", replicas, 1)
    return jnp.where(core == 0, jnp.concatenate([grads, other]), jnp.concatenate([other, grads]))


def local(
    replicas,
    images, image_count, cotangent, w_qkv, b_qv, w_out, b_out, w_fc1, b_fc1, w_fc2, b_fc2,
    gain_one, shift_one, gain_two, shift_two,
):
    group = lax.axis_index("group")

    def full(mine):
        theirs = flip(mine, "group", 2, 1)
        return jnp.where(group == 0, jnp.concatenate([mine, theirs]), jnp.concatenate([theirs, mine]))

    width = images.shape[3]
    hidden = w_fc1.shape[1]
    small = jnp.concatenate([b_qv, b_out, b_fc1, b_fc2, gain_one, shift_one, gain_two, shift_two])
    small = full(small[None]).astype(F32)
    half = width // 2
    offsets = {}
    at = 0
    for name, size in (
        ("b_qv", width), ("b_out", half), ("b_fc1", hidden // 2), ("b_fc2", half),
        ("gain_one", half), ("shift_one", half), ("gain_two", half), ("shift_two", half),
    ):
        offsets[name] = small[:, at : at + size].reshape(1, -1)
        at += size
    bias = offsets["b_qv"]
    bias = jnp.concatenate([bias[:, :width], jnp.zeros_like(bias[:, :width]), bias[:, width:]], axis=1)
    w_qkv_all = full(w_qkv)
    qkv, prob, att = run_attention(images, w_qkv_all, bias, offsets["gain_one"], offsets["shift_one"])
    outputs, dx, datt, grads_b = run_mlp(
        image_count, images, cotangent, att,
        full(w_out), offsets["b_out"], full(w_fc1), offsets["b_fc1"], full(w_fc2), offsets["b_fc2"],
        offsets["gain_two"], offsets["shift_two"],
    )
    input_grad, grads_c = run_attention_back(
        images, qkv, prob, att, datt, dx, w_qkv_all, offsets["gain_one"], offsets["shift_one"]
    )
    sums_b = reduce_grads(grads_b, replicas).astype(F32)
    sums_c = reduce_grads(grads_c, replicas).astype(F32)
    quarter = half // 4
    wide = hidden // 8

    def unfold(block):
        rows = block.shape[1]
        return block.reshape(4, rows // quarter, quarter, width).transpose(0, 2, 1, 3).reshape(half, -1)

    top = hidden // width * quarter
    g_fc1 = unfold(sums_b[:, :top])
    g_fc2 = sums_b[:, top : top + wide].reshape(hidden // 2, width)
    g_out = sums_b[:, top + wide : top + wide + quarter].reshape(half, width)
    rows = sums_b[:, top + wide + quarter]
    g_qkv = unfold(sums_c[:, : 3 * quarter])
    last = sums_c[:, 3 * quarter]
    return (
        outputs, input_grad, g_qkv, last[0], g_out, rows[2, half:], g_fc1, rows[:2].reshape(-1),
        g_fc2, rows[2, :half], last[1, :half], last[1, half:], rows[3, :half], rows[3, half:],
    )


def solution(mesh):
    split = P(None, ("group", "replica"), None, None)
    matrix, vector = P("group", None), P("group")
    return jax.shard_map(
        partial(local, mesh.shape["replica"]),
        mesh=mesh,
        in_specs=(split, P(None, ("group", "replica")), split)
        + (matrix, vector) * 4
        + (vector,) * 4,
        out_specs=(split, split) + (matrix, vector) * 4 + (vector,) * 4,
        check_vma=False,
    )
```

time: 488 us -> 217 us (0.44)
  matrix products: 146 us -> 0 us
  blocking collectives: 123 us -> 0 us
  Pallas kernels: 0 us -> 80 us
  local copies, waits for them, and re-layouts: 62.8 us -> 30 us
  other arithmetic: 46.7 us -> 14.4 us
  starting transfers between devices: 0.24 us -> 27 us
  waiting for transfers between devices: 86.6 us -> 62.6 us
  between operations: 17.1 us -> 0.96 us
    dot_general x92 -> x0, matrix products: 146 us -> none  [the longest x4 26.7 us: forward(): jnp.einsum('bsf,fd->bsd', act, w_fc2, preferred_element_type=jnp.float32)]
    psum x1 -> x0, blocking collectives: 87.7 us -> none  [local(): final = lax.psum(tuple(shares), 'replica')]
    pallas_call x0 -> x3, Pallas kernels: none -> 80 us  [the longest x1 43.7 us: run_mlp(): pl.pallas_call(mlp_kernel, grid=(count,), in_specs=[pl.BlockSpec(memory_s...]
    reduce_scatter x4 -> x0, waiting for transfers between devices: 68.1 us -> none  [the longest x1 24.5 us: local(): lax.psum_scatter(g_fc1.astype(jnp.bfloat16), 'group', scatter_dimension=0...]
    ppermute x0 -> x19, waiting for transfers between devices: none -> 62.6 us  [flip(): return lax.ppermute(value, axis, [(i, i ^ bit) for i in range(size)])]
    ppermute x0 -> x19, starting transfers between devices: none -> 27 us  [flip(): return lax.ppermute(value, axis, [(i, i ^ bit) for i in range(size)])]
    all_gather x4 -> x0, blocking collectives: 25.1 us -> none  [the longest x1 9.47 us: local(): lax.all_gather(w_qkv, 'group', axis=0, tiled=True)]
    another operation x4 -> x0, other arithmetic: 21.6 us -> none  [backward(): jax.vjp(partial(jax.nn.gelu, approximate=False), pre)]
  transfers between devices with their start and end apart: 6 -> 19, of which waited for: 4 -> 8; matrix products, arithmetic and copies ran while one was open for 2% -> 11% of each run, Pallas kernels for 0% -> 17%
where the time goes in v1:
time: 217 us; the launch traced here: 215 us
  Pallas kernels  80 us (37%)
  waiting for transfers between devices  62.6 us (29%)
  local copies, waits for them, and re-layouts  30 us (14%)
  starting transfers between devices  27 us (12%)
  other arithmetic  14.4 us (7%)
    ppermute x19, waiting for transfers between devices, flip(): return lax.ppermute(value, axis, [(i, i ^ bit) for i in range(size)])  62.6 us
    pallas_call x1, Pallas kernels, run_mlp(): pl.pallas_call(mlp_kernel, grid=(count,), in_specs=[pl.BlockSpec(memory_s...  43.7 us
    ppermute x19, starting transfers between devices, flip(): return lax.ppermute(value, axis, [(i, i ^ bit) for i in range(size)])  27 us
    pallas_call x1, Pallas kernels, run_attention_back(): pl.pallas_call(attention_back_kernel, grid=(count,), in_specs=[slot_block...  21.5 us
    pallas_call x1, Pallas kernels, run_attention(): pl.pallas_call(attention_kernel, grid=(count,), in_specs=[slot_block(seq,...  14.8 us
    unnamed x43, local copies, waits for them, and re-layouts  13.4 us
    select_n x4, other arithmetic, full(): jnp.where(group == 0, jnp.concatenate([mine, theirs]), jnp.concatenate([t...  8.46 us
    concatenate x1, local copies, waits for them, and re-layouts, local(): jnp.concatenate([b_qv, b_out, b_fc1, b_fc2, gain_one, shift_one, gain_two...  5.56 us
  transfers between devices with their start and end apart: 19, of which 8 were waited for; matrix products, arithmetic and copies ran while one was open for 11% of the time, Pallas kernels for 17%

profile of v1, /device:TPU:1, one launch (start us, length us, event | category | flops | bytes accessed | tf_op | source)
XLA Modules:
  0.0 215.0 jit_solution(6698659438702296502)
XLA Ops:
  0.7 5.6 %concatenate.62 = bf16[2304]{0:T(1024)(128)(2,1)S(1)} concatenate(bf16[384]{0:T(512)(128)(2,1)} %param.19, bf16[192]{0:T(256)(128)(2,1)} %param.21, bf16[768]{0:T(1024)(128)(2,1)} %param.23, bf16[192]{0:T(256)(128)(2,1)} %param.25, bf16[192]{0:T(256)(128)(2,1)} %param.26, bf16[192]{0:T(256)(128)(2,1)} %param.27, bf16[192]{0:T(256)(128)(2,1)} %param.28, bf16[192]{0:T(256)(128)(2,1)} %param.29), dimensions={0} | concatenate | bytes 9216 | tf_op jit(solution)/shard_map/concatenate | solution.py:418
  6.2 2.1 collective-permute-start.1
  18.2 29.6 %collective-permute-done.2 = bf16[192,384]{1,0:T(8,128)(2,1)} collective-permute-done((bf16[192,384]{1,0:T(8,128)(2,1)}, bf16[192,384]{1,0:T(8,128)(2,1)}, u32[]{:S(2)}, u32[]{:S(2)}) %collective-permute-start.2) | collective-permute-done | bytes 147488 | tf_op jit(solution)/shard_map/ppermute | solution.py:380
  47.8 1.9 maximum_select_fusion.6.wo_ref
  49.8 1.5 maximum_select_fusion.3.w_ref
  51.3 14.8 %attention_fwd.1 = (bf16[8,208,1152]{2,1,0:T(8,128)(2,1)S(1)}, bf16[8,6,208,256]{3,2,1,0:T(8,128)(2,1)S(1)}, bf16[8,208,384]{2,1,0:T(8,128)(2,1)S(1)}) custom-call(bf16[4,2,197,384]{3,2,1,0:T(8,128)(2,1)S(1)} %copy.46.x_ref, bf16[384,1152]{1,0:T(8,128)(2,1)S(1)} %maximum_select_fusion.3.w_ref, f32[1,1152]{1,0:T(1,128)S(1)} %fusion.3.b_ref, ...), custom_call_target="tpu_custom_call" | custom-call | flops 3221225472 | bytes 20971520 | tf_op jit(solution)/shard_map/attention_fwd/pallas_call | solution.py:283
  66.1 2.3 %copy-done.4 = bf16[8,6,208,256]{3,2,1,0:T(8,128)(2,1)} copy-done((bf16[8,6,208,256]{3,2,1,0:T(8,128)(2,1)}, bf16[8,6,208,256]{3,2,1,0:T(8,128)(2,1)S(1)}, u32[]{:S(2)}) %copy-start.4) | copy-done | bytes 5111832
  69.5 3.6 %maximum_select_fusion.1.w1_ref = bf16[384,1536]{1,0:T(8,128)(2,1)} fusion(bf16[192,1536]{1,0:T(8,128)(2,1)} %collective-permute-done.3, bf16[192,1536]{1,0:T(8,128)(2,1)S(1)} %copy-done.11, pred[]{:T(512)S(6)} %eq.6), kind=kLoop, calls=%fused_computation.3 | loop fusion | flops 5308416 | bytes 2359297 | tf_op jit(solution)/shard_map/jit(_where)/select_n | solution.py:414
  74.6 43.7 %mlp_fwd_bwd.1 = (bf16[4,2,197,384]{3,2,1,0:T(8,128)(2,1)}, f32[8,208,384]{2,1,0:T(8,128)}, bf16[8,208,384]{2,1,0:T(8,128)(2,1)}, bf16[2,4,448,384]{3,2,1,0:T(8,128)(2,1)}) custom-call(s32[4,1]{1,0:T(4,128)} %copy.45.count_ref, bf16[4,2,197,384]{3,2,1,0:T(8,128)(2,1)} %copy-done, bf16[4,2,197,384]{3,2,1,0:T(8,128)(2,1)} %copy.47.cot_ref, ...), custom_call_target="tpu_custom_call" | custom-call | flops 12884901888 | bytes 20971520 | tf_op jit(solution)/shard_map/mlp_fwd_bwd/pallas_call | solution.py:305
  119.8 1.9 collective-permute-start.12
  121.7 2.8 %collective-permute-done.12 = bf16[2,2,448,384]{3,2,1,0:T(8,128)(2,1)S(1)} collective-permute-done((bf16[2,2,448,384]{3,2,1,0:T(8,128)(2,1)S(1)}, bf16[2,2,448,384]{3,2,1,0:T(8,128)(2,1)S(1)}, u32[]{:S(2)}, u32[]{:S(2)}) %collective-permute-start.12) | collective-permute-done | bytes 1376288 | tf_op jit(solution)/shard_map/ppermute | solution.py:380
  126.2 21.5 %attention_bwd.1 = (bf16[4,2,197,384]{3,2,1,0:T(8,128)(2,1)}, bf16[2,4,160,384]{3,2,1,0:T(8,128)(2,1)}) custom-call(bf16[4,2,197,384]{3,2,1,0:T(8,128)(2,1)} %copy-done, bf16[8,208,1152]{2,1,0:T(8,128)(2,1)} %copy-done.5, bf16[8,6,208,256]{3,2,1,0:T(8,128)(2,1)} %copy-done.4, bf16[8,208,384]{2,1,0:T(8,128)(2,1)} %copy-done.6, ...), custom_call_target="tpu_custom_call" | custom-call | flops 8589934592 | bytes 20971520 | tf_op jit(solution)/shard_map/attention_bwd/pallas_call | solution.py:348
  153.7 5.7 %collective-permute-done.14 = bf16[1,448,384]{2,1,0:T(8,128)(2,1)S(1)} collective-permute-done((bf16[1,448,384]{2,1,0:T(8,128)(2,1)S(1)}, bf16[1,448,384]{2,1,0:T(8,128)(2,1)S(1)}, u32[]{:S(2)}, u32[]{:S(2)}) %collective-permute-start.14) | collective-permute-done | bytes 344096 | tf_op jit(solution)/shard_map/ppermute | solution.py:380
  162.2 6.0 %collective-permute-done.15 = bf16[1,448,384]{2,1,0:T(8,128)(2,1)S(1)} collective-permute-done((bf16[1,448,384]{2,1,0:T(8,128)(2,1)S(1)}, bf16[1,448,384]{2,1,0:T(8,128)(2,1)S(1)}, u32[]{:S(2)}, u32[]{:S(2)}) %collective-permute-start.15) | collective-permute-done | bytes 344096 | tf_op jit(solution)/shard_map/ppermute | solution.py:380
  168.3 2.6 %collective-permute-start.16 = (bf16[1,448,384]{2,1,0:T(8,128)(2,1)S(1)}, bf16[1,448,384]{2,1,0:T(8,128)(2,1)S(1)}, u32[]{:S(2)}, u32[]{:S(2)}) collective-permute-start(bf16[1,448,384]{2,1,0:T(8,128)(2,1)S(1)} %add.70), channel_id=1, source_target_pairs={{0,8},{1,9},{2,10},{3,11},{4,12},{5,13},{6,14},{7,15},{8,0},{9,1},... | collective-permute-start | bytes 1032200 | tf_op jit(solution)/shard_map/ppermute | solution.py:380
  172.2 7.0 %collective-permute-done.8 = bf16[1,160,384]{2,1,0:T(8,128)(2,1)S(1)} collective-permute-done((bf16[1,160,384]{2,1,0:T(8,128)(2,1)S(1)}, bf16[1,160,384]{2,1,0:T(8,128)(2,1)S(1)}, u32[]{:S(2)}, u32[]{:S(2)}) %collective-permute-start.8) | collective-permute-done | bytes 122912 | tf_op jit(solution)/shard_map/ppermute | solution.py:380
  179.2 2.1 collective-permute-start.9
  181.4 5.7 %collective-permute-done.16 = bf16[1,448,384]{2,1,0:T(8,128)(2,1)S(1)} collective-permute-done((bf16[1,448,384]{2,1,0:T(8,128)(2,1)S(1)}, bf16[1,448,384]{2,1,0:T(8,128)(2,1)S(1)}, u32[]{:S(2)}, u32[]{:S(2)}) %collective-permute-start.16) | collective-permute-done | bytes 344096 | tf_op jit(solution)/shard_map/ppermute | solution.py:380
  188.5 2.4 %collective-permute-done.9 = bf16[1,160,384]{2,1,0:T(8,128)(2,1)S(1)} collective-permute-done((bf16[1,160,384]{2,1,0:T(8,128)(2,1)S(1)}, bf16[1,160,384]{2,1,0:T(8,128)(2,1)S(1)}, u32[]{:S(2)}, u32[]{:S(2)}) %collective-permute-start.9) | collective-permute-done | bytes 122912 | tf_op jit(solution)/shard_map/ppermute | solution.py:380
  192.4 3.5 %collective-permute-done.10 = bf16[1,160,384]{2,1,0:T(8,128)(2,1)S(1)} collective-permute-done((bf16[1,160,384]{2,1,0:T(8,128)(2,1)S(1)}, bf16[1,160,384]{2,1,0:T(8,128)(2,1)S(1)}, u32[]{:S(2)}, u32[]{:S(2)}) %collective-permute-start.10) | collective-permute-done | bytes 122912 | tf_op jit(solution)/shard_map/ppermute | solution.py:380
  196.0 4.6 %collective-permute-start.11 = (bf16[2,160,384]{2,1,0:T(8,128)(2,1)S(1)}, bf16[2,160,384]{2,1,0:T(8,128)(2,1)}, u32[]{:S(2)}, u32[]{:S(2)}) collective-permute-start(bf16[2,160,384]{2,1,0:T(8,128)(2,1)S(1)} %maximum_select_fusion.7), channel_id=1, source_target_pairs={{0,1},{1,0},{2,3},{3,2},{4,5},{5,4},{6,7},{7,6},{8,9},{9,8},{10,11... | collective-permute-start | bytes 737288 | tf_op jit(solution)/shard_map/ppermute | solution.py:380
  200.8 2.0 copy.52
  202.8 2.0 copy.51
  208.7 1.6 fusion
  (110 shorter events, 37.8 us)
Async XLA Ops:
  6.2 8.4 %collective-permute-start.1 = (bf16[1,2304]{1,0:T(2,128)(2,1)S(1)}, bf16[1,2304]{1,0:T(2,128)(2,1)S(1)}, u32[]{:S(2)}, u32[]{:S(2)}) collective-permute-start(bf16[1,2304]{1,0:T(2,128)(2,1)S(1)} %broadcast_in_dim.6), channel_id=1, source_target_pairs={{0,16},{16,0},{1,17},{17,1},{2,18},{18,2},{3,19},{19,3},{4,20},{20... | collective-permute-start | bytes 13832 | tf_op jit(solution)/shard_map/ppermute | solution.py:380
  8.3 41.4 %collective-permute-start = (bf16[192,1152]{1,0:T(8,128)(2,1)}, bf16[192,1152]{1,0:T(8,128)(2,1)}, u32[]{:S(2)}, u32[]{:S(2)}) collective-permute-start(bf16[192,1152]{1,0:T(8,128)(2,1)} %param.18), channel_id=1, source_target_pairs={{0,16},{16,0},{1,17},{17,1},{2,18},{18,2},{3,19},{19,3},{4,20},{20... | collective-permute-start | bytes 1327112 | tf_op jit(solution)/shard_map/ppermute | solution.py:380
  8.4 61.1 %collective-permute-start.3 = (bf16[192,1536]{1,0:T(8,128)(2,1)}, bf16[192,1536]{1,0:T(8,128)(2,1)}, u32[]{:S(2)}, u32[]{:S(2)}) collective-permute-start(bf16[192,1536]{1,0:T(8,128)(2,1)} %param.22), channel_id=1, source_target_pairs={{0,16},{16,0},{1,17},{17,1},{2,18},{18,2},{3,19},{19,3},{4,20},{20... | collective-permute-start | bytes 1769480 | tf_op jit(solution)/shard_map/ppermute | solution.py:380
  9.8 63.4 %collective-permute-start.4 = (bf16[768,384]{1,0:T(8,128)(2,1)}, bf16[768,384]{1,0:T(8,128)(2,1)S(1)}, u32[]{:S(2)}, u32[]{:S(2)}) collective-permute-start(bf16[768,384]{1,0:T(8,128)(2,1)} %param.24), channel_id=1, source_target_pairs={{0,16},{16,0},{1,17},{17,1},{2,18},{18,2},{3,19},{19,3},{4,20},{20... | collective-permute-start | bytes 1769480 | tf_op jit(solution)/shard_map/ppermute | solution.py:380
  9.9 38.0 %collective-permute-start.2 = (bf16[192,384]{1,0:T(8,128)(2,1)}, bf16[192,384]{1,0:T(8,128)(2,1)}, u32[]{:S(2)}, u32[]{:S(2)}) collective-permute-start(bf16[192,384]{1,0:T(8,128)(2,1)} %param.20), channel_id=1, source_target_pairs={{0,16},{16,0},{1,17},{17,1},{2,18},{18,2},{3,19},{19,3},{4,20},{20... | collective-permute-start | bytes 442376 | tf_op jit(solution)/shard_map/ppermute | solution.py:380
  12.7 38.6 %copy-start = (bf16[4,2,197,384]{3,2,1,0:T(8,128)(2,1)}, bf16[4,2,197,384]{3,2,1,0:T(8,128)(2,1)S(1)}, u32[]{:S(2)}) copy-start(bf16[4,2,197,384]{3,2,1,0:T(8,128)(2,1)S(1)} %copy.46.x_ref) | copy-start | bytes 3631108
  12.7 37.0 %copy-start.13 = (bf16[192,1152]{1,0:T(8,128)(2,1)S(1)}, bf16[192,1152]{1,0:T(8,128)(2,1)}, u32[]{:S(2)}) copy-start(bf16[192,1152]{1,0:T(8,128)(2,1)} %param.18) | copy-start | bytes 1327108
  14.9 51.2 %copy-start.2 = (f32[1,384]{1,0:T(1,128)}, f32[1,384]{1,0:T(1,128)S(1)}, u32[]{:S(2)}) copy-start(f32[1,384]{1,0:T(1,128)S(1)} %reshape.82.g_ref) | copy-start | bytes 4612
  15.0 51.1 %copy-start.3 = (f32[1,384]{1,0:T(1,128)}, f32[1,384]{1,0:T(1,128)S(1)}, u32[]{:S(2)}) copy-start(f32[1,384]{1,0:T(1,128)S(1)} %reshape.83.s_ref) | copy-start | bytes 4612
  51.3 18.2 %copy-start.11 = (bf16[192,1536]{1,0:T(8,128)(2,1)S(1)}, bf16[192,1536]{1,0:T(8,128)(2,1)}, u32[]{:S(2)}) copy-start(bf16[192,1536]{1,0:T(8,128)(2,1)} %param.22) | copy-start | bytes 1769476
  119.8 4.6 %collective-permute-start.12 = (bf16[2,2,448,384]{3,2,1,0:T(8,128)(2,1)S(1)}, bf16[2,2,448,384]{3,2,1,0:T(8,128)(2,1)S(1)}, u32[]{:S(2)}, u32[]{:S(2)}) collective-permute-start(bf16[2,2,448,384]{3,2,1,0:T(8,128)(2,1)S(1)} %constant_dynamic-slice_fusion.1), channel_id=1, source_target_pairs={{0,1},{1,0},{2,3},{3,2},{4,5},{5,4},{6,7},{7,6},{8,9},{9,8},{10,11... | collective-permute-start | bytes 4128776 | tf_op jit(solution)/shard_map/ppermute | solution.py:380
  126.0 23.6 %collective-permute-start.13 = (bf16[1,2,448,384]{3,2,1,0:T(8,128)(2,1)S(1)}, bf16[1,2,448,384]{3,2,1,0:T(8,128)(2,1)S(1)}, u32[]{:S(2)}, u32[]{:S(2)}) collective-permute-start(bf16[1,2,448,384]{3,2,1,0:T(8,128)(2,1)S(1)} %constant_dynamic-slice_fusion), channel_id=1, source_target_pairs={{0,16},{16,0},{1,17},{17,1},{2,18},{18,2},{3,19},{19,3},{4,20},{20... | collective-permute-start | bytes 2064392 | tf_op jit(solution)/shard_map/ppermute | solution.py:380
  148.9 2.3 %collective-permute-start.5 = (bf16[2,2,160,384]{3,2,1,0:T(8,128)(2,1)S(1)}, bf16[2,2,160,384]{3,2,1,0:T(8,128)(2,1)}, u32[]{:S(2)}, u32[]{:S(2)}) collective-permute-start(bf16[2,2,160,384]{3,2,1,0:T(8,128)(2,1)S(1)} %constant_dynamic-slice_fusion.3), channel_id=1, source_target_pairs={{0,1},{1,0},{2,3},{3,2},{4,5},{5,4},{6,7},{7,6},{8,9},{9,8},{10,11... | collective-permute-start | bytes 1474568 | tf_op jit(solution)/shard_map/ppermute | solution.py:380
  149.7 9.6 %collective-permute-start.14 = (bf16[1,448,384]{2,1,0:T(8,128)(2,1)S(1)}, bf16[1,448,384]{2,1,0:T(8,128)(2,1)S(1)}, u32[]{:S(2)}, u32[]{:S(2)}) collective-permute-start(bf16[1,448,384]{2,1,0:T(8,128)(2,1)S(1)} %dynamic-slice_bitcast_fusion), channel_id=1, source_target_pairs={{0,2},{1,3},{2,0},{3,1},{4,6},{5,7},{6,4},{7,5},{8,10},{9,11},{10,... | collective-permute-start | bytes 1032200 | tf_op jit(solution)/shard_map/ppermute | solution.py:380
  152.3 8.5 %collective-permute-start.6 = (bf16[1,2,160,384]{3,2,1,0:T(8,128)(2,1)S(1)}, bf16[1,2,160,384]{3,2,1,0:T(8,128)(2,1)S(1)}, u32[]{:S(2)}, u32[]{:S(2)}) collective-permute-start(bf16[1,2,160,384]{3,2,1,0:T(8,128)(2,1)S(1)} %constant_dynamic-slice_fusion.2), channel_id=1, source_target_pairs={{0,16},{16,0},{1,17},{17,1},{2,18},{18,2},{3,19},{19,3},{4,20},{20... | collective-permute-start | bytes 737288 | tf_op jit(solution)/shard_map/ppermute | solution.py:380
  159.4 8.8 %collective-permute-start.15 = (bf16[1,448,384]{2,1,0:T(8,128)(2,1)S(1)}, bf16[1,448,384]{2,1,0:T(8,128)(2,1)S(1)}, u32[]{:S(2)}, u32[]{:S(2)}) collective-permute-start(bf16[1,448,384]{2,1,0:T(8,128)(2,1)S(1)} %bitcast_add_fusion), channel_id=1, source_target_pairs={{0,4},{1,5},{2,6},{3,7},{4,0},{5,1},{6,2},{7,3},{8,12},{9,13},{10,... | collective-permute-start | bytes 1032200 | tf_op jit(solution)/shard_map/ppermute | solution.py:380
  160.9 9.9 %collective-permute-start.7 = (bf16[1,160,384]{2,1,0:T(8,128)(2,1)S(1)}, bf16[1,160,384]{2,1,0:T(8,128)(2,1)S(1)}, u32[]{:S(2)}, u32[]{:S(2)}) collective-permute-start(bf16[1,160,384]{2,1,0:T(8,128)(2,1)S(1)} %dynamic-slice_bitcast_fusion.1), channel_id=1, source_target_pairs={{0,2},{1,3},{2,0},{3,1},{4,6},{5,7},{6,4},{7,5},{8,10},{9,11},{10,... | collective-permute-start | bytes 368648 | tf_op jit(solution)/shard_map/ppermute | solution.py:380
  168.3 18.8 %collective-permute-start.16 = (bf16[1,448,384]{2,1,0:T(8,128)(2,1)S(1)}, bf16[1,448,384]{2,1,0:T(8,128)(2,1)S(1)}, u32[]{:S(2)}, u32[]{:S(2)}) collective-permute-start(bf16[1,448,384]{2,1,0:T(8,128)(2,1)S(1)} %add.70), channel_id=1, source_target_pairs={{0,8},{1,9},{2,10},{3,11},{4,12},{5,13},{6,14},{7,15},{8,0},{9,1},... | collective-permute-start | bytes 1032200 | tf_op jit(solution)/shard_map/ppermute | solution.py:380
  170.8 8.4 %collective-permute-start.8 = (bf16[1,160,384]{2,1,0:T(8,128)(2,1)S(1)}, bf16[1,160,384]{2,1,0:T(8,128)(2,1)S(1)}, u32[]{:S(2)}, u32[]{:S(2)}) collective-permute-start(bf16[1,160,384]{2,1,0:T(8,128)(2,1)S(1)} %bitcast_add_fusion.1), channel_id=1, source_target_pairs={{0,4},{1,5},{2,6},{3,7},{4,0},{5,1},{6,2},{7,3},{8,12},{9,13},{10,... | collective-permute-start | bytes 368648 | tf_op jit(solution)/shard_map/ppermute | solution.py:380
  179.2 11.7 %collective-permute-start.9 = (bf16[1,160,384]{2,1,0:T(8,128)(2,1)S(1)}, bf16[1,160,384]{2,1,0:T(8,128)(2,1)S(1)}, u32[]{:S(2)}, u32[]{:S(2)}) collective-permute-start(bf16[1,160,384]{2,1,0:T(8,128)(2,1)S(1)} %add.65), channel_id=1, source_target_pairs={{0,8},{1,9},{2,10},{3,11},{4,12},{5,13},{6,14},{7,15},{8,0},{9,1},... | collective-permute-start | bytes 368648 | tf_op jit(solution)/shard_map/ppermute | solution.py:380
  187.1 13.5 %collective-permute-start.17 = (bf16[1,448,384]{2,1,0:T(8,128)(2,1)S(1)}, bf16[1,448,384]{2,1,0:T(8,128)(2,1)S(1)}, u32[]{:S(2)}, u32[]{:S(2)}) collective-permute-start(bf16[1,448,384]{2,1,0:T(8,128)(2,1)S(1)} %add.71), channel_id=1, source_target_pairs={{0,2},{1,3},{2,0},{3,1},{4,6},{5,7},{6,4},{7,5},{8,10},{9,11},{10,... | collective-permute-start | bytes 1032200 | tf_op jit(solution)/shard_map/ppermute | solution.py:380
  191.0 4.9 %collective-permute-start.10 = (bf16[1,160,384]{2,1,0:T(8,128)(2,1)S(1)}, bf16[1,160,384]{2,1,0:T(8,128)(2,1)S(1)}, u32[]{:S(2)}, u32[]{:S(2)}) collective-permute-start(bf16[1,160,384]{2,1,0:T(8,128)(2,1)S(1)} %add.66), channel_id=1, source_target_pairs={{0,2},{1,3},{2,0},{3,1},{4,6},{5,7},{6,4},{7,5},{8,10},{9,11},{10,... | collective-permute-start | bytes 368648 | tf_op jit(solution)/shard_map/ppermute | solution.py:380
  196.0 8.8 %collective-permute-start.11 = (bf16[2,160,384]{2,1,0:T(8,128)(2,1)S(1)}, bf16[2,160,384]{2,1,0:T(8,128)(2,1)}, u32[]{:S(2)}, u32[]{:S(2)}) collective-permute-start(bf16[2,160,384]{2,1,0:T(8,128)(2,1)S(1)} %maximum_select_fusion.7), channel_id=1, source_target_pairs={{0,1},{1,0},{2,3},{3,2},{4,5},{5,4},{6,7},{7,6},{8,9},{9,8},{10,11... | collective-permute-start | bytes 737288 | tf_op jit(solution)/shard_map/ppermute | solution.py:380
  200.7 7.9 %collective-permute-start.18 = (bf16[2,448,384]{2,1,0:T(8,128)(2,1)S(1)}, bf16[2,448,384]{2,1,0:T(8,128)(2,1)}, u32[]{:S(2)}, u32[]{:S(2)}) collective-permute-start(bf16[2,448,384]{2,1,0:T(8,128)(2,1)S(1)} %maximum_select_fusion.4), channel_id=1, source_target_pairs={{0,1},{1,0},{2,3},{3,2},{4,5},{5,4},{6,7},{7,6},{8,9},{9,8},{10,11... | collective-permute-start | bytes 2064392 | tf_op jit(solution)/shard_map/ppermute | solution.py:380
  (10 other events, 57.6 us)

commit v2 on v1

v2 whole, which is shorter than its diff:
```python
from functools import partial

import jax
import jax.numpy as jnp
from jax import lax
from jax.experimental import pallas as pl
from jax.experimental.layout import Layout, with_layout_constraint
from jax.experimental.pallas import tpu as pltpu
from jax.sharding import PartitionSpec as P


HEADS = 6
ROWS = 208
KEYS = 256
F32 = jnp.float32
BF16 = jnp.bfloat16
NT = (((1,), (1,)), ((), ()))
TN = (((0,), (0,)), ((), ()))


def mm(a, b):
    return jnp.dot(a, b, preferred_element_type=F32)


def mm_nt(a, b):
    return lax.dot_general(a, b, NT, preferred_element_type=F32)


def mm_tn(a, b):
    return lax.dot_general(a, b, TN, preferred_element_type=F32)


def normalize(values):
    center = values - jnp.mean(values, axis=-1, keepdims=True)
    spread = jnp.mean(center * center, axis=-1, keepdims=True)
    rstd = lax.rsqrt(spread + 1e-06)
    return center * rstd, rstd


def norm_back(grad_normed, hat, rstd, gain):
    grad_hat = grad_normed * gain
    first = jnp.mean(grad_hat, axis=-1, keepdims=True)
    second = jnp.mean(grad_hat * hat, axis=-1, keepdims=True)
    return rstd * (grad_hat - first - hat * second)


def gelu_parts(pre, d_act):
    size = jnp.abs(pre)
    density = jnp.exp2(pre * (pre * -0.7213475204444817))
    t = 1.0 / (1.0 + 0.2316418882663604 * size)
    poly = t * (
        0.127414796
        + t * (-0.142248368 + t * (0.7107068705 + t * (-0.7265760135 + t * 0.5307027145)))
    )
    act = jnp.maximum(pre, 0.0) - size * (poly * density)
    edge = density * (poly - 0.3989422804014327 * size)
    slope = jnp.where(pre < 0.0, edge, 1.0 - edge)
    return act.astype(BF16), (d_act * slope).astype(BF16)


def read_image(ref, micro, slot, seq, target, top):
    tiles = target.shape[1] // 128
    for tile in range(tiles):
        start = micro * (seq * tiles * 2) + 2 * tile + slot
        target[top : top + seq, tile * 128 : tile * 128 + 128] = ref[pl.ds(start, seq, stride=2 * tiles), :]


def write_image(ref, micro, slot, seq, value):
    tiles = value.shape[1] // 128
    for tile in range(tiles):
        start = micro * (seq * tiles * 2) + 2 * tile + slot
        ref[pl.ds(start, seq, stride=2 * tiles), :] = value[:seq, tile * 128 : tile * 128 + 128]


def joined(first, second, row, size):
    return jnp.concatenate([first[row : row + 1, :size], second[row : row + 1, :size]], axis=1)


def ordered(idx_ref, mine, theirs):
    low = idx_ref[0] == 0
    mine, theirs = mine.astype(F32), theirs.astype(F32)
    return jnp.where(low, mine, theirs), jnp.where(low, theirs, mine)


def at(start, size):
    return pl.ds(pl.multiple_of(start, 16), size)


VMEM_SPEC = pl.BlockSpec(memory_space=pltpu.VMEM)


def pack_first_kernel(idx_ref, wq_ref, *refs):
    vectors, first_ref, small_ref = refs[:-2], refs[-2], refs[-1]
    part = wq_ref.shape[0]
    small_ref[...] = jnp.zeros_like(small_ref)
    for k, ref in enumerate(vectors):
        size = ref.shape[0]
        small_ref[k : k + 1, :size] = ref[...].reshape(1, size)
    first_ref[:part, :] = wq_ref[...]
    first_ref[part:, :] = jnp.zeros((16, first_ref.shape[1]), BF16)
    first_ref[part : part + 8, : small_ref.shape[1]] = small_ref[...]


def pack_second_kernel(idx_ref, wo_ref, w1_ref, w2_ref, second_ref):
    part, width = wo_ref.shape
    hidden = w1_ref.shape[1]
    second_ref[:, :width] = wo_ref[...]
    second_ref[:, width : width + hidden] = w1_ref[...]
    for k in range(hidden // width):
        second_ref[:, width + hidden + k * width : width + hidden + (k + 1) * width] = w2_ref[
            k * part : (k + 1) * part, :
        ]


def own_rows(rows, columns):
    return pl.BlockSpec((rows, columns), lambda i, idx: (idx[1], 0))


def run_pack_first(idx, w_qkv, vectors):
    half, wide = w_qkv.shape
    longest = max(v.shape[0] for v in vectors)
    shapes = [(half // 2 + 16, wide), (8, longest)]
    return pl.pallas_call(
        pack_first_kernel,
        grid_spec=pltpu.PrefetchScalarGridSpec(
            num_scalar_prefetch=1,
            grid=(1,),
            in_specs=[own_rows(half // 2, wide)] + [pl.BlockSpec(v.shape, lambda i, idx: (0,)) for v in vectors],
            out_specs=[pl.BlockSpec(s, lambda i, idx: (0, 0)) for s in shapes],
        ),
        out_shape=[jax.ShapeDtypeStruct(s, BF16) for s in shapes],
        name="pack_first",
    )(idx, w_qkv, *vectors)


def run_pack_second(idx, w_out, w_fc1, w_fc2):
    half, width = w_out.shape
    hidden = w_fc1.shape[1]
    part = half // 2
    shape = (part, width + 2 * hidden)
    return pl.pallas_call(
        pack_second_kernel,
        grid_spec=pltpu.PrefetchScalarGridSpec(
            num_scalar_prefetch=1,
            grid=(1,),
            in_specs=[own_rows(part, width), own_rows(part, hidden), own_rows(hidden // 4, width)],
            out_specs=pl.BlockSpec(shape, lambda i, idx: (0, 0)),
        ),
        out_shape=jax.ShapeDtypeStruct(shape, BF16),
        name="pack_second",
    )(idx, w_out, w_fc1, w_fc2)


def attention_kernel(
    idx_ref, x_ref, w_ref, near_ref, far_ref, small_ref,
    qkv_ref, prob_ref, att_ref, whole_ref, vec_ref,
    view, xs, kv, bias, scores,
):
    step = pl.program_id(0)
    half, wide = w_ref.shape
    width = wide // 3
    part = half // 2
    pairs = width // 128
    seq = x_ref.shape[0] * 128 // (width * pl.num_programs(0))

    @pl.when(step == 0)
    def _():
        view[...] = x_ref[...].astype(F32)
        xs[...] = jnp.zeros_like(xs)
        kv[...] = jnp.zeros_like(kv)
        group, core = idx_ref[0], idx_ref[1]
        first, second = ordered(idx_ref, small_ref[...], near_ref[part : part + 8, : small_ref.shape[1]])
        vec_ref[0:1, :] = joined(first, second, 4, half)
        vec_ref[1:2, :] = joined(first, second, 5, half)
        other = (1 - group) * half
        for pair in range(pairs):
            for kind in range(3):
                source = slice(kind * width + pair * 128, kind * width + pair * 128 + 128)
                target = slice((3 * pair + kind) * 128, (3 * pair + kind) * 128 + 128)
                whole_ref[at(group * half, half), target] = w_ref[:, source]
                whole_ref[at(other + core * part, part), target] = near_ref[:part, source]
                whole_ref[at(other + (1 - core) * part, part), target] = far_ref[:part, source]
                lanes = slice(pair * 128, pair * 128 + 128)
                piece = (first[0:1, lanes], jnp.zeros((1, 128), F32), second[0:1, lanes])[kind]
                bias[0:1, target] = piece

    read_image(view, lax.div(step, 2), lax.rem(step, 2), seq, xs, 0)
    hat, _ = normalize(xs[...])
    normed = (hat * vec_ref[0:1, :] + vec_ref[1:2, :]).astype(BF16)
    low_half = lax.broadcasted_iota(jnp.int32, (1, 128), 1) < 64
    column = lax.broadcasted_iota(jnp.int32, (1, KEYS), 1)

    def project(pair):
        lanes = slice(pair * 384, pair * 384 + 384)
        qkv = (mm(normed, whole_ref[:, lanes]) + bias[0:1, lanes]).astype(BF16)
        qkv_ref[0, :, lanes] = qkv
        kv[:ROWS, pair * 256 : pair * 256 + 256] = qkv[:, 128:]

    def masked(values, head):
        mask = low_half if head % 2 == 0 else jnp.logical_not(low_half)
        return jnp.where(mask, values, jnp.zeros_like(values))

    def first_part(head):
        pair = head // 2
        query = qkv_ref[0, :, pair * 384 : pair * 384 + 128] * jnp.array(0.125, BF16)
        scores[head % 2] = mm_nt(query, masked(kv[:, pair * 256 : pair * 256 + 128], head))

    def second_part(head):
        for r in range(0, ROWS, 16):
            value = jnp.where(column < seq, scores[head % 2, r : r + 16], -1e30)
            top = jnp.max(value, axis=-1, keepdims=True)
            grown = jnp.exp(value - top)
            prob_ref[0, head, r : r + 16] = (grown * (1.0 / jnp.sum(grown, axis=-1, keepdims=True))).astype(BF16)

    def third_part(head):
        pair = head // 2
        values = kv[:, pair * 256 + 128 : pair * 256 + 256]
        if head % 2 == 1:
            total = mm(prob_ref[0, head - 1], masked(values, 0)) + mm(prob_ref[0, head], masked(values, 1))
            att_ref[0, :, pair * 128 : pair * 128 + 128] = total.astype(BF16)

    project(0)
    for k in range(HEADS + 2):
        if k < HEADS:
            first_part(k)
        if k % 2 == 0 and k // 2 + 1 < pairs:
            project(k // 2 + 1)
        if k >= 2:
            third_part(k - 2)
        if 1 <= k <= HEADS:
            second_part(k - 1)


def mlp_kernel(
    idx_ref, count_ref, x_ref, cot_ref, att_ref, wo_ref, w1_ref, w2_ref, near_ref, far_ref, small_ref, first_ref,
    out_ref, dx_ref, datt_ref, keep_ref, send_ref,
    view_x, view_c, xs, dys, acts, dpres, pres, dacts, wo, w1, w2, wot, w1t, w2t, vec, b1, out_half, dn_half,
    gw1, gw2, gwo, gsmall,
):
    step = pl.program_id(0)
    last = pl.num_programs(0) - 1
    half, width = wo_ref.shape
    hidden = w1_ref.shape[1]
    part = half // 2
    rows = xs.shape[0]
    seq = x_ref.shape[0] * 128 // (width * 2 * pl.num_programs(0))
    core = idx_ref[1]

    @pl.when(step == 0)
    def _():
        view_x[...] = x_ref[...].astype(F32)
        view_c[...] = cot_ref[...].astype(F32)
        for ref in (xs, dys, gw1, gw2, gwo, gsmall):
            ref[...] = jnp.zeros_like(ref)
        group = idx_ref[0]
        wo[at(group * half, half), :] = wo_ref[...]
        w1[at(group * half, half), :] = w1_ref[...]
        w2[at(group * (hidden // 2), hidden // 2), :] = w2_ref[...]
        other = (1 - group) * half
        for ref, which in ((near_ref, core), (far_ref, 1 - core)):
            wo[at(other + which * part, part), :] = ref[:, :width]
            w1[at(other + which * part, part), :] = ref[:, width : width + hidden]
            base = (1 - group) * (hidden // 2) + which * (hidden // 4)
            for k in range(hidden // width):
                w2[at(base + k * part, part), :] = ref[:, width + hidden + k * width : width + hidden + (k + 1) * width]
        wot[...] = wo[...].T
        w1t[...] = w1[...].T
        w2t[...] = w2[...].T
        first, second = ordered(idx_ref, small_ref[...], first_ref[part : part + 8, : small_ref.shape[1]])
        vec[0:1, :] = joined(first, second, 1, half)
        vec[1:2, :] = joined(first, second, 3, half)
        vec[2:3, :] = joined(first, second, 6, half)
        vec[3:4, :] = joined(first, second, 7, half)
        b1[0:1, : hidden // 2] = first[2:3, :]
        b1[0:1, hidden // 2 :] = second[2:3, :]

    second_valid = (1 < count_ref[step, 0]).astype(F32)
    for slot in range(2):
        read_image(view_x, step, slot, seq, xs, slot * ROWS)
        read_image(view_c, step, slot, seq, dys, slot * ROWS)
    row = lax.broadcasted_iota(jnp.int32, (rows, 1), 0)
    valid = jnp.where(row < ROWS, 1.0, second_valid)
    att = att_ref[...].reshape(rows, width)
    middle = xs[...] + mm(att, wo[...]) + vec[0:1, :]
    hat, rstd = normalize(middle)
    gain = vec[2:3, :]
    normed = (hat * gain + vec[3:4, :]).astype(BF16)
    d_out = dys[...] * valid
    d_mlp = d_out.astype(BF16)
    normed_t = jnp.concatenate([normed.T, jnp.ones((16, rows), BF16)], axis=0)
    d_mlp_t = d_mlp.T
    chunks = hidden // 256
    middle_of = hidden // 2

    def first_part(c):
        cols = slice(c * 256, c * 256 + 256)
        pres[c % 2] = mm(normed, w1[:, cols])
        dacts[c % 2] = mm(d_mlp, w2t[:, cols])

    def second_part(c):
        cols = slice(c * 256, c * 256 + 256)
        bias = b1[0:1, cols]
        for r in range(0, rows, 32):
            act, d_pre = gelu_parts(pres[c % 2, r : r + 32] + bias, dacts[c % 2, r : r + 32])
            acts[r : r + 32, cols] = act
            dpres[r : r + 32, cols] = d_pre

    def third_part(c):
        cols = slice(c * 256, c * 256 + 256)
        gw1[:, cols] += mm(normed_t, dpres[:, cols])
        gw2[:, cols] += mm(d_mlp_t, acts[:, cols])

    for k in range(chunks + 2):
        if k < chunks:
            first_part(k)
        if k >= 2:
            third_part(k - 2)
        if k == chunks // 2 + 1:
            out_half[...] = mm(acts[:, :middle_of], w2[:middle_of, :])
            dn_half[...] = mm(dpres[:, :middle_of], w1t[:middle_of, :])
        if 1 <= k <= chunks:
            second_part(k - 1)

    result = (middle + out_half[...] + mm(acts[:, middle_of:], w2[middle_of:, :]) + vec[1:2, :]) * valid
    for slot in range(2):
        write_image(view_x, step, slot, seq, result[slot * ROWS : slot * ROWS + ROWS])
    d_normed = dn_half[...] + mm(dpres[:, middle_of:], w1t[middle_of:, :])
    dx = d_out + norm_back(d_normed, hat, rstd, gain)
    dx_ref[...] = dx.reshape(2, ROWS, width)
    d_attn = dx.astype(BF16)
    datt_ref[...] = mm(d_attn, wot[...]).astype(BF16).reshape(2, ROWS, width)
    gwo[...] += mm_tn(att, d_attn)

    def fold(values):
        return jnp.sum(values.reshape(rows // 8, 8, width), axis=0)

    gsmall[0] += fold(d_out)
    gsmall[1] += fold(d_attn.astype(F32))
    gsmall[2] += fold(d_normed * hat)
    gsmall[3] += fold(d_normed)

    @pl.when(step == last)
    def _():
        out_ref[...] = view_x[...].astype(BF16)
        quarter = half // 4
        wide = hidden // 8
        gw2_t = gw2[...].T
        small_rows = [jnp.sum(gsmall[k], axis=0, keepdims=True) for k in range(4)]

        def emit(group, quad, ref, side):
            base = group * half + quad * quarter
            top = 0
            for col in range(hidden // width):
                ref[group, side, top : top + quarter, :] = gw1[
                    base : base + quarter, col * width : (col + 1) * width
                ].astype(BF16)
                top += quarter
            start = group * (hidden // 2) + quad * wide
            ref[group, side, top : top + wide, :] = gw2_t[start : start + wide].astype(BF16)
            top += wide
            ref[group, side, top : top + quarter, :] = gwo[base : base + quarter, :].astype(BF16)
            top += quarter
            if quad < 2:
                start = group * (hidden // 2) + quad * width
                value = gw1[width : width + 1, start : start + width]
            else:
                own = slice(group * half, group * half + half)
                value = jnp.concatenate(
                    [small_rows[2 * quad - 4][:, own], small_rows[2 * quad - 3][:, own]], axis=1
                )
            ref[group, side, top : top + 16, :] = jnp.broadcast_to(value, (16, width)).astype(BF16)

        split_quads(core, emit, keep_ref, send_ref)


def split_quads(core, emit, keep_ref, send_ref):
    for mine in range(2):

        @pl.when(core == mine)
        def _():
            for group in range(2):
                for side in range(2):
                    emit(group, 2 * mine + side, keep_ref, side)
                    emit(group, 2 * (1 - mine) + side, send_ref, side)


def attention_back_kernel(
    first_image, last, idx_ref, x_ref, qkv_ref, prob_ref, att_ref, datt_ref, w_ref, vec_ref, *refs
):
    carried = 0 if first_image == 0 else 3
    dqkv_ref, total_ref, sums_ref = refs[carried : carried + 3]
    view, xs, kv, hat_t, d_probs, d_scores = refs[-6:]
    step = pl.program_id(0)
    width = w_ref.shape[0]
    seq = x_ref.shape[0] * 128 // (width * qkv_ref.shape[0] * 8)
    image = first_image + step
    pairs = width // 128

    @pl.when(step == 0)
    def _():
        view[...] = x_ref[...].astype(F32)
        xs[...] = jnp.zeros_like(xs)
        kv[...] = jnp.zeros_like(kv)
        total_ref[...] = refs[1][...] if carried else jnp.zeros_like(total_ref)
        sums_ref[...] = refs[2][...] if carried else jnp.zeros_like(sums_ref)

    read_image(view, lax.div(image, 2), lax.rem(image, 2), seq, xs, 0)
    hat, _ = normalize(xs[...])
    hat_t[...] = hat.astype(BF16).T
    for pair in range(pairs):
        kv[:ROWS, pair * 256 : pair * 256 + 256] = qkv_ref[0, :, pair * 384 + 128 : pair * 384 + 384]
    low_half = lax.broadcasted_iota(jnp.int32, (1, 128), 1) < 64

    def masked(values, head):
        mask = low_half if head % 2 == 0 else jnp.logical_not(low_half)
        return jnp.where(mask, values, jnp.zeros_like(values))

    def lanes(head):
        return slice(head // 2 * 128, head // 2 * 128 + 128)

    def first_part(head):
        pair = head // 2
        d_probs[head % 2] = mm_nt(
            datt_ref[0, :, lanes(head)], masked(kv[:, pair * 256 + 128 : pair * 256 + 256], head)
        )

    def second_part(head):
        for r in range(0, ROWS, 16):
            rows = slice(r, r + 16)
            product = datt_ref[0, rows, lanes(head)].astype(F32) * att_ref[0, rows, lanes(head)].astype(F32)
            delta = jnp.sum(masked(product, head), axis=-1, keepdims=True)
            d_scores[head % 4, rows] = (
                prob_ref[0, head, rows].astype(F32) * (d_probs[head % 2, rows] - delta)
            ).astype(BF16)

    def third_part(pair):
        query = qkv_ref[0, :, pair * 384 : pair * 384 + 128] * jnp.array(0.125, BF16)
        keys = kv[:, pair * 256 : pair * 256 + 128] * jnp.array(0.125, BF16)
        d_att = datt_ref[0, :, pair * 128 : pair * 128 + 128]
        dq = dk = dv = 0.0
        for head in (2 * pair, 2 * pair + 1):
            d_score = d_scores[head % 4]
            dv = dv + mm_tn(prob_ref[0, head], masked(d_att, head))
            dk = dk + mm_tn(d_score, masked(query, head))
            dq = dq + mm(d_score, masked(keys, head))
        top = pair * 384
        dqkv_ref[0, :, top : top + 128] = dq.astype(BF16)
        dqkv_ref[0, :, top + 128 : top + 256] = dk[:ROWS].astype(BF16)
        dqkv_ref[0, :, top + 256 : top + 384] = dv[:ROWS].astype(BF16)

    def fourth_part(pair):
        columns = slice(pair * 384, pair * 384 + 384)
        joined_back = dqkv_ref[0, :, columns]
        total_ref[:, columns] += mm(hat_t[...], joined_back)
        sums_ref[:, columns] += jnp.sum(joined_back.astype(F32).reshape(ROWS // 8, 8, 384), axis=0)

    for k in range(HEADS + 3):
        if k < HEADS:
            first_part(k)
        if k >= 3 and k % 2 == 1:
            third_part(k // 2 - 1)
        if k >= 4 and k % 2 == 0:
            fourth_part(k // 2 - 2)
        if 1 <= k <= HEADS:
            second_part(k - 1)

    if last:
        keep_ref, send_ref = refs[carried + 3 : carried + 5]

        @pl.when(step == pl.num_programs(0) - 1)
        def _():
            half = width // 2
            quarter = half // 4
            total_sums = jnp.sum(sums_ref[...], axis=0, keepdims=True)
            weights = w_ref[...].astype(F32)
            d_gain = jnp.sum((weights * total_ref[...]).reshape(width, 3 * width), axis=1, keepdims=True)
            d_shift = jnp.sum(weights * total_sums, axis=1, keepdims=True)
            columns = jnp.concatenate([vec_ref[...], jnp.zeros((120, width), F32)], axis=0).T
            gain, shift = columns[:, 0:1], columns[:, 1:2]
            total_ref[...] = total_ref[...] * gain + shift * total_sums
            lane = lax.broadcasted_iota(jnp.int32, (1, 128), 1)
            both = jnp.where(lane == 0, d_gain, jnp.where(lane == 1, d_shift, 0.0)).T

            def emit(group, quad, ref, side):
                base = group * half + quad * quarter
                for kind in range(3):
                    for pair in range(pairs):
                        source = slice((3 * pair + kind) * 128, (3 * pair + kind) * 128 + 128)
                        ref[group, side, kind * quarter : (kind + 1) * quarter, pair * 128 : pair * 128 + 128] = (
                            total_ref[base : base + quarter, source].astype(BF16)
                        )
                if quad == 0:
                    kind = 2 * group
                    value = jnp.concatenate(
                        [total_sums[:, (3 * p + kind) * 128 : (3 * p + kind) * 128 + 128] for p in range(pairs)], axis=1
                    )
                else:
                    own = slice(group * half, group * half + half)
                    value = jnp.concatenate([both[0:1, own], both[1:2, own]], axis=1)
                ref[group, side, 3 * quarter : 3 * quarter + 16, :] = jnp.broadcast_to(value, (16, width)).astype(BF16)

            split_quads(idx_ref[1], emit, keep_ref, send_ref)


def input_grad_kernel(x_ref, dqkv_ref, dx_ref, w_ref, vec_ref, din_ref, view, outs, xs, wt):
    step = pl.program_id(0)
    width = w_ref.shape[0]
    seq = x_ref.shape[0] * 128 // (width * 2 * pl.num_programs(0))
    rows = xs.shape[0]

    @pl.when(step == 0)
    def _():
        view[...] = x_ref[...].astype(F32)
        wt[...] = w_ref[...].T
        xs[...] = jnp.zeros_like(xs)

    for slot in range(2):
        read_image(view, step, slot, seq, xs, slot * ROWS)
    d_normed = mm(dqkv_ref[...].reshape(rows, 3 * width), wt[...])
    hat, rstd = normalize(xs[...])
    d_in = dx_ref[...].reshape(rows, width) + norm_back(d_normed, hat, rstd, vec_ref[0:1, :])
    for slot in range(2):
        write_image(outs, step, slot, seq, d_in[slot * ROWS : slot * ROWS + ROWS])

    @pl.when(step == pl.num_programs(0) - 1)
    def _():
        din_ref[...] = outs[...].astype(BF16)


def fixed(*shape):
    return pl.BlockSpec(shape, lambda i: (0,) * len(shape))


def per_image(*shape):
    return pl.BlockSpec((1, *shape), lambda i: (i,) + (0,) * len(shape))


SMEM_SPEC = pl.BlockSpec(memory_space=pltpu.SMEM)


def run_attention(count, idx, view, w_qkv, near, far, small):
    width = w_qkv.shape[1] // 3
    return pl.pallas_call(
        attention_kernel,
        grid=(count,),
        in_specs=[SMEM_SPEC] + [VMEM_SPEC] * 5,
        out_specs=[
            per_image(ROWS, 3 * width), per_image(HEADS, ROWS, KEYS), per_image(ROWS, width),
            fixed(width, 3 * width), fixed(8, width),
        ],
        out_shape=[
            pltpu.HBM((count, ROWS, 3 * width), BF16),
            pltpu.HBM((count, HEADS, ROWS, KEYS), BF16),
            pltpu.HBM((count, ROWS, width), BF16),
            jax.ShapeDtypeStruct((width, 3 * width), BF16),
            jax.ShapeDtypeStruct((8, width), F32),
        ],
        scratch_shapes=[
            pltpu.VMEM(view.shape, F32),
            pltpu.VMEM((ROWS, width), F32),
            pltpu.VMEM((KEYS, 2 * width), BF16),
            pltpu.VMEM((8, 3 * width), F32),
            pltpu.VMEM((2, ROWS, KEYS), F32),
        ],
        compiler_params=pltpu.CompilerParams(vmem_limit_bytes=59 << 20),
        cost_estimate=pl.CostEstimate(flops=5 << 30, bytes_accessed=20 << 20, transcendentals=0),
        name="attention_fwd",
    )(idx, view, w_qkv, near, far, small)


def run_mlp(idx, counts, view, cot, att, wo, w1, w2, near, far, small, first):
    width = wo.shape[1]
    hidden = w1.shape[1]
    micro = counts.shape[0]
    rows = 2 * ROWS
    packed = width // 8 * (hidden // width) + hidden // 8 + width // 8 + 16
    two = pl.BlockSpec((2, ROWS, width), lambda i: (i, 0, 0))
    return pl.pallas_call(
        mlp_kernel,
        grid=(micro,),
        in_specs=[SMEM_SPEC, SMEM_SPEC, VMEM_SPEC, VMEM_SPEC, two] + [VMEM_SPEC] * 7,
        out_specs=[VMEM_SPEC, two, two, VMEM_SPEC, VMEM_SPEC],
        out_shape=[
            jax.ShapeDtypeStruct(view.shape, BF16),
            pltpu.HBM(att.shape, F32),
            pltpu.HBM(att.shape, BF16),
            jax.ShapeDtypeStruct((2, 2, packed, width), BF16),
            jax.ShapeDtypeStruct((2, 2, packed, width), BF16),
        ],
        scratch_shapes=[
            pltpu.VMEM(view.shape, F32),
            pltpu.VMEM(view.shape, F32),
            pltpu.VMEM((rows, width), F32),
            pltpu.VMEM((rows, width), F32),
            pltpu.VMEM((rows, hidden), BF16),
            pltpu.VMEM((rows, hidden), BF16),
            pltpu.VMEM((2, rows, 256), F32),
            pltpu.VMEM((2, rows, 256), F32),
            pltpu.VMEM((width, width), BF16),
            pltpu.VMEM((width, hidden), BF16),
            pltpu.VMEM((hidden, width), BF16),
            pltpu.VMEM((width, width), BF16),
            pltpu.VMEM((hidden, width), BF16),
            pltpu.VMEM((width, hidden), BF16),
            pltpu.VMEM((8, width), F32),
            pltpu.VMEM((8, hidden), F32),
            pltpu.VMEM((rows, width), F32),
            pltpu.VMEM((rows, width), F32),
            pltpu.VMEM((width + 16, hidden), F32),
            pltpu.VMEM((width, hidden), F32),
            pltpu.VMEM((width, width), F32),
            pltpu.VMEM((4, 8, width), F32),
        ],
        compiler_params=pltpu.CompilerParams(vmem_limit_bytes=51 << 20),
        cost_estimate=pl.CostEstimate(flops=12 << 30, bytes_accessed=20 << 20, transcendentals=0),
        name="mlp_fwd_bwd",
    )(idx, counts, view, cot, att, wo, w1, w2, near, far, small, first)


def run_attention_back(begin, end, idx, view, qkv, prob, att, datt, w_qkv, vec, carried):
    count = qkv.shape[0]
    width = w_qkv.shape[0]
    packed = width // 8 * 3 + 16
    last = end == count
    block = lambda *shape: pl.BlockSpec((1, *shape), lambda i: (i + begin,) + (0,) * len(shape))
    any_spec = pl.BlockSpec(memory_space=pl.ANY)
    return pl.pallas_call(
        partial(attention_back_kernel, begin, last),
        grid=(end - begin,),
        in_specs=[
            SMEM_SPEC, VMEM_SPEC, block(ROWS, 3 * width), block(HEADS, ROWS, KEYS),
            block(ROWS, width), block(ROWS, width), VMEM_SPEC, VMEM_SPEC,
        ]
        + ([any_spec, VMEM_SPEC, VMEM_SPEC] if carried else []),
        out_specs=[block(ROWS, 3 * width), VMEM_SPEC, VMEM_SPEC] + ([VMEM_SPEC] * 2 if last else []),
        out_shape=[
            pltpu.HBM((count, ROWS, 3 * width), BF16),
            jax.ShapeDtypeStruct((width, 3 * width), F32),
            jax.ShapeDtypeStruct((8, 3 * width), F32),
        ]
        + [jax.ShapeDtypeStruct((2, 2, packed, width), BF16)] * (2 if last else 0),
        scratch_shapes=[
            pltpu.VMEM(view.shape, F32),
            pltpu.VMEM((ROWS, width), F32),
            pltpu.VMEM((KEYS, 2 * width), BF16),
            pltpu.VMEM((width, ROWS), BF16),
            pltpu.VMEM((2, ROWS, KEYS), F32),
            pltpu.VMEM((4, ROWS, KEYS), BF16),
        ],
        input_output_aliases={8: 0} if carried else {},
        compiler_params=pltpu.CompilerParams(vmem_limit_bytes=54 << 20),
        cost_estimate=pl.CostEstimate(flops=(end - begin) << 30, bytes_accessed=20 << 20, transcendentals=0),
    )(idx, view, qkv, prob, att, datt, w_qkv, vec, *carried)


def run_input_grad(view, dqkv, dx, w_qkv, vec):
    count = dqkv.shape[0]
    width = w_qkv.shape[0]
    two = lambda *shape: pl.BlockSpec((2, *shape), lambda i: (i,) + (0,) * len(shape))
    return pl.pallas_call(
        input_grad_kernel,
        grid=(count // 2,),
        in_specs=[VMEM_SPEC, two(ROWS, 3 * width), two(ROWS, width), VMEM_SPEC, VMEM_SPEC],
        out_specs=VMEM_SPEC,
        out_shape=jax.ShapeDtypeStruct(view.shape, BF16),
        scratch_shapes=[
            pltpu.VMEM(view.shape, F32),
            pltpu.VMEM(view.shape, F32),
            pltpu.VMEM((2 * ROWS, width), F32),
            pltpu.VMEM((3 * width, width), BF16),
        ],
        compiler_params=pltpu.CompilerParams(vmem_limit_bytes=57 << 20),
        cost_estimate=pl.CostEstimate(flops=2 << 30, bytes_accessed=20 << 20, transcendentals=0),
        name="input_grad",
    )(view, dqkv, dx, w_qkv, vec)


def merge_kernel(which, idx_ref, a_ref, b_ref, own_ref, other_ref):
    mine = idx_ref[which]
    own_ref[...] = a_ref[mine] + b_ref[mine]
    other_ref[...] = a_ref[1 - mine] + b_ref[1 - mine]


def merge(idx, which, a, b):
    half = jax.ShapeDtypeStruct(a.shape[1:], BF16)
    vmem = pl.BlockSpec(memory_space=pltpu.VMEM)
    return pl.pallas_call(
        partial(merge_kernel, which),
        in_specs=[SMEM_SPEC, vmem, vmem],
        out_specs=[vmem, vmem],
        out_shape=[half, half],
        name="merge",
    )(idx, a, b)


def flip(value, axis, size, bit):
    return lax.ppermute(value, axis, [(i, i ^ bit) for i in range(size)])


def reduce_grads(idx, keep, send, replicas):
    own, other = merge(idx, 0, keep, flip(send, "replica", replicas, 1))
    own, other = merge(idx, 2, own, flip(other, "group", 2, 1))
    own = own + flip(other, "replica", replicas, 2)
    bit = 4
    while bit < replicas:
        own = own + flip(own, "replica", replicas, bit)
        bit *= 2
    side = flip(own, "replica", replicas, 2)
    far_own = flip(own, "replica", replicas, 1)
    return own, side, far_own, flip(side, "replica", replicas, 1)


def unpack_kernel(idx_ref, *refs):
    ins, outs, (mlp, att) = refs[:8], refs[8:20], refs[20:]
    core, side = idx_ref[1], idx_ref[2]
    places = (2 * core + side, 2 * core + 1 - side, 2 * (1 - core) + side, 2 * (1 - core) + 1 - side)
    for k, place in enumerate(places):
        mlp[place] = ins[k][...].astype(F32)
        att[place] = ins[4 + k][...].astype(F32)
    g_qkv, g_bqv, g_out, g_bout, g_fc1, g_bfc1, g_fc2, g_bfc2, g_gone, g_sone, g_gtwo, g_stwo = outs
    half, width = g_out.shape
    hidden = g_fc1.shape[1]
    quarter = half // 4
    wide = hidden // 8
    for quad in range(4):
        rows = slice(quad * quarter, (quad + 1) * quarter)
        top = 0
        for col in range(hidden // width):
            g_fc1[rows, col * width : (col + 1) * width] = mlp[quad, top : top + quarter]
            top += quarter
        g_fc2[quad * wide : (quad + 1) * wide] = mlp[quad, top : top + wide]
        top += wide
        g_out[rows] = mlp[quad, top : top + quarter]
        top += quarter
        value = mlp[quad, top : top + 1]
        if quad < 2:
            g_bfc1[:, quad * width : (quad + 1) * width] = value
        elif quad == 2:
            g_bfc2[...] = value[:, :half]
            g_bout[...] = value[:, half:]
        else:
            g_gtwo[...] = value[:, :half]
            g_stwo[...] = value[:, half:]
        for col in range(3):
            g_qkv[rows, col * width : (col + 1) * width] = att[quad, col * quarter : (col + 1) * quarter]
        value = att[quad, 3 * quarter : 3 * quarter + 1]
        if quad == 0:
            g_bqv[...] = value
        elif quad == 1:
            g_gone[...] = value[:, :half]
            g_sone[...] = value[:, half:]


def run_unpack(idx, mlp, att, shapes):
    vmem = pl.BlockSpec(memory_space=pltpu.VMEM)
    return pl.pallas_call(
        unpack_kernel,
        in_specs=[SMEM_SPEC] + [vmem] * 8,
        out_specs=[vmem] * 12,
        out_shape=[jax.ShapeDtypeStruct(s if len(s) == 2 else (1, *s), F32) for s in shapes],
        scratch_shapes=[pltpu.VMEM((4, *mlp[0].shape), F32), pltpu.VMEM((4, *att[0].shape), F32)],
        compiler_params=pltpu.CompilerParams(vmem_limit_bytes=40 << 20),
        name="unpack",
    )(idx, *mlp, *att)


def interleaved(images):
    micro, slots, seq, width = images.shape
    blocks = images.reshape(micro, slots, seq, width // 128, 128)
    blocks = with_layout_constraint(blocks, Layout(major_to_minor=(0, 2, 3, 1, 4)))
    return blocks.transpose(0, 2, 3, 1, 4).reshape(-1, 128)


def separated(rows, shape):
    micro, slots, seq, width = shape
    blocks = rows.reshape(micro, seq, width // 128, slots, 128).transpose(0, 1, 3, 2, 4)
    return blocks.reshape(micro, seq, slots, width).transpose(0, 2, 1, 3)


SPLITS = ((0, 2), (2, 6), (6, 8))


def local(
    replicas,
    images, image_count, cotangent, w_qkv, b_qv, w_out, b_out, w_fc1, b_fc1, w_fc2, b_fc2,
    gain_one, shift_one, gain_two, shift_two,
):
    replica = lax.axis_index("replica")
    idx = jnp.stack([lax.axis_index("group"), replica & 1, (replica >> 1) & 1]).astype(jnp.int32)
    count = images.shape[0] * images.shape[1]
    vectors = (b_qv, b_out, b_fc1, b_fc2, gain_one, shift_one, gain_two, shift_two)
    first, small = run_pack_first(idx, w_qkv, vectors)
    second = run_pack_second(idx, w_out, w_fc1, w_fc2)
    near_first = flip(first, "group", 2, 1)
    near_second = flip(second, "group", 2, 1)
    far_first = flip(near_first, "replica", replicas, 1)
    far_second = flip(near_second, "replica", replicas, 1)
    view = interleaved(images)
    qkv, prob, att, w_all, vec = run_attention(count, idx, view, w_qkv, near_first, far_first, small)
    out, dx, datt, keep_b, send_b = run_mlp(
        idx, image_count, view, interleaved(cotangent), att, w_out, w_fc1, w_fc2,
        near_second, far_second, small, near_first,
    )
    carried = ()
    for begin, end in SPLITS:
        carried = run_attention_back(begin, end, idx, view, qkv, prob, att, datt, w_all, vec, carried)
    dqkv, _, _, keep_c, send_c = carried
    din = run_input_grad(view, dqkv, dx, w_all, vec)
    mlp = reduce_grads(idx, keep_b, send_b, replicas)
    attention = reduce_grads(idx, keep_c, send_c, replicas)
    shapes = [v.shape for v in (w_qkv, b_qv, w_out, b_out, w_fc1, b_fc1, w_fc2, b_fc2)] + [gain_one.shape] * 4
    grads = run_unpack(idx, mlp, attention, shapes)
    grads = [g.reshape(s) for g, s in zip(grads, shapes)]
    return (separated(out, images.shape), separated(din, images.shape), *grads)


def step(replicas, *args):
    return local(replicas, *args)


def solution(mesh):
    split = P(None, ("group", "replica"), None, None)
    matrix, vector = P("group", None), P("group")
    return jax.shard_map(
        partial(step, mesh.shape["replica"]),
        mesh=mesh,
        in_specs=(split, P(None, ("group", "replica")), split)
        + (matrix, vector) * 4
        + (vector,) * 4,
        out_specs=(split, split) + (matrix, vector) * 4 + (vector,) * 4,
        check_vma=False,
    )
```

time: 217 us -> 194 us (0.89)
  local copies, waits for them, and re-layouts: 30 us -> 5.15 us
  Pallas kernels: 80 us -> 102 us
  waiting for transfers between devices: 62.6 us -> 49.6 us
  other arithmetic: 14.4 us -> 3.05 us
  starting transfers between devices: 27 us -> 32.6 us
    pallas_call x3 -> x13, Pallas kernels: 80 us -> 102 us  [the longest x1 30.4 us: run_mlp(): pl.pallas_call(mlp_kernel, grid=(micro,), in_specs=[SMEM_SPEC, SMEM_SPEC,...]
    ppermute x19 -> x20, waiting for transfers between devices: 62.6 us -> 49.6 us  [flip(): return lax.ppermute(value, axis, [(i, i ^ bit) for i in range(size)])]
    select_n x6 -> x0, other arithmetic: 8.62 us -> none  [the longest x4 8.46 us: full(): jnp.where(group == 0, jnp.concatenate([mine, theirs]), jnp.concatenate([t...]
    unnamed x43 -> x31, local copies, waits for them, and re-layouts: 13.4 us -> 5.15 us
    ppermute x19 -> x20, starting transfers between devices: 27 us -> 32.6 us  [flip(): return lax.ppermute(value, axis, [(i, i ^ bit) for i in range(size)])]
    concatenate x2 -> x0, local copies, waits for them, and re-layouts: 5.57 us -> none  [the longest x1 5.56 us: local(): jnp.concatenate([b_qv, b_out, b_fc1, b_fc2, gain_one, shift_one, gain_two...]
    slice x11 -> x0, local copies, waits for them, and re-layouts: 3.96 us -> none  [the longest x1 1.18 us: local(): g_fc2 = sums_b[:, top:top + wide].reshape(hidden // 2, width)]
    reshape x7 -> x0, local copies, waits for them, and re-layouts: 3.38 us -> none  [the longest x6 2.78 us: local(): offsets[name] = small[:, at:at + size].reshape(1, -1)]
  transfers between devices with their start and end apart: 19 -> 20, of which waited for: 8 -> 9; matrix products, arithmetic and copies ran while one was open for 11% -> 1% of each run, Pallas kernels for 17% -> 32%
where the time goes in v2:
time: 194 us; the launch traced here: 193 us
  Pallas kernels  102 us (53%)
  waiting for transfers between devices  49.6 us (26%)
  starting transfers between devices  32.6 us (17%)
  local copies, waits for them, and re-layouts  5.15 us (3%)
  other arithmetic  3.05 us (2%)
    ppermute x20, waiting for transfers between devices, flip(): return lax.ppermute(value, axis, [(i, i ^ bit) for i in range(size)])  49.6 us
    ppermute x20, starting transfers between devices, flip(): return lax.ppermute(value, axis, [(i, i ^ bit) for i in range(size)])  32.6 us
    pallas_call x1, Pallas kernels, run_mlp(): pl.pallas_call(mlp_kernel, grid=(micro,), in_specs=[SMEM_SPEC, SMEM_SPEC,...  30.4 us
    pallas_call x3, Pallas kernels, run_attention_back(): pl.pallas_call(partial(attention_back_kernel, begin, last), grid=(end - b...  30.2 us
    pallas_call x1, Pallas kernels, run_attention(): pl.pallas_call(attention_kernel, grid=(count,), in_specs=[SMEM_SPEC] + [V...  17 us
    pallas_call x4, Pallas kernels, merge(): pl.pallas_call(partial(merge_kernel, which), in_specs=[SMEM_SPEC, vmem, v...  9.14 us
    pallas_call x1, Pallas kernels, run_input_grad(): pl.pallas_call(input_grad_kernel, grid=(count // 2,), in_specs=[VMEM_SPEC...  7.75 us
    unnamed x31, local copies, waits for them, and re-layouts  5.15 us
  transfers between devices with their start and end apart: 20, of which 9 were waited for; matrix products, arithmetic and copies ran while one was open for 1% of the time, Pallas kernels for 32%

profile of v2, /device:TPU:1, one launch (start us, length us, event | category | flops | bytes accessed | tf_op | source)
XLA Modules:
  0.0 193.4 jit_solution(13412505682876054083)
XLA Ops:
  1.2 2.6 %pack_second.1 = bf16[96,3456]{1,0:T(8,128)(2,1)} custom-call(s32[3]{0:T(128)} %pad_add_fusion.idx_ref, bf16[192,384]{1,0:T(8,128)(2,1)} %wo_ref.3, bf16[192,1536]{1,0:T(8,128)(2,1)} %w1_ref.3, bf16[768,384]{1,0:T(8,128)(2,1)} %w2_ref.3), custom_call_target="tpu_custom_call" | custom-call | tf_op jit(solution)/shard_map/pack_second/pallas_call | solution.py:141
  5.9 2.4 %pack_first.1 = (bf16[112,1152]{1,0:T(8,128)(2,1)}, bf16[8,768]{1,0:T(8,128)(2,1)}) custom-call(s32[3]{0:T(128)} %pad_add_fusion.idx_ref, bf16[192,1152]{1,0:T(8,128)(2,1)} %w_ref.1, bf16[384]{0:T(512)(128)(2,1)} %refs_0_.1, bf16[192]{0:T(256)(128)(2,1)} %refs_1_.1, bf16[768]{0:T(1024)(128)(2,1)} %refs_2_.1, bf16[192]{0:T(256)(128)(2,1)} %refs_3_.1, ...), custom_call_target="tpu_custom_call" | custom-call | tf_op jit(solution)/shard_map/pack_first/pallas_call | solution.py:123
  8.4 17.9 %collective-permute-done.near_ref.first_ref = bf16[112,1152]{1,0:T(8,128)(2,1)S(1)} collective-permute-done((bf16[112,1152]{1,0:T(8,128)(2,1)}, bf16[112,1152]{1,0:T(8,128)(2,1)S(1)}, u32[]{:S(2)}, u32[]{:S(2)}) %collective-permute-start) | collective-permute-done | bytes 258080 | tf_op jit(solution)/shard_map/ppermute | solution.py:697
  29.4 17.0 %attention_fwd.1 = (bf16[8,208,1152]{2,1,0:T(8,128)(2,1)}, bf16[8,6,208,256]{3,2,1,0:T(8,128)(2,1)}, bf16[8,208,384]{2,1,0:T(8,128)(2,1)}, bf16[384,1152]{1,0:T(8,128)(2,1)}, f32[8,384]{1,0:T(8,128)}) custom-call(s32[3]{0:T(128)} %pad_add_fusion.idx_ref, bf16[4728,128]{1,0:T(8,128)(2,1)} %bitcast.33, bf16[192,1152]{1,0:T(8,128)(2,1)} %w_ref.1, ...), custom_call_target="tpu_custom_call" | custom-call | flops 5368709120 | bytes 20971520 | tf_op jit(solution)/shard_map/attention_fwd/pallas_call | solution.py:543
  47.4 30.4 %mlp_fwd_bwd.1 = (bf16[4728,128]{1,0:T(8,128)(2,1)}, f32[8,208,384]{2,1,0:T(8,128)}, bf16[8,208,384]{2,1,0:T(8,128)(2,1)}, bf16[2,2,448,384]{3,2,1,0:T(8,128)(2,1)}, bf16[2,2,448,384]{3,2,1,0:T(8,128)(2,1)}) custom-call(s32[3]{0:T(128)S(1)} %copy-done.3, s32[4,1]{1,0:T(4,128)S(1)} %copy.31.count_ref, bf16[4728,128]{1,0:T(8,128)(2,1)} %bitcast.34, ...), custom_call_target="tpu_custom_call" | custom-call | flops 12884901888 | bytes 20971520 | tf_op jit(solution)/shard_map/mlp_fwd_bwd/pallas_call | solution.py:578
  78.2 3.0 %collective-permute-done.4.b_ref = bf16[2,2,448,384]{3,2,1,0:T(8,128)(2,1)S(1)} collective-permute-done((bf16[2,2,448,384]{3,2,1,0:T(8,128)(2,1)}, bf16[2,2,448,384]{3,2,1,0:T(8,128)(2,1)S(1)}, u32[]{:S(2)}, u32[]{:S(2)}) %collective-permute-start.4) | collective-permute-done | bytes 1376288 | tf_op jit(solution)/shard_map/ppermute | solution.py:697
  82.3 3.0 %merge.4 = (bf16[2,448,384]{2,1,0:T(8,128)(2,1)}, bf16[2,448,384]{2,1,0:T(8,128)(2,1)}) custom-call(s32[3]{0:T(128)} %pad_add_fusion.idx_ref, bf16[2,2,448,384]{3,2,1,0:T(8,128)(2,1)} %get-tuple-element.72.a_ref, bf16[2,2,448,384]{3,2,1,0:T(8,128)(2,1)} %copy-done.8), custom_call_target="tpu_custom_call" | custom-call | tf_op jit(solution)/shard_map/merge/pallas_call | solution.py:687
  86.8 7.9 %shard_map.254 = (bf16[8,208,1152]{2,1,0:T(8,128)(2,1)}, f32[384,1152]{1,0:T(8,128)}, f32[8,1152]{1,0:T(8,128)}) custom-call(s32[3]{0:T(128)} %pad_add_fusion.idx_ref, bf16[4728,128]{1,0:T(8,128)(2,1)} %bitcast.35, bf16[8,208,1152]{2,1,0:T(8,128)(2,1)} %get-tuple-element.59.qkv_ref, bf16[8,6,208,256]{3,2,1,0:T(8,128)(2,1)} %get-tuple-element.60.prob_ref, ...), custom_call_target="tpu_custom_call" | custom-call | flops 2147483648 | bytes 20971520 | tf_op jit(solution)/shard_map/pallas_call | solution.py:627
  94.7 7.5 %collective-permute-done.5.b_ref = bf16[2,448,384]{2,1,0:T(8,128)(2,1)S(1)} collective-permute-done((bf16[2,448,384]{2,1,0:T(8,128)(2,1)}, bf16[2,448,384]{2,1,0:T(8,128)(2,1)S(1)}, u32[]{:S(2)}, u32[]{:S(2)}) %collective-permute-start.5) | collective-permute-done | bytes 688160 | tf_op jit(solution)/shard_map/ppermute | solution.py:697
  103.0 2.3 %merge.5 = (bf16[448,384]{1,0:T(8,128)(2,1)}, bf16[448,384]{1,0:T(8,128)(2,1)}) custom-call(s32[3]{0:T(128)} %pad_add_fusion.idx_ref, bf16[2,448,384]{2,1,0:T(8,128)(2,1)} %get-tuple-element.74.a_ref, bf16[2,448,384]{2,1,0:T(8,128)(2,1)} %copy-done.9), custom_call_target="tpu_custom_call" | custom-call | tf_op jit(solution)/shard_map/merge/pallas_call | solution.py:687
  106.8 12.5 %shard_map.255 = (bf16[8,208,1152]{2,1,0:T(8,128)(2,1)}, f32[384,1152]{1,0:T(8,128)}, f32[8,1152]{1,0:T(8,128)}) custom-call(s32[3]{0:T(128)} %pad_add_fusion.idx_ref, bf16[4728,128]{1,0:T(8,128)(2,1)} %bitcast.36, bf16[8,208,1152]{2,1,0:T(8,128)(2,1)} %get-tuple-element.59.qkv_ref, ...), custom_call_target="tpu_custom_call", output_to_operand_aliasing={{0}: (8, {})} | custom-call | flops 4294967296 | bytes 20971520 | tf_op jit(solution)/shard_map/pallas_call | solution.py:627
  119.3 9.7 %shard_map.256 = (bf16[8,208,1152]{2,1,0:T(8,128)(2,1)}, f32[384,1152]{1,0:T(8,128)}, f32[8,1152]{1,0:T(8,128)}, bf16[2,2,160,384]{3,2,1,0:T(8,128)(2,1)}, bf16[2,2,160,384]{3,2,1,0:T(8,128)(2,1)}) custom-call(s32[3]{0:T(128)} %pad_add_fusion.idx_ref, bf16[4728,128]{1,0:T(8,128)(2,1)} %bitcast.37, ...), custom_call_target="tpu_custom_call", output_to_operand_aliasing={{0}: (8, {})} | custom-call | flops 2147483648 | bytes 20971520 | tf_op jit(solution)/shard_map/pallas_call | solution.py:627
  132.0 8.3 %collective-permute-done.7 = bf16[448,384]{1,0:T(8,128)(2,1)S(1)} collective-permute-done((bf16[448,384]{1,0:T(8,128)(2,1)S(1)}, bf16[448,384]{1,0:T(8,128)(2,1)S(1)}, u32[]{:S(2)}, u32[]{:S(2)}) %collective-permute-start.7) | collective-permute-done | bytes 344096 | tf_op jit(solution)/shard_map/ppermute | solution.py:697
  140.4 2.4 %collective-permute-start.8 = (bf16[448,384]{1,0:T(8,128)(2,1)S(1)}, bf16[448,384]{1,0:T(8,128)(2,1)S(1)}, u32[]{:S(2)}, u32[]{:S(2)}) collective-permute-start(bf16[448,384]{1,0:T(8,128)(2,1)S(1)} %add.19), channel_id=1, source_target_pairs={{0,8},{1,9},{2,10},{3,11},{4,12},{5,13},{6,14},{7,15},{8,0},{9,1},... | collective-permute-start | bytes 1032200 | tf_op jit(solution)/shard_map/ppermute | solution.py:697
  143.6 2.0 %merge.6 = (bf16[2,160,384]{2,1,0:T(8,128)(2,1)}, bf16[2,160,384]{2,1,0:T(8,128)(2,1)}) custom-call(s32[3]{0:T(128)} %pad_add_fusion.idx_ref, bf16[2,2,160,384]{3,2,1,0:T(8,128)(2,1)} %get-tuple-element.78.a_ref, bf16[2,2,160,384]{3,2,1,0:T(8,128)(2,1)} %copy-done.10), custom_call_target="tpu_custom_call" | custom-call | tf_op jit(solution)/shard_map/merge/pallas_call | solution.py:687
  146.8 5.3 %collective-permute-done.13.b_ref = bf16[2,160,384]{2,1,0:T(8,128)(2,1)S(1)} collective-permute-done((bf16[2,160,384]{2,1,0:T(8,128)(2,1)}, bf16[2,160,384]{2,1,0:T(8,128)(2,1)S(1)}, u32[]{:S(2)}, u32[]{:S(2)}) %collective-permute-start.13) | collective-permute-done | bytes 245792 | tf_op jit(solution)/shard_map/ppermute | solution.py:697
  154.9 2.8 %collective-permute-done.8 = bf16[448,384]{1,0:T(8,128)(2,1)S(1)} collective-permute-done((bf16[448,384]{1,0:T(8,128)(2,1)S(1)}, bf16[448,384]{1,0:T(8,128)(2,1)S(1)}, u32[]{:S(2)}, u32[]{:S(2)}) %collective-permute-start.8) | collective-permute-done | bytes 344096 | tf_op jit(solution)/shard_map/ppermute | solution.py:697
  160.9 3.0 %collective-permute-done.15 = bf16[160,384]{1,0:T(8,128)(2,1)S(1)} collective-permute-done((bf16[160,384]{1,0:T(8,128)(2,1)S(1)}, bf16[160,384]{1,0:T(8,128)(2,1)S(1)}, u32[]{:S(2)}, u32[]{:S(2)}) %collective-permute-start.15) | collective-permute-done | bytes 122912 | tf_op jit(solution)/shard_map/ppermute | solution.py:697
  163.9 2.4 %collective-permute-start.16 = (bf16[160,384]{1,0:T(8,128)(2,1)S(1)}, bf16[160,384]{1,0:T(8,128)(2,1)S(1)}, u32[]{:S(2)}, u32[]{:S(2)}) collective-permute-start(bf16[160,384]{1,0:T(8,128)(2,1)S(1)} %add.22), channel_id=1, source_target_pairs={{0,8},{1,9},{2,10},{3,11},{4,12},{5,13},{6,14},{7,15},{8,0},{9,1},... | collective-permute-start | bytes 368648 | tf_op jit(solution)/shard_map/ppermute | solution.py:697
  166.3 3.6 %collective-permute-start.10 = (bf16[448,384]{1,0:T(8,128)(2,1)S(1)}, bf16[448,384]{1,0:T(8,128)(2,1)S(1)}, u32[]{:S(2)}, u32[]{:S(2)}) collective-permute-start(bf16[448,384]{1,0:T(8,128)(2,1)S(1)} %add.20.refs_0_), channel_id=1, source_target_pairs={{0,1},{1,0},{2,3},{3,2},{4,5},{5,4},{6,7},{7,6},{8,9},{9,8},{10,11... | collective-permute-start | bytes 1032200 | tf_op jit(solution)/shard_map/ppermute | solution.py:697
  170.1 6.9 %collective-permute-start.18 = (bf16[160,384]{1,0:T(8,128)(2,1)S(1)}, bf16[160,384]{1,0:T(8,128)(2,1)S(1)}, u32[]{:S(2)}, u32[]{:S(2)}) collective-permute-start(bf16[160,384]{1,0:T(8,128)(2,1)S(1)} %add.23.refs_4_), channel_id=1, source_target_pairs={{0,1},{1,0},{2,3},{3,2},{4,5},{5,4},{6,7},{7,6},{8,9},{9,8},{10,11... | collective-permute-start | bytes 368648 | tf_op jit(solution)/shard_map/ppermute | solution.py:697
  177.0 4.8 %collective-permute-start.19 = (bf16[160,384]{1,0:T(8,128)(2,1)S(1)}, bf16[160,384]{1,0:T(8,128)(2,1)S(1)}, u32[]{:S(2)}, u32[]{:S(2)}) collective-permute-start(bf16[160,384]{1,0:T(8,128)(2,1)S(1)} %collective-permute-done.17.refs_5_), channel_id=1, source_target_pairs={{0,1},{1,0},{2,3},{3,2},{4,5},{5,4},{6,7},{7,6},{8,9},{9,8},{10,11... | collective-permute-start | bytes 368648 | tf_op jit(solution)/shard_map/ppermute | solution.py:697
  181.8 7.7 %input_grad.1 = bf16[4728,128]{1,0:T(8,128)(2,1)} custom-call(bf16[4728,128]{1,0:T(8,128)(2,1)} %bitcast.38, bf16[8,208,1152]{2,1,0:T(8,128)(2,1)} %get-tuple-element.70.dqkv_ref, f32[8,208,384]{2,1,0:T(8,128)} %get-tuple-element.71.dx_ref, bf16[384,1152]{1,0:T(8,128)(2,1)} %get-tuple-element.62.w_ref, f32[8,384]{1,0:T(8,128)} %get-tuple-element.63.vec_ref), custom_call_target="tpu_custom_call" | custom-call | flops 2147483648 | bytes 20971520 | tf_op jit(solution)/shard_map/input_grad/pallas_call | solution.py:660
  189.6 2.6 %unpack.1 = (f32[192,1152]{1,0:T(8,128)}, f32[1,384]{1,0:T(1,128)S(1)}, f32[192,384]{1,0:T(8,128)}, f32[1,192]{1,0:T(1,128)}, f32[192,1536]{1,0:T(8,128)}, /*ind...) custom-call(s32[3]{0:T(128)S(1)} %copy-done.4, ...), custom_call_target="tpu_custom_call" | custom-call | tf_op jit(solution)/shard_map/unpack/pallas_call | solution.py:756
  (69 shorter events, 24.4 us)
Async XLA Ops:
  0.6 27.0 %copy-start.13 = (s32[4,1]{0,1:T(1,128)S(1)}, s32[4,1]{0,1:T(1,128)}, u32[]{:S(2)}) copy-start(s32[4,1]{0,1:T(1,128)} %param.16) | copy-start | bytes 52
  3.9 23.6 %collective-permute-start.2 = (bf16[96,3456]{1,0:T(8,128)(2,1)}, bf16[96,3456]{1,0:T(8,128)(2,1)S(1)}, u32[]{:S(2)}, u32[]{:S(2)}) collective-permute-start(bf16[96,3456]{1,0:T(8,128)(2,1)} %pack_second.1), channel_id=1, source_target_pairs={{0,16},{16,0},{1,17},{17,1},{2,18},{18,2},{3,19},{19,3},{4,20},{20... | collective-permute-start | bytes 1990664 | tf_op jit(solution)/shard_map/ppermute | solution.py:697
  8.4 17.9 %collective-permute-start = (bf16[112,1152]{1,0:T(8,128)(2,1)}, bf16[112,1152]{1,0:T(8,128)(2,1)S(1)}, u32[]{:S(2)}, u32[]{:S(2)}) collective-permute-start(bf16[112,1152]{1,0:T(8,128)(2,1)} %get-tuple-element.55), channel_id=1, source_target_pairs={{0,16},{16,0},{1,17},{17,1},{2,18},{18,2},{3,19},{19,3},{4,20},{20... | collective-permute-start | bytes 774152 | tf_op jit(solution)/shard_map/ppermute | solution.py:697
  26.3 2.4 %collective-permute-start.1 = (bf16[112,1152]{1,0:T(8,128)(2,1)S(1)}, bf16[112,1152]{1,0:T(8,128)(2,1)S(1)}, u32[]{:S(2)}, u32[]{:S(2)}) collective-permute-start(bf16[112,1152]{1,0:T(8,128)(2,1)S(1)} %collective-permute-done.near_ref.first_ref), channel_id=1, source_target_pairs={{0,1},{1,0},{2,3},{3,2},{4,5},{5,4},{6,7},{7,6},{8,9},{9,8},{10,11... | collective-permute-start | bytes 774152 | tf_op jit(solution)/shard_map/ppermute | solution.py:697
  27.5 18.8 %collective-permute-start.3 = (bf16[96,3456]{1,0:T(8,128)(2,1)S(1)}, bf16[96,3456]{1,0:T(8,128)(2,1)S(1)}, u32[]{:S(2)}, u32[]{:S(2)}) collective-permute-start(bf16[96,3456]{1,0:T(8,128)(2,1)S(1)} %collective-permute-done.2.near_ref), channel_id=1, source_target_pairs={{0,1},{1,0},{2,3},{3,2},{4,5},{5,4},{6,7},{7,6},{8,9},{9,8},{10,11... | collective-permute-start | bytes 1990664 | tf_op jit(solution)/shard_map/ppermute | solution.py:697
  29.4 17.0 %copy-start.2 = (bf16[192,384]{1,0:T(8,128)(2,1)S(1)}, bf16[192,384]{1,0:T(8,128)(2,1)}, u32[]{:S(2)}) copy-start(bf16[192,384]{1,0:T(8,128)(2,1)} %wo_ref.3) | copy-start | bytes 442372
  29.4 17.0 %copy-start.3 = (s32[3]{0:T(128)S(1)}, s32[3]{0:T(128)}, u32[]{:S(2)}) copy-start(s32[3]{0:T(128)} %pad_add_fusion.idx_ref) | copy-start | bytes 40
  29.4 17.0 %copy-start.7 = (bf16[8,768]{1,0:T(8,128)(2,1)S(1)}, bf16[8,768]{1,0:T(8,128)(2,1)}, u32[]{:S(2)}) copy-start(bf16[8,768]{1,0:T(8,128)(2,1)} %get-tuple-element.56.small_ref) | copy-start | bytes 36868
  77.8 3.4 %collective-permute-start.4 = (bf16[2,2,448,384]{3,2,1,0:T(8,128)(2,1)}, bf16[2,2,448,384]{3,2,1,0:T(8,128)(2,1)S(1)}, u32[]{:S(2)}, u32[]{:S(2)}) collective-permute-start(bf16[2,2,448,384]{3,2,1,0:T(8,128)(2,1)} %get-tuple-element.73), channel_id=1, source_target_pairs={{0,1},{1,0},{2,3},{3,2},{4,5},{5,4},{6,7},{7,6},{8,9},{9,8},{10,11... | collective-permute-start | bytes 4128776 | tf_op jit(solution)/shard_map/ppermute | solution.py:697
  85.3 16.8 %collective-permute-start.5 = (bf16[2,448,384]{2,1,0:T(8,128)(2,1)}, bf16[2,448,384]{2,1,0:T(8,128)(2,1)S(1)}, u32[]{:S(2)}, u32[]{:S(2)}) collective-permute-start(bf16[2,448,384]{2,1,0:T(8,128)(2,1)} %get-tuple-element.75), channel_id=1, source_target_pairs={{0,16},{16,0},{1,17},{17,1},{2,18},{18,2},{3,19},{19,3},{4,20},{20... | collective-permute-start | bytes 2064392 | tf_op jit(solution)/shard_map/ppermute | solution.py:697
  105.3 25.3 %collective-permute-start.6 = (bf16[448,384]{1,0:T(8,128)(2,1)}, bf16[448,384]{1,0:T(8,128)(2,1)S(1)}, u32[]{:S(2)}, u32[]{:S(2)}) collective-permute-start(bf16[448,384]{1,0:T(8,128)(2,1)} %get-tuple-element.77), channel_id=1, source_target_pairs={{0,2},{1,3},{2,0},{3,1},{4,6},{5,7},{6,4},{7,5},{8,10},{9,11},{10,... | collective-permute-start | bytes 1032200 | tf_op jit(solution)/shard_map/ppermute | solution.py:697
  129.0 13.8 %collective-permute-start.12 = (bf16[2,2,160,384]{3,2,1,0:T(8,128)(2,1)}, bf16[2,2,160,384]{3,2,1,0:T(8,128)(2,1)S(1)}, u32[]{:S(2)}, u32[]{:S(2)}) collective-permute-start(bf16[2,2,160,384]{3,2,1,0:T(8,128)(2,1)} %get-tuple-element.79), channel_id=1, source_target_pairs={{0,1},{1,0},{2,3},{3,2},{4,5},{5,4},{6,7},{7,6},{8,9},{9,8},{10,11... | collective-permute-start | bytes 1474568 | tf_op jit(solution)/shard_map/ppermute | solution.py:697
  130.7 9.7 %collective-permute-start.7 = (bf16[448,384]{1,0:T(8,128)(2,1)S(1)}, bf16[448,384]{1,0:T(8,128)(2,1)S(1)}, u32[]{:S(2)}, u32[]{:S(2)}) collective-permute-start(bf16[448,384]{1,0:T(8,128)(2,1)S(1)} %add.18), channel_id=1, source_target_pairs={{0,4},{1,5},{2,6},{3,7},{4,0},{5,1},{6,2},{7,3},{8,12},{9,13},{10,... | collective-permute-start | bytes 1032200 | tf_op jit(solution)/shard_map/ppermute | solution.py:697
  140.4 17.3 %collective-permute-start.8 = (bf16[448,384]{1,0:T(8,128)(2,1)S(1)}, bf16[448,384]{1,0:T(8,128)(2,1)S(1)}, u32[]{:S(2)}, u32[]{:S(2)}) collective-permute-start(bf16[448,384]{1,0:T(8,128)(2,1)S(1)} %add.19), channel_id=1, source_target_pairs={{0,8},{1,9},{2,10},{3,11},{4,12},{5,13},{6,14},{7,15},{8,0},{9,1},... | collective-permute-start | bytes 1032200 | tf_op jit(solution)/shard_map/ppermute | solution.py:697
  145.6 6.6 %collective-permute-start.13 = (bf16[2,160,384]{2,1,0:T(8,128)(2,1)}, bf16[2,160,384]{2,1,0:T(8,128)(2,1)S(1)}, u32[]{:S(2)}, u32[]{:S(2)}) collective-permute-start(bf16[2,160,384]{2,1,0:T(8,128)(2,1)} %get-tuple-element.81), channel_id=1, source_target_pairs={{0,16},{16,0},{1,17},{17,1},{2,18},{18,2},{3,19},{19,3},{4,20},{20... | collective-permute-start | bytes 737288 | tf_op jit(solution)/shard_map/ppermute | solution.py:697
  154.7 4.2 %collective-permute-start.14 = (bf16[160,384]{1,0:T(8,128)(2,1)}, bf16[160,384]{1,0:T(8,128)(2,1)S(1)}, u32[]{:S(2)}, u32[]{:S(2)}) collective-permute-start(bf16[160,384]{1,0:T(8,128)(2,1)} %get-tuple-element.83), channel_id=1, source_target_pairs={{0,2},{1,3},{2,0},{3,1},{4,6},{5,7},{6,4},{7,5},{8,10},{9,11},{10,... | collective-permute-start | bytes 368648 | tf_op jit(solution)/shard_map/ppermute | solution.py:697
  157.8 12.1 %collective-permute-start.9 = (bf16[448,384]{1,0:T(8,128)(2,1)S(1)}, bf16[448,384]{1,0:T(8,128)(2,1)S(1)}, u32[]{:S(2)}, u32[]{:S(2)}) collective-permute-start(bf16[448,384]{1,0:T(8,128)(2,1)S(1)} %add.20.refs_0_), channel_id=1, source_target_pairs={{0,2},{1,3},{2,0},{3,1},{4,6},{5,7},{6,4},{7,5},{8,10},{9,11},{10,... | collective-permute-start | bytes 1032200 | tf_op jit(solution)/shard_map/ppermute | solution.py:697
  159.8 4.1 %collective-permute-start.15 = (bf16[160,384]{1,0:T(8,128)(2,1)S(1)}, bf16[160,384]{1,0:T(8,128)(2,1)S(1)}, u32[]{:S(2)}, u32[]{:S(2)}) collective-permute-start(bf16[160,384]{1,0:T(8,128)(2,1)S(1)} %add.21), channel_id=1, source_target_pairs={{0,4},{1,5},{2,6},{3,7},{4,0},{5,1},{6,2},{7,3},{8,12},{9,13},{10,... | collective-permute-start | bytes 368648 | tf_op jit(solution)/shard_map/ppermute | solution.py:697
  163.9 6.1 %collective-permute-start.16 = (bf16[160,384]{1,0:T(8,128)(2,1)S(1)}, bf16[160,384]{1,0:T(8,128)(2,1)S(1)}, u32[]{:S(2)}, u32[]{:S(2)}) collective-permute-start(bf16[160,384]{1,0:T(8,128)(2,1)S(1)} %add.22), channel_id=1, source_target_pairs={{0,8},{1,9},{2,10},{3,11},{4,12},{5,13},{6,14},{7,15},{8,0},{9,1},... | collective-permute-start | bytes 368648 | tf_op jit(solution)/shard_map/ppermute | solution.py:697
  166.3 23.3 %collective-permute-start.10 = (bf16[448,384]{1,0:T(8,128)(2,1)S(1)}, bf16[448,384]{1,0:T(8,128)(2,1)S(1)}, u32[]{:S(2)}, u32[]{:S(2)}) collective-permute-start(bf16[448,384]{1,0:T(8,128)(2,1)S(1)} %add.20.refs_0_), channel_id=1, source_target_pairs={{0,1},{1,0},{2,3},{3,2},{4,5},{5,4},{6,7},{7,6},{8,9},{9,8},{10,11... | collective-permute-start | bytes 1032200 | tf_op jit(solution)/shard_map/ppermute | solution.py:697
  169.9 19.7 %collective-permute-start.11 = (bf16[448,384]{1,0:T(8,128)(2,1)S(1)}, bf16[448,384]{1,0:T(8,128)(2,1)S(1)}, u32[]{:S(2)}, u32[]{:S(2)}) collective-permute-start(bf16[448,384]{1,0:T(8,128)(2,1)S(1)} %collective-permute-done.9.refs_1_), channel_id=1, source_target_pairs={{0,1},{1,0},{2,3},{3,2},{4,5},{5,4},{6,7},{7,6},{8,9},{9,8},{10,11... | collective-permute-start | bytes 1032200 | tf_op jit(solution)/shard_map/ppermute | solution.py:697
  170.0 7.0 %collective-permute-start.17 = (bf16[160,384]{1,0:T(8,128)(2,1)S(1)}, bf16[160,384]{1,0:T(8,128)(2,1)S(1)}, u32[]{:S(2)}, u32[]{:S(2)}) collective-permute-start(bf16[160,384]{1,0:T(8,128)(2,1)S(1)} %add.23.refs_4_), channel_id=1, source_target_pairs={{0,2},{1,3},{2,0},{3,1},{4,6},{5,7},{6,4},{7,5},{8,10},{9,11},{10,... | collective-permute-start | bytes 368648 | tf_op jit(solution)/shard_map/ppermute | solution.py:697
  170.1 19.4 %collective-permute-start.18 = (bf16[160,384]{1,0:T(8,128)(2,1)S(1)}, bf16[160,384]{1,0:T(8,128)(2,1)S(1)}, u32[]{:S(2)}, u32[]{:S(2)}) collective-permute-start(bf16[160,384]{1,0:T(8,128)(2,1)S(1)} %add.23.refs_4_), channel_id=1, source_target_pairs={{0,1},{1,0},{2,3},{3,2},{4,5},{5,4},{6,7},{7,6},{8,9},{9,8},{10,11... | collective-permute-start | bytes 368648 | tf_op jit(solution)/shard_map/ppermute | solution.py:697
  177.0 12.6 %collective-permute-start.19 = (bf16[160,384]{1,0:T(8,128)(2,1)S(1)}, bf16[160,384]{1,0:T(8,128)(2,1)S(1)}, u32[]{:S(2)}, u32[]{:S(2)}) collective-permute-start(bf16[160,384]{1,0:T(8,128)(2,1)S(1)} %collective-permute-done.17.refs_5_), channel_id=1, source_target_pairs={{0,1},{1,0},{2,3},{3,2},{4,5},{5,4},{6,7},{7,6},{8,9},{9,8},{10,11... | collective-permute-start | bytes 368648 | tf_op jit(solution)/shard_map/ppermute | solution.py:697
  (11 other events, 60.5 us)

commit v3 on v2

--- a/solution.py
+++ b/solution.py
@@ -80,6 +80,37 @@
     low = idx_ref[0] == 0
     mine, theirs = mine.astype(F32), theirs.astype(F32)
     return jnp.where(low, mine, theirs), jnp.where(low, theirs, mine)
+
+
+def fetch(pairs, sem, first, step, steps):
+    def copies(k, slot):
+        return [
+            pltpu.make_async_copy(source.at[pl.ds(2 * (first + k), 2)], target.at[slot], sem.at[n, slot])
+            for n, (source, target) in enumerate(pairs)
+        ]
+
+    now = lax.rem(step, 2)
+
+    @pl.when(step == 0)
+    def _():
+        for copy in copies(0, 0):
+            copy.start()
+
+    @pl.when(step + 1 < steps)
+    def _():
+        for copy in copies(step + 1, 1 - now):
+            copy.start()
+
+    for copy in copies(step, now):
+        copy.wait()
+    return [target.at[now] for _, target in pairs]
+
+
+HBM_SPEC = pl.BlockSpec(memory_space=pltpu.HBM)
+
+
+def in_hbm(*arrays):
+    return [pltpu.with_memory_space_constraint(array, pltpu.HBM) for array in arrays]
 
 
 def at(start, size):
@@ -153,25 +184,27 @@
 
 def attention_kernel(
     idx_ref, x_ref, w_ref, near_ref, far_ref, small_ref,
-    qkv_ref, prob_ref, att_ref, whole_ref, vec_ref,
-    view, xs, kv, bias, scores,
+    qkv_ref, prob_ref, att_ref, hat_ref, rstd_ref, whole_ref, vec_ref, b1_ref,
+    raw, view, xs, kv, bias, scores, raw_sem,
 ):
     step = pl.program_id(0)
     half, wide = w_ref.shape
     width = wide // 3
     part = half // 2
     pairs = width // 128
-    seq = x_ref.shape[0] * 128 // (width * pl.num_programs(0))
+    seq = x_ref.shape[0] * 128 // (width * 2 * pl.num_programs(0))
 
     @pl.when(step == 0)
     def _():
-        view[...] = x_ref[...].astype(F32)
+        load = pltpu.make_async_copy(x_ref, raw, raw_sem)
+        load.start()
         xs[...] = jnp.zeros_like(xs)
         kv[...] = jnp.zeros_like(kv)
         group, core = idx_ref[0], idx_ref[1]
         first, second = ordered(idx_ref, small_ref[...], near_ref[part : part + 8, : small_ref.shape[1]])
-        vec_ref[0:1, :] = joined(first, second, 4, half)
-        vec_ref[1:2, :] = joined(first, second, 5, half)
+        for k, row in enumerate((4, 5, 1, 3, 6, 7)):
+            vec_ref[k : k + 1, :] = joined(first, second, row, half)
+        b1_ref[0:1, :] = jnp.concatenate([first[2:3, :], second[2:3, :]], axis=1)
         other = (1 - group) * half
         for pair in range(pairs):
             for kind in range(3):
@@ -183,9 +216,14 @@
                 lanes = slice(pair * 128, pair * 128 + 128)
                 piece = (first[0:1, lanes], jnp.zeros((1, 128), F32), second[0:1, lanes])[kind]
                 bias[0:1, target] = piece
-
-    read_image(view, lax.div(step, 2), lax.rem(step, 2), seq, xs, 0)
-    hat, _ = normalize(xs[...])
+        load.wait()
+        view[...] = raw[...].astype(F32)
+
+    for slot in range(2):
+        read_image(view, step, slot, seq, xs, slot * ROWS)
+    hat, rstd = normalize(xs[...])
+    hat_ref[...] = hat.astype(BF16).reshape(2, ROWS, width)
+    rstd_ref[...] = jnp.broadcast_to(rstd, (2 * ROWS, 128)).reshape(2, ROWS, 128)
     normed = (hat * vec_ref[0:1, :] + vec_ref[1:2, :]).astype(BF16)
     low_half = lax.broadcasted_iota(jnp.int32, (1, 128), 1) < 64
     column = lax.broadcasted_iota(jnp.int32, (1, KEYS), 1)
@@ -193,49 +231,54 @@
     def project(pair):
         lanes = slice(pair * 384, pair * 384 + 384)
         qkv = (mm(normed, whole_ref[:, lanes]) + bias[0:1, lanes]).astype(BF16)
-        qkv_ref[0, :, lanes] = qkv
-        kv[:ROWS, pair * 256 : pair * 256 + 256] = qkv[:, 128:]
+        for slot in range(2):
+            part = qkv[slot * ROWS : slot * ROWS + ROWS]
+            qkv_ref[slot, :, lanes] = part
+            kv[slot, :ROWS, pair * 256 : pair * 256 + 256] = part[:, 128:]
 
     def masked(values, head):
         mask = low_half if head % 2 == 0 else jnp.logical_not(low_half)
         return jnp.where(mask, values, jnp.zeros_like(values))
 
-    def first_part(head):
+    def first_part(slot, head):
         pair = head // 2
-        query = qkv_ref[0, :, pair * 384 : pair * 384 + 128] * jnp.array(0.125, BF16)
-        scores[head % 2] = mm_nt(query, masked(kv[:, pair * 256 : pair * 256 + 128], head))
-
-    def second_part(head):
+        query = qkv_ref[slot, :, pair * 384 : pair * 384 + 128] * jnp.array(0.125, BF16)
+        scores[slot, head % 2] = mm_nt(query, masked(kv[slot, :, pair * 256 : pair * 256 + 128], head))
+
+    def second_part(slot, head):
         for r in range(0, ROWS, 16):
-            value = jnp.where(column < seq, scores[head % 2, r : r + 16], -1e30)
+            value = jnp.where(column < seq, scores[slot, head % 2, r : r + 16], -1e30)
             top = jnp.max(value, axis=-1, keepdims=True)
             grown = jnp.exp(value - top)
-            prob_ref[0, head, r : r + 16] = (grown * (1.0 / jnp.sum(grown, axis=-1, keepdims=True))).astype(BF16)
-
-    def third_part(head):
+            prob_ref[slot, head, r : r + 16] = (
+                grown * (1.0 / jnp.sum(grown, axis=-1, keepdims=True))
+            ).astype(BF16)
+
+    def third_part(slot, head):
         pair = head // 2
-        values = kv[:, pair * 256 + 128 : pair * 256 + 256]
+        values = kv[slot, :, pair * 256 + 128 : pair * 256 + 256]
         if head % 2 == 1:
-            total = mm(prob_ref[0, head - 1], masked(values, 0)) + mm(prob_ref[0, head], masked(values, 1))
-            att_ref[0, :, pair * 128 : pair * 128 + 128] = total.astype(BF16)
+            total = mm(prob_ref[slot, head - 1], masked(values, 0)) + mm(prob_ref[slot, head], masked(values, 1))
+            att_ref[slot, :, pair * 128 : pair * 128 + 128] = total.astype(BF16)
 
     project(0)
     for k in range(HEADS + 2):
-        if k < HEADS:
-            first_part(k)
-        if k % 2 == 0 and k // 2 + 1 < pairs:
-            project(k // 2 + 1)
-        if k >= 2:
-            third_part(k - 2)
-        if 1 <= k <= HEADS:
-            second_part(k - 1)
+        for slot in range(2):
+            if k < HEADS:
+                first_part(slot, k)
+            if k >= 2:
+                third_part(slot, k - 2)
+            if slot == 0 and k % 2 == 0 and k // 2 + 1 < pairs:
+                project(k // 2 + 1)
+            if 1 <= k <= HEADS:
+                second_part(slot, k - 1)
 
 
 def mlp_kernel(
-    idx_ref, count_ref, x_ref, cot_ref, att_ref, wo_ref, w1_ref, w2_ref, near_ref, far_ref, small_ref, first_ref,
-    out_ref, dx_ref, datt_ref, keep_ref, send_ref,
-    view_x, view_c, xs, dys, acts, dpres, pres, dacts, wo, w1, w2, wot, w1t, w2t, vec, b1, out_half, dn_half,
-    gw1, gw2, gwo, gsmall,
+    idx_ref, count_ref, x_ref, cot_ref, att_hbm, wo_ref, w1_ref, w2_ref, near_ref, far_ref, vec, b1,
+    act_ref, middle_ref, dx_ref, datt_ref, w2, keep_ref, send_ref,
+    view_x, view_c, xs, dys, acts, dpres, pres, dacts, wo, w1, wot, w1t, w2t, dn_half,
+    gw1, gw2, gwo, gsmall, att_buf, raw, att_sem, raw_sem,
 ):
     step = pl.program_id(0)
     last = pl.num_programs(0) - 1
@@ -248,8 +291,9 @@
 
     @pl.when(step == 0)
     def _():
-        view_x[...] = x_ref[...].astype(F32)
-        view_c[...] = cot_ref[...].astype(F32)
+        loads = [pltpu.make_async_copy(ref, raw.at[k], raw_sem.at[k]) for k, ref in enumerate((x_ref, cot_ref))]
+        for load in loads:
+            load.start()
         for ref in (xs, dys, gw1, gw2, gwo, gsmall):
             ref[...] = jnp.zeros_like(ref)
         group = idx_ref[0]
@@ -266,14 +310,11 @@
         wot[...] = wo[...].T
         w1t[...] = w1[...].T
         w2t[...] = w2[...].T
-        first, second = ordered(idx_ref, small_ref[...], first_ref[part : part + 8, : small_ref.shape[1]])
-        vec[0:1, :] = joined(first, second, 1, half)
-        vec[1:2, :] = joined(first, second, 3, half)
-        vec[2:3, :] = joined(first, second, 6, half)
-        vec[3:4, :] = joined(first, second, 7, half)
-        b1[0:1, : hidden // 2] = first[2:3, :]
-        b1[0:1, hidden // 2 :] = second[2:3, :]
-
+        for load, target, k in zip(loads, (view_x, view_c), range(2)):
+            load.wait()
+            target[...] = raw[k].astype(F32)
+
+    (att_ref,) = fetch([(att_hbm, att_buf)], att_sem, 0, step, last + 1)
     second_valid = (1 < count_ref[step, 0]).astype(F32)
     for slot in range(2):
         read_image(view_x, step, slot, seq, xs, slot * ROWS)
@@ -281,10 +322,10 @@
     row = lax.broadcasted_iota(jnp.int32, (rows, 1), 0)
     valid = jnp.where(row < ROWS, 1.0, second_valid)
     att = att_ref[...].reshape(rows, width)
-    middle = xs[...] + mm(att, wo[...]) + vec[0:1, :]
+    middle = xs[...] + mm(att, wo[...]) + vec[2:3, :]
     hat, rstd = normalize(middle)
-    gain = vec[2:3, :]
-    normed = (hat * gain + vec[3:4, :]).astype(BF16)
+    gain = vec[4:5, :]
+    normed = (hat * gain + vec[5:6, :]).astype(BF16)
     d_out = dys[...] * valid
     d_mlp = d_out.astype(BF16)
     normed_t = jnp.concatenate([normed.T, jnp.ones((16, rows), BF16)], axis=0)
@@ -303,6 +344,8 @@
         for r in range(0, rows, 32):
             act, d_pre = gelu_parts(pres[c % 2, r : r + 32] + bias, dacts[c % 2, r : r + 32])
             acts[r : r + 32, cols] = act
+            act_ref[r // ROWS, r % ROWS : r % ROWS + 16, cols] = act[:16]
+            act_ref[(r + 16) // ROWS, (r + 16) % ROWS : (r + 16) % ROWS + 16, cols] = act[16:]
             dpres[r : r + 32, cols] = d_pre
 
     def third_part(c):
@@ -316,18 +359,15 @@
         if k >= 2:
             third_part(k - 2)
         if k == chunks // 2 + 1:
-            out_half[...] = mm(acts[:, :middle_of], w2[:middle_of, :])
             dn_half[...] = mm(dpres[:, :middle_of], w1t[:middle_of, :])
         if 1 <= k <= chunks:
             second_part(k - 1)
 
-    result = (middle + out_half[...] + mm(acts[:, middle_of:], w2[middle_of:, :]) + vec[1:2, :]) * valid
-    for slot in range(2):
-        write_image(view_x, step, slot, seq, result[slot * ROWS : slot * ROWS + ROWS])
+    middle_ref[...] = middle.reshape(2, ROWS, width)
     d_normed = dn_half[...] + mm(dpres[:, middle_of:], w1t[middle_of:, :])
     dx = d_out + norm_back(d_normed, hat, rstd, gain)
-    dx_ref[...] = dx.reshape(2, ROWS, width)
     d_attn = dx.astype(BF16)
+    dx_ref[...] = d_attn.reshape(2, ROWS, width)
     datt_ref[...] = mm(d_attn, wot[...]).astype(BF16).reshape(2, ROWS, width)
     gwo[...] += mm_tn(att, d_attn)
 
@@ -341,7 +381,6 @@
 
     @pl.when(step == last)
     def _():
-        out_ref[...] = view_x[...].astype(BF16)
         quarter = half // 4
         wide = hidden // 8
         gw2_t = gw2[...].T
@@ -385,30 +424,30 @@
 
 
 def attention_back_kernel(
-    first_image, last, idx_ref, x_ref, qkv_ref, prob_ref, att_ref, datt_ref, w_ref, vec_ref, *refs
+    first_micro, last, idx_ref, hat_hbm, qkv_hbm, prob_hbm, att_hbm, datt_hbm, w_ref, vec_ref, *refs
 ):
-    carried = 0 if first_image == 0 else 3
+    carried = 0 if first_micro == 0 else 3
     dqkv_ref, total_ref, sums_ref = refs[carried : carried + 3]
-    view, xs, kv, hat_t, d_probs, d_scores = refs[-6:]
+    kv, hat_t, d_probs, d_scores = refs[-10:-6]
+    buffers, sem = refs[-6:-1], refs[-1]
     step = pl.program_id(0)
     width = w_ref.shape[0]
-    seq = x_ref.shape[0] * 128 // (width * qkv_ref.shape[0] * 8)
-    image = first_image + step
     pairs = width // 128
+    sources = (hat_hbm, datt_hbm, qkv_hbm, att_hbm, prob_hbm)
+    hat_ref, datt_ref, qkv_ref, att_ref, prob_ref = fetch(
+        list(zip(sources, buffers)), sem, first_micro, step, pl.num_programs(0)
+    )
 
     @pl.when(step == 0)
     def _():
-        view[...] = x_ref[...].astype(F32)
-        xs[...] = jnp.zeros_like(xs)
         kv[...] = jnp.zeros_like(kv)
-        total_ref[...] = refs[1][...] if carried else jnp.zeros_like(total_ref)
-        sums_ref[...] = refs[2][...] if carried else jnp.zeros_like(sums_ref)
-
-    read_image(view, lax.div(image, 2), lax.rem(image, 2), seq, xs, 0)
-    hat, _ = normalize(xs[...])
-    hat_t[...] = hat.astype(BF16).T
+        if not carried:
+            total_ref[...] = jnp.zeros_like(total_ref)
+            sums_ref[...] = jnp.zeros_like(sums_ref)
+
+    hat_t[...] = hat_ref[...].reshape(2 * ROWS, width).T
     for pair in range(pairs):
-        kv[:ROWS, pair * 256 : pair * 256 + 256] = qkv_ref[0, :, pair * 384 + 128 : pair * 384 + 384]
+        kv[:, :ROWS, pair * 256 : pair * 256 + 256] = qkv_ref[:, :, pair * 384 + 128 : pair * 384 + 384]
     low_half = lax.broadcasted_iota(jnp.int32, (1, 128), 1) < 64
 
     def masked(values, head):
@@ -418,51 +457,52 @@
     def lanes(head):
         return slice(head // 2 * 128, head // 2 * 128 + 128)
 
-    def first_part(head):
+    def first_part(slot, head):
         pair = head // 2
-        d_probs[head % 2] = mm_nt(
-            datt_ref[0, :, lanes(head)], masked(kv[:, pair * 256 + 128 : pair * 256 + 256], head)
+        d_probs[slot, head % 2] = mm_nt(
+            datt_ref[slot, :, lanes(head)], masked(kv[slot, :, pair * 256 + 128 : pair * 256 + 256], head)
         )
 
-    def second_part(head):
+    def second_part(slot, head):
         for r in range(0, ROWS, 16):
             rows = slice(r, r + 16)
-            product = datt_ref[0, rows, lanes(head)].astype(F32) * att_ref[0, rows, lanes(head)].astype(F32)
+            product = datt_ref[slot, rows, lanes(head)].astype(F32) * att_ref[slot, rows, lanes(head)].astype(F32)
             delta = jnp.sum(masked(product, head), axis=-1, keepdims=True)
-            d_scores[head % 4, rows] = (
-                prob_ref[0, head, rows].astype(F32) * (d_probs[head % 2, rows] - delta)
+            d_scores[slot, head % 4, rows] = (
+                prob_ref[slot, head, rows].astype(F32) * (d_probs[slot, head % 2, rows] - delta)
             ).astype(BF16)
 
-    def third_part(pair):
-        query = qkv_ref[0, :, pair * 384 : pair * 384 + 128] * jnp.array(0.125, BF16)
-        keys = kv[:, pair * 256 : pair * 256 + 128] * jnp.array(0.125, BF16)
-        d_att = datt_ref[0, :, pair * 128 : pair * 128 + 128]
+    def third_part(slot, pair):
+        query = qkv_ref[slot, :, pair * 384 : pair * 384 + 128] * jnp.array(0.125, BF16)
+        keys = kv[slot, :, pair * 256 : pair * 256 + 128] * jnp.array(0.125, BF16)
+        d_att = datt_ref[slot, :, pair * 128 : pair * 128 + 128]
         dq = dk = dv = 0.0
         for head in (2 * pair, 2 * pair + 1):
-            d_score = d_scores[head % 4]
-            dv = dv + mm_tn(prob_ref[0, head], masked(d_att, head))
+            d_score = d_scores[slot, head % 4]
+            dv = dv + mm_tn(prob_ref[slot, head], masked(d_att, head))
             dk = dk + mm_tn(d_score, masked(query, head))
             dq = dq + mm(d_score, masked(keys, head))
         top = pair * 384
-        dqkv_ref[0, :, top : top + 128] = dq.astype(BF16)
-        dqkv_ref[0, :, top + 128 : top + 256] = dk[:ROWS].astype(BF16)
-        dqkv_ref[0, :, top + 256 : top + 384] = dv[:ROWS].astype(BF16)
+        dqkv_ref[slot, :, top : top + 128] = dq.astype(BF16)
+        dqkv_ref[slot, :, top + 128 : top + 256] = dk[:ROWS].astype(BF16)
+        dqkv_ref[slot, :, top + 256 : top + 384] = dv[:ROWS].astype(BF16)
 
     def fourth_part(pair):
         columns = slice(pair * 384, pair * 384 + 384)
-        joined_back = dqkv_ref[0, :, columns]
+        joined_back = dqkv_ref[:, :, columns].reshape(2 * ROWS, 384)
         total_ref[:, columns] += mm(hat_t[...], joined_back)
-        sums_ref[:, columns] += jnp.sum(joined_back.astype(F32).reshape(ROWS // 8, 8, 384), axis=0)
+        sums_ref[:, columns] += jnp.sum(joined_back.astype(F32).reshape(ROWS // 4, 8, 384), axis=0)
 
     for k in range(HEADS + 3):
-        if k < HEADS:
-            first_part(k)
-        if k >= 3 and k % 2 == 1:
-            third_part(k // 2 - 1)
-        if k >= 4 and k % 2 == 0:
-            fourth_part(k // 2 - 2)
-        if 1 <= k <= HEADS:
-            second_part(k - 1)
+        for slot in range(2):
+            if k < HEADS:
+                first_part(slot, k)
+            if k >= 3 and k % 2 == 1:
+                third_part(slot, k // 2 - 1)
+            if slot == 0 and k >= 4 and k % 2 == 0:
+                fourth_part(k // 2 - 2)
+            if 1 <= k <= HEADS:
+                second_part(slot, k - 1)
 
     if last:
         keep_ref, send_ref = refs[carried + 3 : carried + 5]
@@ -502,37 +542,52 @@
             split_quads(idx_ref[1], emit, keep_ref, send_ref)
 
 
-def input_grad_kernel(x_ref, dqkv_ref, dx_ref, w_ref, vec_ref, din_ref, view, outs, xs, wt):
+def input_grad_kernel(hat_hbm, rstd_hbm, dqkv_hbm, dx_hbm, w_ref, vec_ref, din_ref, outs, wt, *refs):
     step = pl.program_id(0)
     width = w_ref.shape[0]
-    seq = x_ref.shape[0] * 128 // (width * 2 * pl.num_programs(0))
-    rows = xs.shape[0]
+    micros = pl.num_programs(0)
+    seq = din_ref.shape[0] * 128 // (width * 2 * micros)
+    rows = 2 * ROWS
+    sources = (hat_hbm, rstd_hbm, dqkv_hbm, dx_hbm)
+    hat_ref, rstd_ref, dqkv_ref, dx_ref = fetch(list(zip(sources, refs[:-1])), refs[-1], 0, step, micros)
 
     @pl.when(step == 0)
     def _():
-        view[...] = x_ref[...].astype(F32)
         wt[...] = w_ref[...].T
-        xs[...] = jnp.zeros_like(xs)
-
-    for slot in range(2):
-        read_image(view, step, slot, seq, xs, slot * ROWS)
+
     d_normed = mm(dqkv_ref[...].reshape(rows, 3 * width), wt[...])
-    hat, rstd = normalize(xs[...])
-    d_in = dx_ref[...].reshape(rows, width) + norm_back(d_normed, hat, rstd, vec_ref[0:1, :])
+    hat = hat_ref[...].reshape(rows, width).astype(F32)
+    rstd = rstd_ref[...].reshape(rows, 128)[:, 0:1]
+    d_in = dx_ref[...].reshape(rows, width).astype(F32) + norm_back(d_normed, hat, rstd, vec_ref[0:1, :])
     for slot in range(2):
         write_image(outs, step, slot, seq, d_in[slot * ROWS : slot * ROWS + ROWS])
 
-    @pl.when(step == pl.num_programs(0) - 1)
+    @pl.when(step == micros - 1)
     def _():
         din_ref[...] = outs[...].astype(BF16)
 
 
-def fixed(*shape):
-    return pl.BlockSpec(shape, lambda i: (0,) * len(shape))
-
-
-def per_image(*shape):
-    return pl.BlockSpec((1, *shape), lambda i: (i,) + (0,) * len(shape))
+def outputs_kernel(count_ref, act_hbm, middle_hbm, w2_ref, vec_ref, out_ref, outs, act_buf, middle_buf, sem):
+    step = pl.program_id(0)
+    hidden, width = w2_ref.shape
+    micros = pl.num_programs(0)
+    seq = out_ref.shape[0] * 128 // (width * 2 * micros)
+    rows = 2 * ROWS
+    act_ref, middle_ref = fetch([(act_hbm, act_buf), (middle_hbm, middle_buf)], sem, 0, step, micros)
+    row = lax.broadcasted_iota(jnp.int32, (rows, 1), 0)
+    valid = jnp.where(row < ROWS, 1.0, (1 < count_ref[step, 0]).astype(F32))
+    mlp = mm(act_ref[...].reshape(rows, hidden), w2_ref[...]) + vec_ref[3:4, :]
+    result = (middle_ref[...].reshape(rows, width) + mlp) * valid
+    for slot in range(2):
+        write_image(outs, step, slot, seq, result[slot * ROWS : slot * ROWS + ROWS])
+
+    @pl.when(step == micros - 1)
+    def _():
+        out_ref[...] = outs[...].astype(BF16)
+
+
+def per_pair(*shape):
+    return pl.BlockSpec((2, *shape), lambda i: (i,) + (0,) * len(shape))
 
 
 SMEM_SPEC = pl.BlockSpec(memory_space=pltpu.SMEM)
@@ -542,33 +597,38 @@
     width = w_qkv.shape[1] // 3
     return pl.pallas_call(
         attention_kernel,
-        grid=(count,),
-        in_specs=[SMEM_SPEC] + [VMEM_SPEC] * 5,
+        grid=(count // 2,),
+        in_specs=[SMEM_SPEC, HBM_SPEC] + [VMEM_SPEC] * 4,
         out_specs=[
-            per_image(ROWS, 3 * width), per_image(HEADS, ROWS, KEYS), per_image(ROWS, width),
-            fixed(width, 3 * width), fixed(8, width),
+            per_pair(ROWS, 3 * width), per_pair(HEADS, ROWS, KEYS), per_pair(ROWS, width),
+            per_pair(ROWS, width), per_pair(ROWS, 128), VMEM_SPEC, VMEM_SPEC, VMEM_SPEC,
         ],
         out_shape=[
             pltpu.HBM((count, ROWS, 3 * width), BF16),
             pltpu.HBM((count, HEADS, ROWS, KEYS), BF16),
             pltpu.HBM((count, ROWS, width), BF16),
+            pltpu.HBM((count, ROWS, width), BF16),
+            pltpu.HBM((count, ROWS, 128), F32),
             jax.ShapeDtypeStruct((width, 3 * width), BF16),
             jax.ShapeDtypeStruct((8, width), F32),
+            jax.ShapeDtypeStruct((8, 2 * small.shape[1]), F32),
         ],
         scratch_shapes=[
+            pltpu.VMEM(view.shape, BF16),
             pltpu.VMEM(view.shape, F32),
-            pltpu.VMEM((ROWS, width), F32),
-            pltpu.VMEM((KEYS, 2 * width), BF16),
+            pltpu.VMEM((2 * ROWS, width), F32),
+            pltpu.VMEM((2, KEYS, 2 * width), BF16),
             pltpu.VMEM((8, 3 * width), F32),
-            pltpu.VMEM((2, ROWS, KEYS), F32),
+            pltpu.VMEM((2, 2, ROWS, KEYS), F32),
+            pltpu.SemaphoreType.DMA,
         ],
-        compiler_params=pltpu.CompilerParams(vmem_limit_bytes=59 << 20),
+        compiler_params=pltpu.CompilerParams(vmem_limit_bytes=22 << 20),
         cost_estimate=pl.CostEstimate(flops=5 << 30, bytes_accessed=20 << 20, transcendentals=0),
         name="attention_fwd",
-    )(idx, view, w_qkv, near, far, small)
-
-
-def run_mlp(idx, counts, view, cot, att, wo, w1, w2, near, far, small, first):
+    )(idx, *in_hbm(view), w_qkv, near, far, small)
+
+
+def run_mlp(idx, counts, view, cot, att, wo, w1, w2, near, far, vec, b1):
     width = wo.shape[1]
     hidden = w1.shape[1]
     micro = counts.shape[0]
@@ -578,12 +638,14 @@
     return pl.pallas_call(
         mlp_kernel,
         grid=(micro,),
-        in_specs=[SMEM_SPEC, SMEM_SPEC, VMEM_SPEC, VMEM_SPEC, two] + [VMEM_SPEC] * 7,
-        out_specs=[VMEM_SPEC, two, two, VMEM_SPEC, VMEM_SPEC],
+        in_specs=[SMEM_SPEC, SMEM_SPEC, HBM_SPEC, HBM_SPEC, HBM_SPEC] + [VMEM_SPEC] * 7,
+        out_specs=[per_pair(ROWS, hidden), two, two, two, VMEM_SPEC, VMEM_SPEC, VMEM_SPEC],
         out_shape=[
-            jax.ShapeDtypeStruct(view.shape, BF16),
+            pltpu.HBM((2 * micro, ROWS, hidden), BF16),
             pltpu.HBM(att.shape, F32),
             pltpu.HBM(att.shape, BF16),
+            pltpu.HBM(att.shape, BF16),
+            jax.ShapeDtypeStruct((hidden, width), BF16),
             jax.ShapeDtypeStruct((2, 2, packed, width), BF16),
             jax.ShapeDtypeStruct((2, 2, packed, width), BF16),
         ],
@@ -598,41 +660,38 @@
             pltpu.VMEM((2, rows, 256), F32),
             pltpu.VMEM((width, width), BF16),
             pltpu.VMEM((width, hidden), BF16),
-            pltpu.VMEM((hidden, width), BF16),
             pltpu.VMEM((width, width), BF16),
             pltpu.VMEM((hidden, width), BF16),
             pltpu.VMEM((width, hidden), BF16),
-            pltpu.VMEM((8, width), F32),
-            pltpu.VMEM((8, hidden), F32),
-            pltpu.VMEM((rows, width), F32),
             pltpu.VMEM((rows, width), F32),
             pltpu.VMEM((width + 16, hidden), F32),
             pltpu.VMEM((width, hidden), F32),
             pltpu.VMEM((width, width), F32),
             pltpu.VMEM((4, 8, width), F32),
+            pltpu.VMEM((2, 2, ROWS, width), BF16),
+            pltpu.VMEM((2, *view.shape), BF16),
+            pltpu.SemaphoreType.DMA((1, 2)),
+            pltpu.SemaphoreType.DMA((2,)),
         ],
-        compiler_params=pltpu.CompilerParams(vmem_limit_bytes=51 << 20),
+        compiler_params=pltpu.CompilerParams(vmem_limit_bytes=40 << 20),
         cost_estimate=pl.CostEstimate(flops=12 << 30, bytes_accessed=20 << 20, transcendentals=0),
         name="mlp_fwd_bwd",
-    )(idx, counts, view, cot, att, wo, w1, w2, near, far, small, first)
-
-
-def run_attention_back(begin, end, idx, view, qkv, prob, att, datt, w_qkv, vec, carried):
+    )(idx, counts, *in_hbm(view, cot, att), wo, w1, w2, near, far, vec, b1)
+
+
+def run_attention_back(begin, end, idx, hat, qkv, prob, att, datt, w_qkv, vec, carried):
     count = qkv.shape[0]
     width = w_qkv.shape[0]
     packed = width // 8 * 3 + 16
-    last = end == count
-    block = lambda *shape: pl.BlockSpec((1, *shape), lambda i: (i + begin,) + (0,) * len(shape))
-    any_spec = pl.BlockSpec(memory_space=pl.ANY)
+    last = 2 * end == count
+    block = pl.BlockSpec((2, ROWS, 3 * width), lambda i: (i + begin, 0, 0))
+    two = lambda *shape: pltpu.VMEM((2, 2, *shape), BF16)
     return pl.pallas_call(
         partial(attention_back_kernel, begin, last),
         grid=(end - begin,),
-        in_specs=[
-            SMEM_SPEC, VMEM_SPEC, block(ROWS, 3 * width), block(HEADS, ROWS, KEYS),
-            block(ROWS, width), block(ROWS, width), VMEM_SPEC, VMEM_SPEC,
-        ]
-        + ([any_spec, VMEM_SPEC, VMEM_SPEC] if carried else []),
-        out_specs=[block(ROWS, 3 * width), VMEM_SPEC, VMEM_SPEC] + ([VMEM_SPEC] * 2 if last else []),
+        in_specs=[SMEM_SPEC] + [HBM_SPEC] * 5 + [VMEM_SPEC] * 2
+        + ([HBM_SPEC, VMEM_SPEC, VMEM_SPEC] if carried else []),
+        out_specs=[block, VMEM_SPEC, VMEM_SPEC] + ([VMEM_SPEC] * 2 if last else []),
         out_shape=[
             pltpu.HBM((count, ROWS, 3 * width), BF16),
             jax.ShapeDtypeStruct((width, 3 * width), F32),
@@ -640,39 +699,59 @@
         ]
         + [jax.ShapeDtypeStruct((2, 2, packed, width), BF16)] * (2 if last else 0),
         scratch_shapes=[
-            pltpu.VMEM(view.shape, F32),
-            pltpu.VMEM((ROWS, width), F32),
-            pltpu.VMEM((KEYS, 2 * width), BF16),
-            pltpu.VMEM((width, ROWS), BF16),
-            pltpu.VMEM((2, ROWS, KEYS), F32),
-            pltpu.VMEM((4, ROWS, KEYS), BF16),
+            pltpu.VMEM((2, KEYS, 2 * width), BF16),
+            pltpu.VMEM((width, 2 * ROWS), BF16),
+            pltpu.VMEM((2, 2, ROWS, KEYS), F32),
+            pltpu.VMEM((2, 4, ROWS, KEYS), BF16),
+            two(ROWS, width), two(ROWS, width), two(ROWS, 3 * width), two(ROWS, width), two(HEADS, ROWS, KEYS),
+            pltpu.SemaphoreType.DMA((5, 2)),
         ],
-        input_output_aliases={8: 0} if carried else {},
-        compiler_params=pltpu.CompilerParams(vmem_limit_bytes=54 << 20),
-        cost_estimate=pl.CostEstimate(flops=(end - begin) << 30, bytes_accessed=20 << 20, transcendentals=0),
-    )(idx, view, qkv, prob, att, datt, w_qkv, vec, *carried)
-
-
-def run_input_grad(view, dqkv, dx, w_qkv, vec):
+        input_output_aliases={8: 0, 9: 1, 10: 2} if carried else {},
+        compiler_params=pltpu.CompilerParams(vmem_limit_bytes=18 << 20),
+        cost_estimate=pl.CostEstimate(flops=(end - begin) << 31, bytes_accessed=20 << 20, transcendentals=0),
+    )(idx, *in_hbm(hat, qkv, prob, att, datt), w_qkv, vec, *in_hbm(*carried[:1]), *carried[1:])
+
+
+def run_input_grad(view_shape, hat, rstd, dqkv, dx, w_qkv, vec):
     count = dqkv.shape[0]
     width = w_qkv.shape[0]
-    two = lambda *shape: pl.BlockSpec((2, *shape), lambda i: (i,) + (0,) * len(shape))
+    two = lambda dtype, *shape: pltpu.VMEM((2, 2, *shape), dtype)
     return pl.pallas_call(
         input_grad_kernel,
         grid=(count // 2,),
-        in_specs=[VMEM_SPEC, two(ROWS, 3 * width), two(ROWS, width), VMEM_SPEC, VMEM_SPEC],
+        in_specs=[HBM_SPEC] * 4 + [VMEM_SPEC] * 2,
         out_specs=VMEM_SPEC,
-        out_shape=jax.ShapeDtypeStruct(view.shape, BF16),
+        out_shape=jax.ShapeDtypeStruct(view_shape, BF16),
         scratch_shapes=[
-            pltpu.VMEM(view.shape, F32),
-            pltpu.VMEM(view.shape, F32),
-            pltpu.VMEM((2 * ROWS, width), F32),
+            pltpu.VMEM(view_shape, F32),
             pltpu.VMEM((3 * width, width), BF16),
+            two(BF16, ROWS, width), two(F32, ROWS, 128), two(BF16, ROWS, 3 * width), two(BF16, ROWS, width),
+            pltpu.SemaphoreType.DMA((4, 2)),
         ],
-        compiler_params=pltpu.CompilerParams(vmem_limit_bytes=57 << 20),
+        compiler_params=pltpu.CompilerParams(vmem_limit_bytes=14 << 20),
         cost_estimate=pl.CostEstimate(flops=2 << 30, bytes_accessed=20 << 20, transcendentals=0),
         name="input_grad",
-    )(view, dqkv, dx, w_qkv, vec)
+    )(*in_hbm(hat, rstd, dqkv, dx), w_qkv, vec)
+
+
+def run_outputs(view_shape, counts, act, middle, w2, vec):
+    count, _, hidden = act.shape
+    width = w2.shape[1]
+    return pl.pallas_call(
+        outputs_kernel,
+        grid=(count // 2,),
+        in_specs=[SMEM_SPEC] + [HBM_SPEC] * 2 + [VMEM_SPEC] * 2,
+        out_specs=VMEM_SPEC,
+        out_shape=jax.ShapeDtypeStruct(view_shape, BF16),
+        scratch_shapes=[
+            pltpu.VMEM(view_shape, F32),
+            pltpu.VMEM((2, 2, ROWS, hidden), BF16), pltpu.VMEM((2, 2, ROWS, width), F32),
+            pltpu.SemaphoreType.DMA((2, 2)),
+        ],
+        compiler_params=pltpu.CompilerParams(vmem_limit_bytes=14 << 20),
+        cost_estimate=pl.CostEstimate(flops=2 << 30, bytes_accessed=20 << 20, transcendentals=0),
+        name="layer_outputs",
+    )(counts, *in_hbm(act, middle), w2, vec)
 
 
 def merge_kernel(which, idx_ref, a_ref, b_ref, own_ref, other_ref):
@@ -682,14 +761,12 @@
 
 
 def merge(idx, which, a, b):
-    half = jax.ShapeDtypeStruct(a.shape[1:], BF16)
-    vmem = pl.BlockSpec(memory_space=pltpu.VMEM)
     return pl.pallas_call(
         partial(merge_kernel, which),
-        in_specs=[SMEM_SPEC, vmem, vmem],
-        out_specs=[vmem, vmem],
-        out_shape=[half, half],
-        name="merge",
+        in_specs=[SMEM_SPEC, VMEM_SPEC, VMEM_SPEC],
+        out_specs=[VMEM_SPEC, VMEM_SPEC],
+        out_shape=[jax.ShapeDtypeStruct(a.shape[1:], BF16)] * 2,
+        compiler_params=pltpu.CompilerParams(vmem_limit_bytes=4 << 20),
     )(idx, a, b)
 
 
@@ -698,26 +775,32 @@
 
 
 def reduce_grads(idx, keep, send, replicas):
-    own, other = merge(idx, 0, keep, flip(send, "replica", replicas, 1))
-    own, other = merge(idx, 2, own, flip(other, "group", 2, 1))
-    own = own + flip(other, "replica", replicas, 2)
+    got = flip(send, "replica", replicas, 1)
+    own, other = merge(idx, 0, keep, got)
+    got = flip(other, "group", 2, 1)
+    own, other = merge(idx, 2, own, got)
+    got = flip(other, "replica", replicas, 2)
+    own = own + got
     bit = 4
     while bit < replicas:
-        own = own + flip(own, "replica", replicas, bit)
+        got = flip(own, "replica", replicas, bit)
+        own = own + got
         bit *= 2
     side = flip(own, "replica", replicas, 2)
     far_own = flip(own, "replica", replicas, 1)
     return own, side, far_own, flip(side, "replica", replicas, 1)
 
 
-def unpack_kernel(idx_ref, *refs):
-    ins, outs, (mlp, att) = refs[:8], refs[8:20], refs[20:]
+def places(idx_ref):
     core, side = idx_ref[1], idx_ref[2]
-    places = (2 * core + side, 2 * core + 1 - side, 2 * (1 - core) + side, 2 * (1 - core) + 1 - side)
-    for k, place in enumerate(places):
+    return 2 * core + side, 2 * core + 1 - side, 2 * (1 - core) + side, 2 * (1 - core) + 1 - side
+
+
+def unpack_mlp_kernel(idx_ref, *refs):
+    ins, outs, mlp = refs[:4], refs[4:12], refs[12]
+    for k, place in enumerate(places(idx_ref)):
         mlp[place] = ins[k][...].astype(F32)
-        att[place] = ins[4 + k][...].astype(F32)
-    g_qkv, g_bqv, g_out, g_bout, g_fc1, g_bfc1, g_fc2, g_bfc2, g_gone, g_sone, g_gtwo, g_stwo = outs
+    g_out, g_bout, g_fc1, g_bfc1, g_fc2, g_bfc2, g_gtwo, g_stwo = outs
     half, width = g_out.shape
     hidden = g_fc1.shape[1]
     quarter = half // 4
@@ -734,34 +817,44 @@
         top += quarter
         value = mlp[quad, top : top + 1]
         if quad < 2:
-            g_bfc1[:, quad * width : (quad + 1) * width] = value
+            g_bfc1[quad * width : (quad + 1) * width] = value.reshape(width)
         elif quad == 2:
-            g_bfc2[...] = value[:, :half]
-            g_bout[...] = value[:, half:]
+            g_bfc2[...] = value[:, :half].reshape(half)
+            g_bout[...] = value[:, half:].reshape(half)
         else:
-            g_gtwo[...] = value[:, :half]
-            g_stwo[...] = value[:, half:]
+            g_gtwo[...] = value[:, :half].reshape(half)
+            g_stwo[...] = value[:, half:].reshape(half)
+
+
+def unpack_attention_kernel(idx_ref, *refs):
+    ins, outs, att = refs[:4], refs[4:8], refs[8]
+    for k, place in enumerate(places(idx_ref)):
+        att[place] = ins[k][...].astype(F32)
+    g_qkv, g_bqv, g_gone, g_sone = outs
+    half = g_qkv.shape[0]
+    width = 2 * half
+    quarter = half // 4
+    for quad in range(4):
+        rows = slice(quad * quarter, (quad + 1) * quarter)
         for col in range(3):
             g_qkv[rows, col * width : (col + 1) * width] = att[quad, col * quarter : (col + 1) * quarter]
         value = att[quad, 3 * quarter : 3 * quarter + 1]
         if quad == 0:
-            g_bqv[...] = value
+            g_bqv[...] = value.reshape(width)
         elif quad == 1:
-            g_gone[...] = value[:, :half]
-            g_sone[...] = value[:, half:]
-
-
-def run_unpack(idx, mlp, att, shapes):
-    vmem = pl.BlockSpec(memory_space=pltpu.VMEM)
+            g_gone[...] = value[:, :half].reshape(half)
+            g_sone[...] = value[:, half:].reshape(half)
+
+
+def run_unpack(kernel, idx, parts, shapes):
     return pl.pallas_call(
-        unpack_kernel,
-        in_specs=[SMEM_SPEC] + [vmem] * 8,
-        out_specs=[vmem] * 12,
-        out_shape=[jax.ShapeDtypeStruct(s if len(s) == 2 else (1, *s), F32) for s in shapes],
-        scratch_shapes=[pltpu.VMEM((4, *mlp[0].shape), F32), pltpu.VMEM((4, *att[0].shape), F32)],
-        compiler_params=pltpu.CompilerParams(vmem_limit_bytes=40 << 20),
-        name="unpack",
-    )(idx, *mlp, *att)
+        kernel,
+        in_specs=[SMEM_SPEC] + [VMEM_SPEC] * 4,
+        out_specs=[VMEM_SPEC] * len(shapes),
+        out_shape=[jax.ShapeDtypeStruct(s, F32) for s in shapes],
+        scratch_shapes=[pltpu.VMEM((4, *parts[0].shape), F32)],
+        compiler_params=pltpu.CompilerParams(vmem_limit_bytes=8 << 20),
+    )(idx, *parts)
 
 
 def interleaved(images):
@@ -777,7 +870,7 @@
     return blocks.reshape(micro, seq, slots, width).transpose(0, 2, 1, 3)
 
 
-SPLITS = ((0, 2), (2, 6), (6, 8))
+SPLITS = ((0, 1), (1, 4))
 
 
 def local(
@@ -796,22 +889,31 @@
     far_first = flip(near_first, "replica", replicas, 1)
     far_second = flip(near_second, "replica", replicas, 1)
     view = interleaved(images)
-    qkv, prob, att, w_all, vec = run_attention(count, idx, view, w_qkv, near_first, far_first, small)
-    out, dx, datt, keep_b, send_b = run_mlp(
+    qkv, prob, att, hat, rstd, w_all, vec, b1 = run_attention(count, idx, view, w_qkv, near_first, far_first, small)
+    act, middle, dx, datt, w_two, keep_b, send_b = run_mlp(
         idx, image_count, view, interleaved(cotangent), att, w_out, w_fc1, w_fc2,
-        near_second, far_second, small, near_first,
+        near_second, far_second, vec, b1,
     )
     carried = ()
     for begin, end in SPLITS:
-        carried = run_attention_back(begin, end, idx, view, qkv, prob, att, datt, w_all, vec, carried)
+        carried = run_attention_back(begin, end, idx, hat, qkv, prob, att, datt, w_all, vec, carried)
     dqkv, _, _, keep_c, send_c = carried
-    din = run_input_grad(view, dqkv, dx, w_all, vec)
+    din = run_input_grad(view.shape, hat, rstd, dqkv, dx, w_all, vec)
+    out = run_outputs(view.shape, image_count, act, middle, w_two, vec)
     mlp = reduce_grads(idx, keep_b, send_b, replicas)
     attention = reduce_grads(idx, keep_c, send_c, replicas)
-    shapes = [v.shape for v in (w_qkv, b_qv, w_out, b_out, w_fc1, b_fc1, w_fc2, b_fc2)] + [gain_one.shape] * 4
-    grads = run_unpack(idx, mlp, attention, shapes)
-    grads = [g.reshape(s) for g, s in zip(grads, shapes)]
-    return (separated(out, images.shape), separated(din, images.shape), *grads)
+    shape_of = lambda *arrays: [v.shape for v in arrays]
+    g_out, g_bout, g_fc1, g_bfc1, g_fc2, g_bfc2, g_gtwo, g_stwo = run_unpack(
+        unpack_mlp_kernel, idx, mlp,
+        shape_of(w_out, b_out, w_fc1, b_fc1, w_fc2, b_fc2, gain_two, shift_two),
+    )
+    g_qkv, g_bqv, g_gone, g_sone = run_unpack(
+        unpack_attention_kernel, idx, attention, shape_of(w_qkv, b_qv, gain_one, shift_one)
+    )
+    return (
+        separated(out, images.shape), separated(din, images.shape),
+        g_qkv, g_bqv, g_out, g_bout, g_fc1, g_bfc1, g_fc2, g_bfc2, g_gone, g_sone, g_gtwo, g_stwo,
+    )
 
 
 def step(replicas, *args):

time: 194 us -> 171 us (0.88)
  Pallas kernels: 102 us -> 85.5 us
  starting transfers between devices: 32.6 us -> 22.9 us
  waiting for transfers between devices: 49.6 us -> 59 us
  local copies, waits for them, and re-layouts: 5.15 us -> 0.83 us
  other arithmetic: 3.05 us -> 0.94 us
    pallas_call x3 -> x2, Pallas kernels: 30.2 us -> 19.7 us  [run_attention_back(): pl.pallas_call(partial(attention_back_kernel, begin, last), grid=(end - b...]
    ppermute x20, starting transfers between devices: 32.6 us -> 22.9 us  [flip(): return lax.ppermute(value, axis, [(i, i ^ bit) for i in range(size)])]
    ppermute x20, waiting for transfers between devices: 49.6 us -> 59 us  [flip(): return lax.ppermute(value, axis, [(i, i ^ bit) for i in range(size)])]
    unnamed x31 -> x15, local copies, waits for them, and re-layouts: 5.15 us -> 0.83 us
    pallas_call x1, Pallas kernels: 30.4 us -> 27.2 us  [run_mlp(): pl.pallas_call(mlp_kernel, grid=(micro,), in_specs=[SMEM_SPEC, SMEM_SPEC,...]
    pallas_call x7 -> x9, Pallas kernels: 36.5 us -> 33.4 us  [the longest x1 12.2 us: run_attention(): pl.pallas_call(attention_kernel, grid=(count // 2,), in_specs=[SMEM_SPEC,...]
  transfers between devices with their start and end apart: 20 -> 20, of which waited for: 9 -> 9; matrix products, arithmetic and copies ran while one was open for 1% -> 0% of each run, Pallas kernels for 32% -> 30%
where the time goes in v3:
time: 171 us; the launch traced here: 170 us
  Pallas kernels  85.5 us (50%)
  waiting for transfers between devices  59 us (35%)
  starting transfers between devices  22.9 us (13%)
    ppermute x20, waiting for transfers between devices, flip(): return lax.ppermute(value, axis, [(i, i ^ bit) for i in range(size)])  59 us
    pallas_call x1, Pallas kernels, run_mlp(): pl.pallas_call(mlp_kernel, grid=(micro,), in_specs=[SMEM_SPEC, SMEM_SPEC,...  27.2 us
    ppermute x20, starting transfers between devices, flip(): return lax.ppermute(value, axis, [(i, i ^ bit) for i in range(size)])  22.9 us
    pallas_call x2, Pallas kernels, run_attention_back(): pl.pallas_call(partial(attention_back_kernel, begin, last), grid=(end - b...  19.7 us
    pallas_call x1, Pallas kernels, run_attention(): pl.pallas_call(attention_kernel, grid=(count // 2,), in_specs=[SMEM_SPEC,...  12.2 us
    pallas_call x1, Pallas kernels, run_outputs(): pl.pallas_call(outputs_kernel, grid=(count // 2,), in_specs=[SMEM_SPEC] +...  7.39 us
    pallas_call x1, Pallas kernels, run_input_grad(): pl.pallas_call(input_grad_kernel, grid=(count // 2,), in_specs=[HBM_SPEC]...  7.19 us
    pallas_call x2, Pallas kernels, run_unpack(): pl.pallas_call(kernel, in_specs=[SMEM_SPEC] + [VMEM_SPEC] * 4, out_specs=...  3.96 us
  transfers between devices with their start and end apart: 20, of which 9 were waited for; matrix products, arithmetic and copies ran while one was open for 0% of the time, Pallas kernels for 30%

profile of v3, /device:TPU:1, one launch (start us, length us, event | category | flops | bytes accessed | tf_op | source)
XLA Modules:
  0.0 170.0 jit_solution(16206444130492064010)
XLA Ops:
  1.3 2.8 %pack_second.1 = bf16[96,3456]{1,0:T(8,128)(2,1)} custom-call(s32[3]{0:T(128)} %pad_add_fusion.idx_ref, bf16[192,384]{1,0:T(8,128)(2,1)} %wo_ref.3, bf16[192,1536]{1,0:T(8,128)(2,1)} %w1_ref.3, bf16[768,384]{1,0:T(8,128)(2,1)} %w2_ref.3), custom_call_target="tpu_custom_call" | custom-call | tf_op jit(solution)/shard_map/pack_second/pallas_call | solution.py:172
  4.0 2.0 %collective-permute-start.2 = (bf16[96,3456]{1,0:T(8,128)(2,1)}, bf16[96,3456]{1,0:T(8,128)(2,1)S(1)}, u32[]{:S(2)}, u32[]{:S(2)}) collective-permute-start(bf16[96,3456]{1,0:T(8,128)(2,1)} %pack_second.1), channel_id=1, source_target_pairs={{0,16},{16,0},{1,17},{17,1},{2,18},{18,2},{3,19},{19,3},{4,20},{20... | collective-permute-start | bytes 1990664 | tf_op jit(solution)/shard_map/ppermute | solution.py:774
  6.1 2.4 %pack_first.1 = (bf16[112,1152]{1,0:T(8,128)(2,1)}, bf16[8,768]{1,0:T(8,128)(2,1)}) custom-call(s32[3]{0:T(128)} %pad_add_fusion.idx_ref, bf16[192,1152]{1,0:T(8,128)(2,1)} %w_ref.1, bf16[384]{0:T(512)(128)(2,1)} %refs_0_.1, bf16[192]{0:T(256)(128)(2,1)} %refs_1_.1, bf16[768]{0:T(1024)(128)(2,1)} %refs_2_.1, bf16[192]{0:T(256)(128)(2,1)} %refs_3_.1, ...), custom_call_target="tpu_custom_call" | custom-call | tf_op jit(solution)/shard_map/pack_first/pallas_call | solution.py:154
  8.5 17.9 %collective-permute-done.near_ref = bf16[112,1152]{1,0:T(8,128)(2,1)S(1)} collective-permute-done((bf16[112,1152]{1,0:T(8,128)(2,1)}, bf16[112,1152]{1,0:T(8,128)(2,1)S(1)}, u32[]{:S(2)}, u32[]{:S(2)}) %collective-permute-start) | collective-permute-done | bytes 258080 | tf_op jit(solution)/shard_map/ppermute | solution.py:774
  29.5 12.2 %attention_fwd.1 = (bf16[8,208,1152]{2,1,0:T(8,128)(2,1)}, bf16[8,6,208,256]{3,2,1,0:T(8,128)(2,1)}, bf16[8,208,384]{2,1,0:T(8,128)(2,1)}, bf16[8,208,384]{2,1,0...) custom-call(s32[3]{0:T(128)S(1)} %copy-done.4, ...), custom_call_target="tpu_custom_call" | custom-call | flops 5368709120 | bytes 20971520 | tf_op jit(solution)/shard_map/attention_fwd/pallas_call | solution.py:598
  41.8 27.2 %mlp_fwd_bwd.1 = (bf16[8,208,1536]{2,1,0:T(8,128)(2,1)}, f32[8,208,384]{2,1,0:T(8,128)}, bf16[8,208,384]{2,1,0:T(8,128)(2,1)}, bf16[8,208,384]{2,1,0:T(8,128)(2,...) custom-call(s32[3]{0:T(128)S(1)} %copy-done.4, ...), custom_call_target="tpu_custom_call" | custom-call | flops 12884901888 | bytes 20971520 | tf_op jit(solution)/shard_map/mlp_fwd_bwd/pallas_call | solution.py:638
  69.5 2.8 %collective-permute-done.12.b_ref = bf16[2,2,448,384]{3,2,1,0:T(8,128)(2,1)S(1)} collective-permute-done((bf16[2,2,448,384]{3,2,1,0:T(8,128)(2,1)S(1)}, bf16[2,2,448,384]{3,2,1,0:T(8,128)(2,1)S(1)}, u32[]{:S(2)}, u32[]{:S(2)}) %collective-permute-start.12) | collective-permute-done | bytes 1376288 | tf_op jit(solution)/shard_map/ppermute | solution.py:774
  74.5 6.2 %shard_map.254 = (bf16[8,208,1152]{2,1,0:T(8,128)(2,1)}, f32[384,1152]{1,0:T(8,128)S(1)}, f32[8,1152]{1,0:T(8,128)S(1)}) custom-call(s32[3]{0:T(128)S(1)} %copy-done.4, bf16[8,208,384]{2,1,0:T(8,128)(2,1)} %get-tuple-element.65.hat_hbm, bf16[8,208,1152]{2,1,0:T(8,128)(2,1)} %get-tuple-element.67.qkv_hbm, ...), custom_call_target="tpu_custom_call" | custom-call | flops 2147483648 | bytes 20971520 | tf_op jit(solution)/shard_map/pallas_call | solution.py:689
  80.7 9.0 %collective-permute-done.13.b_ref = bf16[2,448,384]{2,1,0:T(8,128)(2,1)S(1)} collective-permute-done((bf16[2,448,384]{2,1,0:T(8,128)(2,1)S(1)}, bf16[2,448,384]{2,1,0:T(8,128)(2,1)S(1)}, u32[]{:S(2)}, u32[]{:S(2)}) %collective-permute-start.13) | collective-permute-done | bytes 688160 | tf_op jit(solution)/shard_map/ppermute | solution.py:774
  91.9 13.5 %shard_map.255 = (bf16[8,208,1152]{2,1,0:T(8,128)(2,1)}, f32[384,1152]{1,0:T(8,128)S(1)}, f32[8,1152]{1,0:T(8,128)S(1)}, bf16[2,2,160,384]{3,2,1,0:T(8,128)(2,1)S(1)}, bf16[2,2,160,384]{3,2,1,0:T(8,128)(2,1)S(1)}) custom-call(s32[3]{0:T(128)S(1)} %copy-done.4, ...), custom_call_target="tpu_custom_call", output_to_operand_aliasing={{0}: (8, {}), {1}: (9, {}), {2}: (10, {})} | custom-call | flops 6442450944 | bytes 20971520 | tf_op jit(solution)/shard_map/pallas_call | solution.py:689
  105.4 1.6 collective-permute-start.4
  108.5 8.3 %collective-permute-done.15 = bf16[448,384]{1,0:T(8,128)(2,1)S(1)} collective-permute-done((bf16[448,384]{1,0:T(8,128)(2,1)S(1)}, bf16[448,384]{1,0:T(8,128)(2,1)S(1)}, u32[]{:S(2)}, u32[]{:S(2)}) %collective-permute-start.15) | collective-permute-done | bytes 344096 | tf_op jit(solution)/shard_map/ppermute | solution.py:774
  116.8 2.4 %collective-permute-start.16 = (bf16[448,384]{1,0:T(8,128)(2,1)S(1)}, bf16[448,384]{1,0:T(8,128)(2,1)S(1)}, u32[]{:S(2)}, u32[]{:S(2)}) collective-permute-start(bf16[448,384]{1,0:T(8,128)(2,1)S(1)} %add.22), channel_id=1, source_target_pairs={{0,8},{1,9},{2,10},{3,11},{4,12},{5,13},{6,14},{7,15},{8,0},{9,1},... | collective-permute-start | bytes 1032200 | tf_op jit(solution)/shard_map/ppermute | solution.py:774
  121.1 5.2 %collective-permute-done.5.b_ref = bf16[2,160,384]{2,1,0:T(8,128)(2,1)S(1)} collective-permute-done((bf16[2,160,384]{2,1,0:T(8,128)(2,1)S(1)}, bf16[2,160,384]{2,1,0:T(8,128)(2,1)S(1)}, u32[]{:S(2)}, u32[]{:S(2)}) %collective-permute-start.5) | collective-permute-done | bytes 245792 | tf_op jit(solution)/shard_map/ppermute | solution.py:774
  127.2 7.0 %collective-permute-done.16 = bf16[448,384]{1,0:T(8,128)(2,1)S(1)} collective-permute-done((bf16[448,384]{1,0:T(8,128)(2,1)S(1)}, bf16[448,384]{1,0:T(8,128)(2,1)S(1)}, u32[]{:S(2)}, u32[]{:S(2)}) %collective-permute-start.16) | collective-permute-done | bytes 344096 | tf_op jit(solution)/shard_map/ppermute | solution.py:774
  134.5 1.6 collective-permute-start.7
  136.1 2.3 %collective-permute-done.7 = bf16[160,384]{1,0:T(8,128)(2,1)S(1)} collective-permute-done((bf16[160,384]{1,0:T(8,128)(2,1)S(1)}, bf16[160,384]{1,0:T(8,128)(2,1)S(1)}, u32[]{:S(2)}, u32[]{:S(2)}) %collective-permute-start.7) | collective-permute-done | bytes 122912 | tf_op jit(solution)/shard_map/ppermute | solution.py:774
  138.4 3.8 %collective-permute-start.8 = (bf16[160,384]{1,0:T(8,128)(2,1)S(1)}, bf16[160,384]{1,0:T(8,128)(2,1)S(1)}, u32[]{:S(2)}, u32[]{:S(2)}) collective-permute-start(bf16[160,384]{1,0:T(8,128)(2,1)S(1)} %add.19), channel_id=1, source_target_pairs={{0,8},{1,9},{2,10},{3,11},{4,12},{5,13},{6,14},{7,15},{8,0},{9,1},... | collective-permute-start | bytes 368648 | tf_op jit(solution)/shard_map/ppermute | solution.py:774
  142.2 5.5 %collective-permute-done.8 = bf16[160,384]{1,0:T(8,128)(2,1)S(1)} collective-permute-done((bf16[160,384]{1,0:T(8,128)(2,1)S(1)}, bf16[160,384]{1,0:T(8,128)(2,1)S(1)}, u32[]{:S(2)}, u32[]{:S(2)}) %collective-permute-start.8) | collective-permute-done | bytes 122912 | tf_op jit(solution)/shard_map/ppermute | solution.py:774
  149.0 1.7 collective-permute-start.18
  150.7 7.4 %layer_outputs.1 = bf16[4728,128]{1,0:T(8,128)(2,1)} custom-call(s32[4,1]{1,0:T(4,128)S(1)} %copy.33.count_ref, bf16[8,208,1536]{2,1,0:T(8,128)(2,1)} %get-tuple-element.62.act_hbm, f32[8,208,384]{2,1,0:T(8,128)} %get-tuple-element.63.middle_hbm, bf16[1536,384]{1,0:T(8,128)(2,1)S(1)} %get-tuple-element.64.w2_ref, f32[8,384]{1,0:T(8,128)S(1)} %get-tuple-element.60.vec.vec_ref), custom_call_target="tpu_custom_call" | custom-call | flops 2147483648 | bytes 20971520 | tf_op jit(solution)/shard_map/layer_outputs/pallas_call | solution.py:740
  158.8 7.2 %input_grad.1 = bf16[4728,128]{1,0:T(8,128)(2,1)} custom-call(bf16[8,208,384]{2,1,0:T(8,128)(2,1)} %get-tuple-element.65.hat_hbm, f32[8,208,128]{2,1,0:T(8,128)} %get-tuple-element.66.rstd_hbm, bf16[8,208,1152]{2,1,0:T(8,128)(2,1)} %get-tuple-element.74.dqkv_hbm, bf16[8,208,384]{2,1,0:T(8,128)(2,1)} %get-tuple-element.75.dx_hbm, ...), custom_call_target="tpu_custom_call" | custom-call | flops 2147483648 | bytes 20971520 | tf_op jit(solution)/shard_map/input_grad/pallas_call | solution.py:719
  166.0 1.6 shard_map.258
  167.6 2.4 %shard_map.261 = (f32[192,384]{1,0:T(8,128)}, f32[192]{0:T(256)}, f32[192,1536]{1,0:T(8,128)}, f32[768]{0:T(1024)}, f32[768,384]{1,0:T(8,128)}, /*index=5*/f32[192]{0:T(256)}, f32[192]{0:T(256)}, f32[192]{0:T(256)}) custom-call(s32[3]{0:T(128)S(1)} %copy-done.4, bf16[448,384]{1,0:T(8,128)(2,1)S(1)} %add.23.refs_0_, ...), custom_call_target="tpu_custom_call" | custom-call | tf_op jit(solution)/shard_map/pallas_call | solution.py:850
  (52 shorter events, 15.3 us)
Async XLA Ops:
  0.6 28.2 %copy-start.2 = (bf16[192,1152]{1,0:T(8,128)(2,1)S(1)}, bf16[192,1152]{1,0:T(8,128)(2,1)}, u32[]{:S(2)}) copy-start(bf16[192,1152]{1,0:T(8,128)(2,1)} %w_ref.1) | copy-start | bytes 1327108
  0.7 27.0 %copy-start.6 = (s32[4,1]{0,1:T(1,128)S(1)}, s32[4,1]{0,1:T(1,128)}, u32[]{:S(2)}) copy-start(s32[4,1]{0,1:T(1,128)} %param.16) | copy-start | bytes 52
  1.3 27.6 %copy-start.4 = (s32[3]{0:T(128)S(1)}, s32[3]{0:T(128)}, u32[]{:S(2)}) copy-start(s32[3]{0:T(128)} %pad_add_fusion.idx_ref) | copy-start | bytes 40
  4.0 23.6 %collective-permute-start.2 = (bf16[96,3456]{1,0:T(8,128)(2,1)}, bf16[96,3456]{1,0:T(8,128)(2,1)S(1)}, u32[]{:S(2)}, u32[]{:S(2)}) collective-permute-start(bf16[96,3456]{1,0:T(8,128)(2,1)} %pack_second.1), channel_id=1, source_target_pairs={{0,16},{16,0},{1,17},{17,1},{2,18},{18,2},{3,19},{19,3},{4,20},{20... | collective-permute-start | bytes 1990664 | tf_op jit(solution)/shard_map/ppermute | solution.py:774
  8.5 17.9 %collective-permute-start = (bf16[112,1152]{1,0:T(8,128)(2,1)}, bf16[112,1152]{1,0:T(8,128)(2,1)S(1)}, u32[]{:S(2)}, u32[]{:S(2)}) collective-permute-start(bf16[112,1152]{1,0:T(8,128)(2,1)} %get-tuple-element.57), channel_id=1, source_target_pairs={{0,16},{16,0},{1,17},{17,1},{2,18},{18,2},{3,19},{19,3},{4,20},{20... | collective-permute-start | bytes 774152 | tf_op jit(solution)/shard_map/ppermute | solution.py:774
  26.4 2.4 %collective-permute-start.1 = (bf16[112,1152]{1,0:T(8,128)(2,1)S(1)}, bf16[112,1152]{1,0:T(8,128)(2,1)S(1)}, u32[]{:S(2)}, u32[]{:S(2)}) collective-permute-start(bf16[112,1152]{1,0:T(8,128)(2,1)S(1)} %collective-permute-done.near_ref), channel_id=1, source_target_pairs={{0,1},{1,0},{2,3},{3,2},{4,5},{5,4},{6,7},{7,6},{8,9},{9,8},{10,11... | collective-permute-start | bytes 774152 | tf_op jit(solution)/shard_map/ppermute | solution.py:774
  27.7 14.1 %collective-permute-start.3 = (bf16[96,3456]{1,0:T(8,128)(2,1)S(1)}, bf16[96,3456]{1,0:T(8,128)(2,1)S(1)}, u32[]{:S(2)}, u32[]{:S(2)}) collective-permute-start(bf16[96,3456]{1,0:T(8,128)(2,1)S(1)} %collective-permute-done.2.near_ref), channel_id=1, source_target_pairs={{0,1},{1,0},{2,3},{3,2},{4,5},{5,4},{6,7},{7,6},{8,9},{9,8},{10,11... | collective-permute-start | bytes 1990664 | tf_op jit(solution)/shard_map/ppermute | solution.py:774
  29.5 12.3 %copy-start.3 = (bf16[192,384]{1,0:T(8,128)(2,1)S(1)}, bf16[192,384]{1,0:T(8,128)(2,1)}, u32[]{:S(2)}) copy-start(bf16[192,384]{1,0:T(8,128)(2,1)} %wo_ref.3) | copy-start | bytes 442372
  69.1 3.2 %collective-permute-start.12 = (bf16[2,2,448,384]{3,2,1,0:T(8,128)(2,1)S(1)}, bf16[2,2,448,384]{3,2,1,0:T(8,128)(2,1)S(1)}, u32[]{:S(2)}, u32[]{:S(2)}) collective-permute-start(bf16[2,2,448,384]{3,2,1,0:T(8,128)(2,1)S(1)} %get-tuple-element.85), channel_id=1, source_target_pairs={{0,1},{1,0},{2,3},{3,2},{4,5},{5,4},{6,7},{7,6},{8,9},{9,8},{10,11... | collective-permute-start | bytes 4128776 | tf_op jit(solution)/shard_map/ppermute | solution.py:774
  73.0 16.7 %collective-permute-start.13 = (bf16[2,448,384]{2,1,0:T(8,128)(2,1)S(1)}, bf16[2,448,384]{2,1,0:T(8,128)(2,1)S(1)}, u32[]{:S(2)}, u32[]{:S(2)}) collective-permute-start(bf16[2,448,384]{2,1,0:T(8,128)(2,1)S(1)} %get-tuple-element.87), channel_id=1, source_target_pairs={{0,16},{16,0},{1,17},{17,1},{2,18},{18,2},{3,19},{19,3},{4,20},{20... | collective-permute-start | bytes 2064392 | tf_op jit(solution)/shard_map/ppermute | solution.py:774
  90.3 16.7 %collective-permute-start.14 = (bf16[448,384]{1,0:T(8,128)(2,1)S(1)}, bf16[448,384]{1,0:T(8,128)(2,1)S(1)}, u32[]{:S(2)}, u32[]{:S(2)}) collective-permute-start(bf16[448,384]{1,0:T(8,128)(2,1)S(1)} %get-tuple-element.89), channel_id=1, source_target_pairs={{0,2},{1,3},{2,0},{3,1},{4,6},{5,7},{6,4},{7,5},{8,10},{9,11},{10,... | collective-permute-start | bytes 1032200 | tf_op jit(solution)/shard_map/ppermute | solution.py:774
  105.4 13.8 %collective-permute-start.4 = (bf16[2,2,160,384]{3,2,1,0:T(8,128)(2,1)S(1)}, bf16[2,2,160,384]{3,2,1,0:T(8,128)(2,1)S(1)}, u32[]{:S(2)}, u32[]{:S(2)}) collective-permute-start(bf16[2,2,160,384]{3,2,1,0:T(8,128)(2,1)S(1)} %get-tuple-element.77), channel_id=1, source_target_pairs={{0,1},{1,0},{2,3},{3,2},{4,5},{5,4},{6,7},{7,6},{8,9},{9,8},{10,11... | collective-permute-start | bytes 1474568 | tf_op jit(solution)/shard_map/ppermute | solution.py:774
  107.1 9.7 %collective-permute-start.15 = (bf16[448,384]{1,0:T(8,128)(2,1)S(1)}, bf16[448,384]{1,0:T(8,128)(2,1)S(1)}, u32[]{:S(2)}, u32[]{:S(2)}) collective-permute-start(bf16[448,384]{1,0:T(8,128)(2,1)S(1)} %add.21), channel_id=1, source_target_pairs={{0,4},{1,5},{2,6},{3,7},{4,0},{5,1},{6,2},{7,3},{8,12},{9,13},{10,... | collective-permute-start | bytes 1032200 | tf_op jit(solution)/shard_map/ppermute | solution.py:774
  116.8 17.3 %collective-permute-start.16 = (bf16[448,384]{1,0:T(8,128)(2,1)S(1)}, bf16[448,384]{1,0:T(8,128)(2,1)S(1)}, u32[]{:S(2)}, u32[]{:S(2)}) collective-permute-start(bf16[448,384]{1,0:T(8,128)(2,1)S(1)} %add.22), channel_id=1, source_target_pairs={{0,8},{1,9},{2,10},{3,11},{4,12},{5,13},{6,14},{7,15},{8,0},{9,1},... | collective-permute-start | bytes 1032200 | tf_op jit(solution)/shard_map/ppermute | solution.py:774
  119.9 6.4 %collective-permute-start.5 = (bf16[2,160,384]{2,1,0:T(8,128)(2,1)S(1)}, bf16[2,160,384]{2,1,0:T(8,128)(2,1)S(1)}, u32[]{:S(2)}, u32[]{:S(2)}) collective-permute-start(bf16[2,160,384]{2,1,0:T(8,128)(2,1)S(1)} %get-tuple-element.79), channel_id=1, source_target_pairs={{0,16},{16,0},{1,17},{17,1},{2,18},{18,2},{3,19},{19,3},{4,20},{20... | collective-permute-start | bytes 737288 | tf_op jit(solution)/shard_map/ppermute | solution.py:774
  126.9 7.6 %collective-permute-start.6 = (bf16[160,384]{1,0:T(8,128)(2,1)S(1)}, bf16[160,384]{1,0:T(8,128)(2,1)S(1)}, u32[]{:S(2)}, u32[]{:S(2)}) collective-permute-start(bf16[160,384]{1,0:T(8,128)(2,1)S(1)} %get-tuple-element.81), channel_id=1, source_target_pairs={{0,2},{1,3},{2,0},{3,1},{4,6},{5,7},{6,4},{7,5},{8,10},{9,11},{10,... | collective-permute-start | bytes 368648 | tf_op jit(solution)/shard_map/ppermute | solution.py:774
  134.2 16.5 %collective-permute-start.17 = (bf16[448,384]{1,0:T(8,128)(2,1)S(1)}, bf16[448,384]{1,0:T(8,128)(2,1)S(1)}, u32[]{:S(2)}, u32[]{:S(2)}) collective-permute-start(bf16[448,384]{1,0:T(8,128)(2,1)S(1)} %add.23.refs_0_), channel_id=1, source_target_pairs={{0,2},{1,3},{2,0},{3,1},{4,6},{5,7},{6,4},{7,5},{8,10},{9,11},{10,... | collective-permute-start | bytes 1032200 | tf_op jit(solution)/shard_map/ppermute | solution.py:774
  134.5 3.8 %collective-permute-start.7 = (bf16[160,384]{1,0:T(8,128)(2,1)S(1)}, bf16[160,384]{1,0:T(8,128)(2,1)S(1)}, u32[]{:S(2)}, u32[]{:S(2)}) collective-permute-start(bf16[160,384]{1,0:T(8,128)(2,1)S(1)} %add.18), channel_id=1, source_target_pairs={{0,4},{1,5},{2,6},{3,7},{4,0},{5,1},{6,2},{7,3},{8,12},{9,13},{10,... | collective-permute-start | bytes 368648 | tf_op jit(solution)/shard_map/ppermute | solution.py:774
  138.4 9.3 %collective-permute-start.8 = (bf16[160,384]{1,0:T(8,128)(2,1)S(1)}, bf16[160,384]{1,0:T(8,128)(2,1)S(1)}, u32[]{:S(2)}, u32[]{:S(2)}) collective-permute-start(bf16[160,384]{1,0:T(8,128)(2,1)S(1)} %add.19), channel_id=1, source_target_pairs={{0,8},{1,9},{2,10},{3,11},{4,12},{5,13},{6,14},{7,15},{8,0},{9,1},... | collective-permute-start | bytes 368648 | tf_op jit(solution)/shard_map/ppermute | solution.py:774
  147.7 11.0 %collective-permute-start.9 = (bf16[160,384]{1,0:T(8,128)(2,1)S(1)}, bf16[160,384]{1,0:T(8,128)(2,1)S(1)}, u32[]{:S(2)}, u32[]{:S(2)}) collective-permute-start(bf16[160,384]{1,0:T(8,128)(2,1)S(1)} %add.20.refs_0_), channel_id=1, source_target_pairs={{0,2},{1,3},{2,0},{3,1},{4,6},{5,7},{6,4},{7,5},{8,10},{9,11},{10,... | collective-permute-start | bytes 368648 | tf_op jit(solution)/shard_map/ppermute | solution.py:774
  149.0 18.5 %collective-permute-start.18 = (bf16[448,384]{1,0:T(8,128)(2,1)S(1)}, bf16[448,384]{1,0:T(8,128)(2,1)S(1)}, u32[]{:S(2)}, u32[]{:S(2)}) collective-permute-start(bf16[448,384]{1,0:T(8,128)(2,1)S(1)} %add.23.refs_0_), channel_id=1, source_target_pairs={{0,1},{1,0},{2,3},{3,2},{4,5},{5,4},{6,7},{7,6},{8,9},{9,8},{10,11... | collective-permute-start | bytes 1032200 | tf_op jit(solution)/shard_map/ppermute | solution.py:774
  150.7 16.9 %collective-permute-start.19 = (bf16[448,384]{1,0:T(8,128)(2,1)S(1)}, bf16[448,384]{1,0:T(8,128)(2,1)S(1)}, u32[]{:S(2)}, u32[]{:S(2)}) collective-permute-start(bf16[448,384]{1,0:T(8,128)(2,1)S(1)} %collective-permute-done.17.refs_1_), channel_id=1, source_target_pairs={{0,1},{1,0},{2,3},{3,2},{4,5},{5,4},{6,7},{7,6},{8,9},{9,8},{10,11... | collective-permute-start | bytes 1032200 | tf_op jit(solution)/shard_map/ppermute | solution.py:774
  158.1 7.9 %collective-permute-start.10 = (bf16[160,384]{1,0:T(8,128)(2,1)S(1)}, bf16[160,384]{1,0:T(8,128)(2,1)S(1)}, u32[]{:S(2)}, u32[]{:S(2)}) collective-permute-start(bf16[160,384]{1,0:T(8,128)(2,1)S(1)} %add.20.refs_0_), channel_id=1, source_target_pairs={{0,1},{1,0},{2,3},{3,2},{4,5},{5,4},{6,7},{7,6},{8,9},{9,8},{10,11... | collective-permute-start | bytes 368648 | tf_op jit(solution)/shard_map/ppermute | solution.py:774
  158.7 7.3 %collective-permute-start.11 = (bf16[160,384]{1,0:T(8,128)(2,1)S(1)}, bf16[160,384]{1,0:T(8,128)(2,1)S(1)}, u32[]{:S(2)}, u32[]{:S(2)}) collective-permute-start(bf16[160,384]{1,0:T(8,128)(2,1)S(1)} %collective-permute-done.9.refs_1_), channel_id=1, source_target_pairs={{0,1},{1,0},{2,3},{3,2},{4,5},{5,4},{6,7},{7,6},{8,9},{9,8},{10,11... | collective-permute-start | bytes 368648 | tf_op jit(solution)/shard_map/ppermute | solution.py:774
  (3 other events, 25.2 us)

commit v4 on v3

--- a/solution.py
+++ b/solution.py
@@ -774,32 +774,54 @@
     return lax.ppermute(value, axis, [(i, i ^ bit) for i in range(size)])
 
 
-def reduce_grads(idx, keep, send, replicas):
-    got = flip(send, "replica", replicas, 1)
-    own, other = merge(idx, 0, keep, got)
-    got = flip(other, "group", 2, 1)
-    own, other = merge(idx, 2, own, got)
-    got = flip(other, "replica", replicas, 2)
-    own = own + got
-    bit = 4
+def exchange(own, replicas, bit):
     while bit < replicas:
         got = flip(own, "replica", replicas, bit)
         own = own + got
         bit *= 2
+    return own
+
+
+def reduce_grads(idx, keep, send, replicas):
+    own, other = merge(idx, 0, keep, flip(send, "replica", replicas, 1))
+    own, other = merge(idx, 2, own, flip(other, "group", 2, 1))
+    got = flip(other, "replica", replicas, 2)
+    own = own + got
+    own = exchange(own, replicas, 4)
     side = flip(own, "replica", replicas, 2)
     far_own = flip(own, "replica", replicas, 1)
     return own, side, far_own, flip(side, "replica", replicas, 1)
 
 
+def reduce_large_grads(idx, keep, send, replicas):
+    own, other = merge(idx, 0, keep, flip(send, "replica", replicas, 1))
+    own, other = merge(idx, 2, own, flip(other, "group", 2, 1))
+    halves = (2, own.shape[0] // 2, own.shape[1])
+    got = flip(other, "replica", replicas, 2)
+    own, other = merge(idx, 3, own.reshape(halves), got.reshape(halves))
+    got = flip(other, "replica", replicas, 4)
+    own = own + got
+    own = exchange(own, replicas, 8)
+    next_own = flip(own, "replica", replicas, 4)
+    side = flip(own, "replica", replicas, 2)
+    next_side = flip(next_own, "replica", replicas, 2)
+    parts = (own, next_own, side, next_side)
+    far = [flip(part, "replica", replicas, 1) for part in parts]
+    return (*parts, *far)
+
+
 def places(idx_ref):
     core, side = idx_ref[1], idx_ref[2]
     return 2 * core + side, 2 * core + 1 - side, 2 * (1 - core) + side, 2 * (1 - core) + 1 - side
 
 
 def unpack_mlp_kernel(idx_ref, *refs):
-    ins, outs, mlp = refs[:4], refs[4:12], refs[12]
+    ins, outs, mlp = refs[:8], refs[8:16], refs[16]
+    low = idx_ref[3]
+    lines = ins[0].shape[0]
     for k, place in enumerate(places(idx_ref)):
-        mlp[place] = ins[k][...].astype(F32)
+        mlp[place, at(low * lines, lines)] = ins[2 * k][...].astype(F32)
+        mlp[place, at((1 - low) * lines, lines)] = ins[2 * k + 1][...].astype(F32)
     g_out, g_bout, g_fc1, g_bfc1, g_fc2, g_bfc2, g_gtwo, g_stwo = outs
     half, width = g_out.shape
     hidden = g_fc1.shape[1]
@@ -849,10 +871,10 @@
 def run_unpack(kernel, idx, parts, shapes):
     return pl.pallas_call(
         kernel,
-        in_specs=[SMEM_SPEC] + [VMEM_SPEC] * 4,
+        in_specs=[SMEM_SPEC] + [VMEM_SPEC] * len(parts),
         out_specs=[VMEM_SPEC] * len(shapes),
         out_shape=[jax.ShapeDtypeStruct(s, F32) for s in shapes],
-        scratch_shapes=[pltpu.VMEM((4, *parts[0].shape), F32)],
+        scratch_shapes=[pltpu.VMEM((4, parts[0].shape[0] * len(parts) // 4, parts[0].shape[1]), F32)],
         compiler_params=pltpu.CompilerParams(vmem_limit_bytes=8 << 20),
     )(idx, *parts)
 
@@ -879,7 +901,7 @@
     gain_one, shift_one, gain_two, shift_two,
 ):
     replica = lax.axis_index("replica")
-    idx = jnp.stack([lax.axis_index("group"), replica & 1, (replica >> 1) & 1]).astype(jnp.int32)
+    idx = jnp.stack([lax.axis_index("group"), replica & 1, (replica >> 1) & 1, (replica >> 2) & 1]).astype(jnp.int32)
     count = images.shape[0] * images.shape[1]
     vectors = (b_qv, b_out, b_fc1, b_fc2, gain_one, shift_one, gain_two, shift_two)
     first, small = run_pack_first(idx, w_qkv, vectors)
@@ -900,7 +922,7 @@
     dqkv, _, _, keep_c, send_c = carried
     din = run_input_grad(view.shape, hat, rstd, dqkv, dx, w_all, vec)
     out = run_outputs(view.shape, image_count, act, middle, w_two, vec)
-    mlp = reduce_grads(idx, keep_b, send_b, replicas)
+    mlp = reduce_large_grads(idx, keep_b, send_b, replicas)
     attention = reduce_grads(idx, keep_c, send_c, replicas)
     shape_of = lambda *arrays: [v.shape for v in arrays]
     g_out, g_bout, g_fc1, g_bfc1, g_fc2, g_bfc2, g_gtwo, g_stwo = run_unpack(

time: 171 us -> 152 us (0.89)
  waiting for transfers between devices: 59 us -> 34.1 us
  starting transfers between devices: 22.9 us -> 28.9 us
    ppermute x20 -> x24, waiting for transfers between devices: 59 us -> 34.1 us  [flip(): return lax.ppermute(value, axis, [(i, i ^ bit) for i in range(size)])]
    ppermute x20 -> x24, starting transfers between devices: 22.9 us -> 28.9 us  [flip(): return lax.ppermute(value, axis, [(i, i ^ bit) for i in range(size)])]
  transfers between devices with their start and end apart: 20 -> 24, of which waited for: 9 -> 8; matrix products, arithmetic and copies ran while one was open for 0% -> 0% of each run, Pallas kernels for 30% -> 35%
where the time goes in v4:
time: 152 us; the launch traced here: 151 us
  Pallas kernels  86 us (57%)
  waiting for transfers between devices  34.1 us (22%)
  starting transfers between devices  28.9 us (19%)
    ppermute x24, waiting for transfers between devices, flip(): return lax.ppermute(value, axis, [(i, i ^ bit) for i in range(size)])  34.1 us
    ppermute x24, starting transfers between devices, flip(): return lax.ppermute(value, axis, [(i, i ^ bit) for i in range(size)])  28.9 us
    pallas_call x1, Pallas kernels, run_mlp(): pl.pallas_call(mlp_kernel, grid=(micro,), in_specs=[SMEM_SPEC, SMEM_SPEC,...  27.2 us
    pallas_call x2, Pallas kernels, run_attention_back(): pl.pallas_call(partial(attention_back_kernel, begin, last), grid=(end - b...  19.7 us
    pallas_call x1, Pallas kernels, run_attention(): pl.pallas_call(attention_kernel, grid=(count // 2,), in_specs=[SMEM_SPEC,...  12.2 us
    pallas_call x1, Pallas kernels, run_outputs(): pl.pallas_call(outputs_kernel, grid=(count // 2,), in_specs=[SMEM_SPEC] +...  7.39 us
    pallas_call x1, Pallas kernels, run_input_grad(): pl.pallas_call(input_grad_kernel, grid=(count // 2,), in_specs=[HBM_SPEC]...  7.2 us
    pallas_call x2, Pallas kernels, run_unpack(): pl.pallas_call(kernel, in_specs=[SMEM_SPEC] + [VMEM_SPEC] * len(parts), o...  3.97 us
  transfers between devices with their start and end apart: 24, of which 8 were waited for; matrix products, arithmetic and copies ran while one was open for 0% of the time, Pallas kernels for 35%

profile of v4, /device:TPU:1, one launch (start us, length us, event | category | flops | bytes accessed | tf_op | source)
XLA Modules:
  0.0 151.4 jit_solution(2420901461917320399)
XLA Ops:
  1.3 2.8 %pack_second.1 = bf16[96,3456]{1,0:T(8,128)(2,1)} custom-call(s32[4]{0:T(128)} %pad_add_fusion.idx_ref, bf16[192,384]{1,0:T(8,128)(2,1)} %wo_ref.3, bf16[192,1536]{1,0:T(8,128)(2,1)} %w1_ref.3, bf16[768,384]{1,0:T(8,128)(2,1)} %w2_ref.3), custom_call_target="tpu_custom_call" | custom-call | tf_op jit(solution)/shard_map/pack_second/pallas_call | solution.py:172
  4.0 2.0 %collective-permute-start.2 = (bf16[96,3456]{1,0:T(8,128)(2,1)}, bf16[96,3456]{1,0:T(8,128)(2,1)S(1)}, u32[]{:S(2)}, u32[]{:S(2)}) collective-permute-start(bf16[96,3456]{1,0:T(8,128)(2,1)} %pack_second.1), channel_id=1, source_target_pairs={{0,16},{16,0},{1,17},{17,1},{2,18},{18,2},{3,19},{19,3},{4,20},{20... | collective-permute-start | bytes 1990664 | tf_op jit(solution)/shard_map/ppermute | solution.py:774
  6.1 2.4 %pack_first.1 = (bf16[112,1152]{1,0:T(8,128)(2,1)}, bf16[8,768]{1,0:T(8,128)(2,1)}) custom-call(s32[4]{0:T(128)} %pad_add_fusion.idx_ref, bf16[192,1152]{1,0:T(8,128)(2,1)} %w_ref.1, bf16[384]{0:T(512)(128)(2,1)} %refs_0_.1, bf16[192]{0:T(256)(128)(2,1)} %refs_1_.1, bf16[768]{0:T(1024)(128)(2,1)} %refs_2_.1, bf16[192]{0:T(256)(128)(2,1)} %refs_3_.1, ...), custom_call_target="tpu_custom_call" | custom-call | tf_op jit(solution)/shard_map/pack_first/pallas_call | solution.py:154
  8.5 17.9 %collective-permute-done.near_ref = bf16[112,1152]{1,0:T(8,128)(2,1)S(1)} collective-permute-done((bf16[112,1152]{1,0:T(8,128)(2,1)}, bf16[112,1152]{1,0:T(8,128)(2,1)S(1)}, u32[]{:S(2)}, u32[]{:S(2)}) %collective-permute-start) | collective-permute-done | bytes 258080 | tf_op jit(solution)/shard_map/ppermute | solution.py:774
  29.5 12.2 %attention_fwd.1 = (bf16[8,208,1152]{2,1,0:T(8,128)(2,1)}, bf16[8,6,208,256]{3,2,1,0:T(8,128)(2,1)}, bf16[8,208,384]{2,1,0:T(8,128)(2,1)}, bf16[8,208,384]{2,1,0...) custom-call(s32[4]{0:T(128)S(1)} %copy-done.4, ...), custom_call_target="tpu_custom_call" | custom-call | flops 5368709120 | bytes 20971520 | tf_op jit(solution)/shard_map/attention_fwd/pallas_call | solution.py:598
  41.8 27.2 %mlp_fwd_bwd.1 = (bf16[8,208,1536]{2,1,0:T(8,128)(2,1)}, f32[8,208,384]{2,1,0:T(8,128)}, bf16[8,208,384]{2,1,0:T(8,128)(2,1)}, bf16[8,208,384]{2,1,0:T(8,128)(2,...) custom-call(s32[4]{0:T(128)S(1)} %copy-done.4, ...), custom_call_target="tpu_custom_call" | custom-call | flops 12884901888 | bytes 20971520 | tf_op jit(solution)/shard_map/mlp_fwd_bwd/pallas_call | solution.py:638
  69.4 6.2 %shard_map.254 = (bf16[8,208,1152]{2,1,0:T(8,128)(2,1)}, f32[384,1152]{1,0:T(8,128)S(1)}, f32[8,1152]{1,0:T(8,128)S(1)}) custom-call(s32[4]{0:T(128)S(1)} %copy-done.4, bf16[8,208,384]{2,1,0:T(8,128)(2,1)} %get-tuple-element.67.hat_hbm, bf16[8,208,1152]{2,1,0:T(8,128)(2,1)} %get-tuple-element.69.qkv_hbm, ...), custom_call_target="tpu_custom_call" | custom-call | flops 2147483648 | bytes 20971520 | tf_op jit(solution)/shard_map/pallas_call | solution.py:689
  76.4 1.5 %collective-permute-start.13 = (bf16[2,448,384]{2,1,0:T(8,128)(2,1)S(1)}, bf16[2,448,384]{2,1,0:T(8,128)(2,1)S(1)}, u32[]{:S(2)}, u32[]{:S(2)}) collective-permute-start(bf16[2,448,384]{2,1,0:T(8,128)(2,1)S(1)} %get-tuple-element.89), channel_id=1, source_target_pairs={{0,16},{16,0},{1,17},{17,1},{2,18},{18,2},{3,19},{19,3},{4,20},{20... | collective-permute-start | bytes 2064392 | tf_op jit(solution)/shard_map/ppermute | solution.py:774
  77.9 13.5 %shard_map.255 = (bf16[8,208,1152]{2,1,0:T(8,128)(2,1)}, f32[384,1152]{1,0:T(8,128)S(1)}, f32[8,1152]{1,0:T(8,128)S(1)}, bf16[2,2,160,384]{3,2,1,0:T(8,128)(2,1)S(1)}, bf16[2,2,160,384]{3,2,1,0:T(8,128)(2,1)S(1)}) custom-call(s32[4]{0:T(128)S(1)} %copy-done.4, ...), custom_call_target="tpu_custom_call", output_to_operand_aliasing={{0}: (8, {}), {1}: (9, {}), {2}: (10, {})} | custom-call | flops 6442450944 | bytes 20971520 | tf_op jit(solution)/shard_map/pallas_call | solution.py:689
  91.9 1.3 collective-permute-done.13.b_ref
  93.9 1.5 %collective-permute-start.14 = (bf16[448,384]{1,0:T(8,128)(2,1)S(1)}, bf16[448,384]{1,0:T(8,128)(2,1)S(1)}, u32[]{:S(2)}, u32[]{:S(2)}) collective-permute-start(bf16[448,384]{1,0:T(8,128)(2,1)S(1)} %get-tuple-element.91), channel_id=1, source_target_pairs={{0,2},{1,3},{2,0},{3,1},{4,6},{5,7},{6,4},{7,5},{8,10},{9,11},{10,... | collective-permute-start | bytes 1032200 | tf_op jit(solution)/shard_map/ppermute | solution.py:774
  97.4 5.3 %collective-permute-done.14 = bf16[448,384]{1,0:T(8,128)(2,1)S(1)} collective-permute-done((bf16[448,384]{1,0:T(8,128)(2,1)S(1)}, bf16[448,384]{1,0:T(8,128)(2,1)S(1)}, u32[]{:S(2)}, u32[]{:S(2)}) %collective-permute-start.14) | collective-permute-done | bytes 344096 | tf_op jit(solution)/shard_map/ppermute | solution.py:774
  103.3 1.6 %collective-permute-start.15 = (bf16[224,384]{1,0:T(8,128)(2,1)S(1)}, bf16[224,384]{1,0:T(8,128)(2,1)S(1)}, u32[]{:S(2)}, u32[]{:S(2)}) collective-permute-start(bf16[224,384]{1,0:T(8,128)(2,1)S(1)} %get-tuple-element.93), channel_id=1, source_target_pairs={{0,4},{1,5},{2,6},{3,7},{4,0},{5,1},{6,2},{7,3},{8,12},{9,13},{10,... | collective-permute-start | bytes 516104 | tf_op jit(solution)/shard_map/ppermute | solution.py:774
  105.4 1.3 collective-permute-start.6
  107.7 2.5 %collective-permute-start.16 = (bf16[224,384]{1,0:T(8,128)(2,1)S(1)}, bf16[224,384]{1,0:T(8,128)(2,1)S(1)}, u32[]{:S(2)}, u32[]{:S(2)}) collective-permute-start(bf16[224,384]{1,0:T(8,128)(2,1)S(1)} %add.18), channel_id=1, source_target_pairs={{0,8},{1,9},{2,10},{3,11},{4,12},{5,13},{6,14},{7,15},{8,0},{9,1},... | collective-permute-start | bytes 516104 | tf_op jit(solution)/shard_map/ppermute | solution.py:774
  110.3 1.4 collective-permute-start.7
  111.6 3.9 %collective-permute-done.16 = bf16[224,384]{1,0:T(8,128)(2,1)S(1)} collective-permute-done((bf16[224,384]{1,0:T(8,128)(2,1)S(1)}, bf16[224,384]{1,0:T(8,128)(2,1)S(1)}, u32[]{:S(2)}, u32[]{:S(2)}) %collective-permute-start.16) | collective-permute-done | bytes 172064 | tf_op jit(solution)/shard_map/ppermute | solution.py:774
  115.8 5.1 %collective-permute-start.8 = (bf16[160,384]{1,0:T(8,128)(2,1)S(1)}, bf16[160,384]{1,0:T(8,128)(2,1)S(1)}, u32[]{:S(2)}, u32[]{:S(2)}) collective-permute-start(bf16[160,384]{1,0:T(8,128)(2,1)S(1)} %add.16), channel_id=1, source_target_pairs={{0,8},{1,9},{2,10},{3,11},{4,12},{5,13},{6,14},{7,15},{8,0},{9,1},... | collective-permute-start | bytes 368648 | tf_op jit(solution)/shard_map/ppermute | solution.py:774
  120.9 3.1 %collective-permute-done.8 = bf16[160,384]{1,0:T(8,128)(2,1)S(1)} collective-permute-done((bf16[160,384]{1,0:T(8,128)(2,1)S(1)}, bf16[160,384]{1,0:T(8,128)(2,1)S(1)}, u32[]{:S(2)}, u32[]{:S(2)}) %collective-permute-start.8) | collective-permute-done | bytes 122912 | tf_op jit(solution)/shard_map/ppermute | solution.py:774
  124.0 3.1 %collective-permute-start.10 = (bf16[160,384]{1,0:T(8,128)(2,1)S(1)}, bf16[160,384]{1,0:T(8,128)(2,1)S(1)}, u32[]{:S(2)}, u32[]{:S(2)}) collective-permute-start(bf16[160,384]{1,0:T(8,128)(2,1)S(1)} %add.17.refs_0_), channel_id=1, source_target_pairs={{0,1},{1,0},{2,3},{3,2},{4,5},{5,4},{6,7},{7,6},{8,9},{9,8},{10,11... | collective-permute-start | bytes 368648 | tf_op jit(solution)/shard_map/ppermute | solution.py:774
  129.8 7.4 %layer_outputs.1 = bf16[4728,128]{1,0:T(8,128)(2,1)} custom-call(s32[4,1]{1,0:T(4,128)S(1)} %copy.33.count_ref, bf16[8,208,1536]{2,1,0:T(8,128)(2,1)} %get-tuple-element.64.act_hbm, f32[8,208,384]{2,1,0:T(8,128)} %get-tuple-element.65.middle_hbm, bf16[1536,384]{1,0:T(8,128)(2,1)S(1)} %get-tuple-element.66.w2_ref, f32[8,384]{1,0:T(8,128)S(1)} %get-tuple-element.62.vec.vec_ref), custom_call_target="tpu_custom_call" | custom-call | flops 2147483648 | bytes 20971520 | tf_op jit(solution)/shard_map/layer_outputs/pallas_call | solution.py:740
  140.2 7.2 %input_grad.1 = bf16[4728,128]{1,0:T(8,128)(2,1)} custom-call(bf16[8,208,384]{2,1,0:T(8,128)(2,1)} %get-tuple-element.67.hat_hbm, f32[8,208,128]{2,1,0:T(8,128)} %get-tuple-element.68.rstd_hbm, bf16[8,208,1152]{2,1,0:T(8,128)(2,1)} %get-tuple-element.76.dqkv_hbm, bf16[8,208,384]{2,1,0:T(8,128)(2,1)} %get-tuple-element.77.dx_hbm, ...), custom_call_target="tpu_custom_call" | custom-call | flops 2147483648 | bytes 20971520 | tf_op jit(solution)/shard_map/input_grad/pallas_call | solution.py:719
  147.4 1.6 %shard_map.258 = (f32[192,1152]{1,0:T(8,128)}, f32[384]{0:T(512)}, f32[192]{0:T(256)}, f32[192]{0:T(256)}) custom-call(s32[4]{0:T(128)S(1)} %copy-done.4, bf16[160,384]{1,0:T(8,128)(2,1)S(1)} %add.17.refs_0_, bf16[160,384]{1,0:T(8,128)(2,1)S(1)} %collective-permute-done.9.refs_1_, bf16[160,384]{1,0:T(8,128)(2,1)S(1)} %collective-permute-done.10.refs_2_, ...), custom_call_target="tpu_custom_call" | custom-call | tf_op jit(solution)/shard_map/pallas_call | solution.py:872
  149.1 2.4 %shard_map.262 = (f32[192,384]{1,0:T(8,128)}, f32[192]{0:T(256)}, f32[192,1536]{1,0:T(8,128)}, f32[768]{0:T(1024)}, f32[768,384]{1,0:T(8,128)}, /*index=5*/f32[192]{0:T(256)}, f32[192]{0:T(256)}, f32[192]{0:T(256)}) custom-call(s32[4]{0:T(128)S(1)} %copy-done.4, bf16[224,384]{1,0:T(8,128)(2,1)S(1)} %add.19.refs_0_, ...), custom_call_target="tpu_custom_call" | custom-call | tf_op jit(solution)/shard_map/pallas_call | solution.py:872
  (60 shorter events, 16.0 us)
Async XLA Ops:
  4.0 23.6 %collective-permute-start.2 = (bf16[96,3456]{1,0:T(8,128)(2,1)}, bf16[96,3456]{1,0:T(8,128)(2,1)S(1)}, u32[]{:S(2)}, u32[]{:S(2)}) collective-permute-start(bf16[96,3456]{1,0:T(8,128)(2,1)} %pack_second.1), channel_id=1, source_target_pairs={{0,16},{16,0},{1,17},{17,1},{2,18},{18,2},{3,19},{19,3},{4,20},{20... | collective-permute-start | bytes 1990664 | tf_op jit(solution)/shard_map/ppermute | solution.py:774
  8.5 17.9 %collective-permute-start = (bf16[112,1152]{1,0:T(8,128)(2,1)}, bf16[112,1152]{1,0:T(8,128)(2,1)S(1)}, u32[]{:S(2)}, u32[]{:S(2)}) collective-permute-start(bf16[112,1152]{1,0:T(8,128)(2,1)} %get-tuple-element.59), channel_id=1, source_target_pairs={{0,16},{16,0},{1,17},{17,1},{2,18},{18,2},{3,19},{19,3},{4,20},{20... | collective-permute-start | bytes 774152 | tf_op jit(solution)/shard_map/ppermute | solution.py:774
  26.4 2.4 %collective-permute-start.1 = (bf16[112,1152]{1,0:T(8,128)(2,1)S(1)}, bf16[112,1152]{1,0:T(8,128)(2,1)S(1)}, u32[]{:S(2)}, u32[]{:S(2)}) collective-permute-start(bf16[112,1152]{1,0:T(8,128)(2,1)S(1)} %collective-permute-done.near_ref), channel_id=1, source_target_pairs={{0,1},{1,0},{2,3},{3,2},{4,5},{5,4},{6,7},{7,6},{8,9},{9,8},{10,11... | collective-permute-start | bytes 774152 | tf_op jit(solution)/shard_map/ppermute | solution.py:774
  27.7 14.1 %collective-permute-start.3 = (bf16[96,3456]{1,0:T(8,128)(2,1)S(1)}, bf16[96,3456]{1,0:T(8,128)(2,1)S(1)}, u32[]{:S(2)}, u32[]{:S(2)}) collective-permute-start(bf16[96,3456]{1,0:T(8,128)(2,1)S(1)} %collective-permute-done.2.near_ref), channel_id=1, source_target_pairs={{0,1},{1,0},{2,3},{3,2},{4,5},{5,4},{6,7},{7,6},{8,9},{9,8},{10,11... | collective-permute-start | bytes 1990664 | tf_op jit(solution)/shard_map/ppermute | solution.py:774
  69.0 6.6 %collective-permute-start.12 = (bf16[2,2,448,384]{3,2,1,0:T(8,128)(2,1)S(1)}, bf16[2,2,448,384]{3,2,1,0:T(8,128)(2,1)S(1)}, u32[]{:S(2)}, u32[]{:S(2)}) collective-permute-start(bf16[2,2,448,384]{3,2,1,0:T(8,128)(2,1)S(1)} %get-tuple-element.87), channel_id=1, source_target_pairs={{0,1},{1,0},{2,3},{3,2},{4,5},{5,4},{6,7},{7,6},{8,9},{9,8},{10,11... | collective-permute-start | bytes 4128776 | tf_op jit(solution)/shard_map/ppermute | solution.py:774
  76.4 16.9 %collective-permute-start.13 = (bf16[2,448,384]{2,1,0:T(8,128)(2,1)S(1)}, bf16[2,448,384]{2,1,0:T(8,128)(2,1)S(1)}, u32[]{:S(2)}, u32[]{:S(2)}) collective-permute-start(bf16[2,448,384]{2,1,0:T(8,128)(2,1)S(1)} %get-tuple-element.89), channel_id=1, source_target_pairs={{0,16},{16,0},{1,17},{17,1},{2,18},{18,2},{3,19},{19,3},{4,20},{20... | collective-permute-start | bytes 2064392 | tf_op jit(solution)/shard_map/ppermute | solution.py:774
  91.4 4.0 %collective-permute-start.4 = (bf16[2,2,160,384]{3,2,1,0:T(8,128)(2,1)S(1)}, bf16[2,2,160,384]{3,2,1,0:T(8,128)(2,1)S(1)}, u32[]{:S(2)}, u32[]{:S(2)}) collective-permute-start(bf16[2,2,160,384]{3,2,1,0:T(8,128)(2,1)S(1)} %get-tuple-element.79), channel_id=1, source_target_pairs={{0,1},{1,0},{2,3},{3,2},{4,5},{5,4},{6,7},{7,6},{8,9},{9,8},{10,11... | collective-permute-start | bytes 1474568 | tf_op jit(solution)/shard_map/ppermute | solution.py:774
  93.9 8.7 %collective-permute-start.14 = (bf16[448,384]{1,0:T(8,128)(2,1)S(1)}, bf16[448,384]{1,0:T(8,128)(2,1)S(1)}, u32[]{:S(2)}, u32[]{:S(2)}) collective-permute-start(bf16[448,384]{1,0:T(8,128)(2,1)S(1)} %get-tuple-element.91), channel_id=1, source_target_pairs={{0,2},{1,3},{2,0},{3,1},{4,6},{5,7},{6,4},{7,5},{8,10},{9,11},{10,... | collective-permute-start | bytes 1032200 | tf_op jit(solution)/shard_map/ppermute | solution.py:774
  96.1 8.7 %collective-permute-start.5 = (bf16[2,160,384]{2,1,0:T(8,128)(2,1)S(1)}, bf16[2,160,384]{2,1,0:T(8,128)(2,1)S(1)}, u32[]{:S(2)}, u32[]{:S(2)}) collective-permute-start(bf16[2,160,384]{2,1,0:T(8,128)(2,1)S(1)} %get-tuple-element.81), channel_id=1, source_target_pairs={{0,16},{16,0},{1,17},{17,1},{2,18},{18,2},{3,19},{19,3},{4,20},{20... | collective-permute-start | bytes 737288 | tf_op jit(solution)/shard_map/ppermute | solution.py:774
  103.3 4.4 %collective-permute-start.15 = (bf16[224,384]{1,0:T(8,128)(2,1)S(1)}, bf16[224,384]{1,0:T(8,128)(2,1)S(1)}, u32[]{:S(2)}, u32[]{:S(2)}) collective-permute-start(bf16[224,384]{1,0:T(8,128)(2,1)S(1)} %get-tuple-element.93), channel_id=1, source_target_pairs={{0,4},{1,5},{2,6},{3,7},{4,0},{5,1},{6,2},{7,3},{8,12},{9,13},{10,... | collective-permute-start | bytes 516104 | tf_op jit(solution)/shard_map/ppermute | solution.py:774
  105.4 4.8 %collective-permute-start.6 = (bf16[160,384]{1,0:T(8,128)(2,1)S(1)}, bf16[160,384]{1,0:T(8,128)(2,1)S(1)}, u32[]{:S(2)}, u32[]{:S(2)}) collective-permute-start(bf16[160,384]{1,0:T(8,128)(2,1)S(1)} %get-tuple-element.83), channel_id=1, source_target_pairs={{0,2},{1,3},{2,0},{3,1},{4,6},{5,7},{6,4},{7,5},{8,10},{9,11},{10,... | collective-permute-start | bytes 368648 | tf_op jit(solution)/shard_map/ppermute | solution.py:774
  107.7 7.9 %collective-permute-start.16 = (bf16[224,384]{1,0:T(8,128)(2,1)S(1)}, bf16[224,384]{1,0:T(8,128)(2,1)S(1)}, u32[]{:S(2)}, u32[]{:S(2)}) collective-permute-start(bf16[224,384]{1,0:T(8,128)(2,1)S(1)} %add.18), channel_id=1, source_target_pairs={{0,8},{1,9},{2,10},{3,11},{4,12},{5,13},{6,14},{7,15},{8,0},{9,1},... | collective-permute-start | bytes 516104 | tf_op jit(solution)/shard_map/ppermute | solution.py:774
  110.3 5.5 %collective-permute-start.7 = (bf16[160,384]{1,0:T(8,128)(2,1)S(1)}, bf16[160,384]{1,0:T(8,128)(2,1)S(1)}, u32[]{:S(2)}, u32[]{:S(2)}) collective-permute-start(bf16[160,384]{1,0:T(8,128)(2,1)S(1)} %add.15), channel_id=1, source_target_pairs={{0,4},{1,5},{2,6},{3,7},{4,0},{5,1},{6,2},{7,3},{8,12},{9,13},{10,... | collective-permute-start | bytes 368648 | tf_op jit(solution)/shard_map/ppermute | solution.py:774
  115.6 13.0 %collective-permute-start.17 = (bf16[224,384]{1,0:T(8,128)(2,1)S(1)}, bf16[224,384]{1,0:T(8,128)(2,1)S(1)}, u32[]{:S(2)}, u32[]{:S(2)}) collective-permute-start(bf16[224,384]{1,0:T(8,128)(2,1)S(1)} %add.19.refs_0_), channel_id=1, source_target_pairs={{0,4},{1,5},{2,6},{3,7},{4,0},{5,1},{6,2},{7,3},{8,12},{9,13},{10,... | collective-permute-start | bytes 516104 | tf_op jit(solution)/shard_map/ppermute | solution.py:774
  115.8 8.2 %collective-permute-start.8 = (bf16[160,384]{1,0:T(8,128)(2,1)S(1)}, bf16[160,384]{1,0:T(8,128)(2,1)S(1)}, u32[]{:S(2)}, u32[]{:S(2)}) collective-permute-start(bf16[160,384]{1,0:T(8,128)(2,1)S(1)} %add.16), channel_id=1, source_target_pairs={{0,8},{1,9},{2,10},{3,11},{4,12},{5,13},{6,14},{7,15},{8,0},{9,1},... | collective-permute-start | bytes 368648 | tf_op jit(solution)/shard_map/ppermute | solution.py:774
  124.0 14.3 %collective-permute-start.10 = (bf16[160,384]{1,0:T(8,128)(2,1)S(1)}, bf16[160,384]{1,0:T(8,128)(2,1)S(1)}, u32[]{:S(2)}, u32[]{:S(2)}) collective-permute-start(bf16[160,384]{1,0:T(8,128)(2,1)S(1)} %add.17.refs_0_), channel_id=1, source_target_pairs={{0,1},{1,0},{2,3},{3,2},{4,5},{5,4},{6,7},{7,6},{8,9},{9,8},{10,11... | collective-permute-start | bytes 368648 | tf_op jit(solution)/shard_map/ppermute | solution.py:774
  127.1 10.1 %collective-permute-start.9 = (bf16[160,384]{1,0:T(8,128)(2,1)S(1)}, bf16[160,384]{1,0:T(8,128)(2,1)S(1)}, u32[]{:S(2)}, u32[]{:S(2)}) collective-permute-start(bf16[160,384]{1,0:T(8,128)(2,1)S(1)} %add.17.refs_0_), channel_id=1, source_target_pairs={{0,2},{1,3},{2,0},{3,1},{4,6},{5,7},{6,4},{7,5},{8,10},{9,11},{10,... | collective-permute-start | bytes 368648 | tf_op jit(solution)/shard_map/ppermute | solution.py:774
  128.4 10.4 %collective-permute-start.18 = (bf16[224,384]{1,0:T(8,128)(2,1)S(1)}, bf16[224,384]{1,0:T(8,128)(2,1)S(1)}, u32[]{:S(2)}, u32[]{:S(2)}) collective-permute-start(bf16[224,384]{1,0:T(8,128)(2,1)S(1)} %add.19.refs_0_), channel_id=1, source_target_pairs={{0,2},{1,3},{2,0},{3,1},{4,6},{5,7},{6,4},{7,5},{8,10},{9,11},{10,... | collective-permute-start | bytes 516104 | tf_op jit(solution)/shard_map/ppermute | solution.py:774
  128.6 10.7 %collective-permute-start.19 = (bf16[224,384]{1,0:T(8,128)(2,1)S(1)}, bf16[224,384]{1,0:T(8,128)(2,1)S(1)}, u32[]{:S(2)}, u32[]{:S(2)}) collective-permute-start(bf16[224,384]{1,0:T(8,128)(2,1)S(1)} %collective-permute-done.17.refs_1_), channel_id=1, source_target_pairs={{0,2},{1,3},{2,0},{3,1},{4,6},{5,7},{6,4},{7,5},{8,10},{9,11},{10,... | collective-permute-start | bytes 516104 | tf_op jit(solution)/shard_map/ppermute | solution.py:774
  137.2 10.2 %collective-permute-start.11 = (bf16[160,384]{1,0:T(8,128)(2,1)S(1)}, bf16[160,384]{1,0:T(8,128)(2,1)S(1)}, u32[]{:S(2)}, u32[]{:S(2)}) collective-permute-start(bf16[160,384]{1,0:T(8,128)(2,1)S(1)} %collective-permute-done.9.refs_1_), channel_id=1, source_target_pairs={{0,1},{1,0},{2,3},{3,2},{4,5},{5,4},{6,7},{7,6},{8,9},{9,8},{10,11... | collective-permute-start | bytes 368648 | tf_op jit(solution)/shard_map/ppermute | solution.py:774
  138.2 10.8 %collective-permute-start.20 = (bf16[224,384]{1,0:T(8,128)(2,1)S(1)}, bf16[224,384]{1,0:T(8,128)(2,1)S(1)}, u32[]{:S(2)}, u32[]{:S(2)}) collective-permute-start(bf16[224,384]{1,0:T(8,128)(2,1)S(1)} %add.19.refs_0_), channel_id=1, source_target_pairs={{0,1},{1,0},{2,3},{3,2},{4,5},{5,4},{6,7},{7,6},{8,9},{9,8},{10,11... | collective-permute-start | bytes 516104 | tf_op jit(solution)/shard_map/ppermute | solution.py:774
  138.3 10.8 %collective-permute-start.21 = (bf16[224,384]{1,0:T(8,128)(2,1)S(1)}, bf16[224,384]{1,0:T(8,128)(2,1)S(1)}, u32[]{:S(2)}, u32[]{:S(2)}) collective-permute-start(bf16[224,384]{1,0:T(8,128)(2,1)S(1)} %collective-permute-done.17.refs_1_), channel_id=1, source_target_pairs={{0,1},{1,0},{2,3},{3,2},{4,5},{5,4},{6,7},{7,6},{8,9},{9,8},{10,11... | collective-permute-start | bytes 516104 | tf_op jit(solution)/shard_map/ppermute | solution.py:774
  138.7 10.3 %collective-permute-start.22 = (bf16[224,384]{1,0:T(8,128)(2,1)S(1)}, bf16[224,384]{1,0:T(8,128)(2,1)S(1)}, u32[]{:S(2)}, u32[]{:S(2)}) collective-permute-start(bf16[224,384]{1,0:T(8,128)(2,1)S(1)} %collective-permute-done.18.refs_2_), channel_id=1, source_target_pairs={{0,1},{1,0},{2,3},{3,2},{4,5},{5,4},{6,7},{7,6},{8,9},{9,8},{10,11... | collective-permute-start | bytes 516104 | tf_op jit(solution)/shard_map/ppermute | solution.py:774
  139.3 9.8 %collective-permute-start.23 = (bf16[224,384]{1,0:T(8,128)(2,1)S(1)}, bf16[224,384]{1,0:T(8,128)(2,1)S(1)}, u32[]{:S(2)}, u32[]{:S(2)}) collective-permute-start(bf16[224,384]{1,0:T(8,128)(2,1)S(1)} %collective-permute-done.19.refs_3_), channel_id=1, source_target_pairs={{0,1},{1,0},{2,3},{3,2},{4,5},{5,4},{6,7},{7,6},{8,9},{9,8},{10,11... | collective-permute-start | bytes 516104 | tf_op jit(solution)/shard_map/ppermute | solution.py:774
  (7 other events, 120.2 us)

commit v5 on v4

--- a/solution.py
+++ b/solution.py
@@ -182,23 +182,77 @@
     )(idx, w_out, w_fc1, w_fc2)
 
 
+def load_view(source, raw, view, sem):
+    load = pltpu.make_async_copy(source, raw, sem)
+    load.start()
+    load.wait()
+    view[...] = raw[...].astype(F32)
+
+
+def prepare_images_kernel(x_hbm, low_ref, hat_ref, rstd_ref, raw, view, xs, sem):
+    step = pl.program_id(0)
+    width = xs.shape[1]
+    seq = x_hbm.shape[0] * 128 // (width * 2 * pl.num_programs(0))
+
+    @pl.when(step == 0)
+    def _():
+        xs[...] = jnp.zeros_like(xs)
+        load_view(x_hbm, raw, view, sem)
+
+    for slot in range(2):
+        read_image(view, step, slot, seq, xs, slot * ROWS)
+    value = xs[...]
+    hat, rstd = normalize(value)
+    low_ref[...] = value.astype(BF16).reshape(2, ROWS, width)
+    hat_ref[...] = hat.reshape(2, ROWS, width)
+    rstd_ref[...] = jnp.broadcast_to(rstd, (2 * ROWS, 128)).reshape(2, ROWS, 128)
+
+
+def prepare_cotangent_kernel(x_hbm, low_ref, raw, view, xs, sem):
+    step = pl.program_id(0)
+    width = xs.shape[1]
+    seq = x_hbm.shape[0] * 128 // (width * 2 * pl.num_programs(0))
+
+    @pl.when(step == 0)
+    def _():
+        xs[...] = jnp.zeros_like(xs)
+        load_view(x_hbm, raw, view, sem)
+
+    for slot in range(2):
+        read_image(view, step, slot, seq, xs, slot * ROWS)
+    low_ref[...] = xs[...].astype(BF16).reshape(2, ROWS, width)
+
+
+def run_prepare(kernel, view, count, width, outs):
+    return pl.pallas_call(
+        kernel,
+        grid=(count // 2,),
+        in_specs=[HBM_SPEC],
+        out_specs=[per_pair(ROWS, columns) for columns, _ in outs],
+        out_shape=[pltpu.HBM((count, ROWS, columns), dtype) for columns, dtype in outs],
+        scratch_shapes=[
+            pltpu.VMEM(view.shape, BF16), pltpu.VMEM(view.shape, F32), pltpu.VMEM((2 * ROWS, width), F32),
+            pltpu.SemaphoreType.DMA,
+        ],
+        compiler_params=pltpu.CompilerParams(vmem_limit_bytes=14 << 20),
+        cost_estimate=pl.CostEstimate(flops=1 << 28, bytes_accessed=8 << 20, transcendentals=0),
+    )(*in_hbm(view))
+
+
 def attention_kernel(
-    idx_ref, x_ref, w_ref, near_ref, far_ref, small_ref,
-    qkv_ref, prob_ref, att_ref, hat_ref, rstd_ref, whole_ref, vec_ref, b1_ref,
-    raw, view, xs, kv, bias, scores, raw_sem,
+    seq, idx_ref, hat_hbm, w_ref, near_ref, far_ref, small_ref,
+    qkv_ref, prob_ref, att_ref, whole_ref, vec_ref, b1_ref,
+    kv, bias, scores, hat_buf, hat_sem,
 ):
     step = pl.program_id(0)
     half, wide = w_ref.shape
     width = wide // 3
     part = half // 2
     pairs = width // 128
-    seq = x_ref.shape[0] * 128 // (width * 2 * pl.num_programs(0))
+    (hat_ref,) = fetch([(hat_hbm, hat_buf)], hat_sem, 0, step, pl.num_programs(0))
 
     @pl.when(step == 0)
     def _():
-        load = pltpu.make_async_copy(x_ref, raw, raw_sem)
-        load.start()
-        xs[...] = jnp.zeros_like(xs)
         kv[...] = jnp.zeros_like(kv)
         group, core = idx_ref[0], idx_ref[1]
         first, second = ordered(idx_ref, small_ref[...], near_ref[part : part + 8, : small_ref.shape[1]])
@@ -216,14 +270,8 @@
                 lanes = slice(pair * 128, pair * 128 + 128)
                 piece = (first[0:1, lanes], jnp.zeros((1, 128), F32), second[0:1, lanes])[kind]
                 bias[0:1, target] = piece
-        load.wait()
-        view[...] = raw[...].astype(F32)
-
-    for slot in range(2):
-        read_image(view, step, slot, seq, xs, slot * ROWS)
-    hat, rstd = normalize(xs[...])
-    hat_ref[...] = hat.astype(BF16).reshape(2, ROWS, width)
-    rstd_ref[...] = jnp.broadcast_to(rstd, (2 * ROWS, 128)).reshape(2, ROWS, 128)
+
+    hat = hat_ref[...].reshape(2 * ROWS, width)
     normed = (hat * vec_ref[0:1, :] + vec_ref[1:2, :]).astype(BF16)
     low_half = lax.broadcasted_iota(jnp.int32, (1, 128), 1) < 64
     column = lax.broadcasted_iota(jnp.int32, (1, KEYS), 1)
@@ -275,26 +323,22 @@
 
 
 def mlp_kernel(
-    idx_ref, count_ref, x_ref, cot_ref, att_hbm, wo_ref, w1_ref, w2_ref, near_ref, far_ref, vec, b1,
+    idx_ref, count_ref, x_hbm, cot_hbm, att_hbm, wo_ref, w1_ref, w2_ref, near_ref, far_ref, vec, b1,
     act_ref, middle_ref, dx_ref, datt_ref, w2, keep_ref, send_ref,
-    view_x, view_c, xs, dys, acts, dpres, pres, dacts, wo, w1, wot, w1t, w2t, dn_half,
-    gw1, gw2, gwo, gsmall, att_buf, raw, att_sem, raw_sem,
+    acts, dpres, pres, dacts, wo, w1, wot, w1t, w2t, dn_half,
+    gw1, gw2, gwo, gsmall, x_buf, cot_buf, att_buf, sem,
 ):
     step = pl.program_id(0)
     last = pl.num_programs(0) - 1
     half, width = wo_ref.shape
     hidden = w1_ref.shape[1]
     part = half // 2
-    rows = xs.shape[0]
-    seq = x_ref.shape[0] * 128 // (width * 2 * pl.num_programs(0))
+    rows = 2 * ROWS
     core = idx_ref[1]
 
     @pl.when(step == 0)
     def _():
-        loads = [pltpu.make_async_copy(ref, raw.at[k], raw_sem.at[k]) for k, ref in enumerate((x_ref, cot_ref))]
-        for load in loads:
-            load.start()
-        for ref in (xs, dys, gw1, gw2, gwo, gsmall):
+        for ref in (gw1, gw2, gwo, gsmall):
             ref[...] = jnp.zeros_like(ref)
         group = idx_ref[0]
         wo[at(group * half, half), :] = wo_ref[...]
@@ -310,23 +354,19 @@
         wot[...] = wo[...].T
         w1t[...] = w1[...].T
         w2t[...] = w2[...].T
-        for load, target, k in zip(loads, (view_x, view_c), range(2)):
-            load.wait()
-            target[...] = raw[k].astype(F32)
-
-    (att_ref,) = fetch([(att_hbm, att_buf)], att_sem, 0, step, last + 1)
+
+    x_ref, cot_ref, att_ref = fetch(
+        [(x_hbm, x_buf), (cot_hbm, cot_buf), (att_hbm, att_buf)], sem, 0, step, last + 1
+    )
     second_valid = (1 < count_ref[step, 0]).astype(F32)
-    for slot in range(2):
-        read_image(view_x, step, slot, seq, xs, slot * ROWS)
-        read_image(view_c, step, slot, seq, dys, slot * ROWS)
     row = lax.broadcasted_iota(jnp.int32, (rows, 1), 0)
     valid = jnp.where(row < ROWS, 1.0, second_valid)
     att = att_ref[...].reshape(rows, width)
-    middle = xs[...] + mm(att, wo[...]) + vec[2:3, :]
+    middle = x_ref[...].reshape(rows, width).astype(F32) + mm(att, wo[...]) + vec[2:3, :]
     hat, rstd = normalize(middle)
     gain = vec[4:5, :]
     normed = (hat * gain + vec[5:6, :]).astype(BF16)
-    d_out = dys[...] * valid
+    d_out = cot_ref[...].reshape(rows, width).astype(F32) * valid
     d_mlp = d_out.astype(BF16)
     normed_t = jnp.concatenate([normed.T, jnp.ones((16, rows), BF16)], axis=0)
     d_mlp_t = d_mlp.T
@@ -445,7 +485,7 @@
             total_ref[...] = jnp.zeros_like(total_ref)
             sums_ref[...] = jnp.zeros_like(sums_ref)
 
-    hat_t[...] = hat_ref[...].reshape(2 * ROWS, width).T
+    hat_t[...] = hat_ref[...].reshape(2 * ROWS, width).astype(BF16).T
     for pair in range(pairs):
         kv[:, :ROWS, pair * 256 : pair * 256 + 256] = qkv_ref[:, :, pair * 384 + 128 : pair * 384 + 384]
     low_half = lax.broadcasted_iota(jnp.int32, (1, 128), 1) < 64
@@ -556,7 +596,7 @@
         wt[...] = w_ref[...].T
 
     d_normed = mm(dqkv_ref[...].reshape(rows, 3 * width), wt[...])
-    hat = hat_ref[...].reshape(rows, width).astype(F32)
+    hat = hat_ref[...].reshape(rows, width)
     rstd = rstd_ref[...].reshape(rows, 128)[:, 0:1]
     d_in = dx_ref[...].reshape(rows, width).astype(F32) + norm_back(d_normed, hat, rstd, vec_ref[0:1, :])
     for slot in range(2):
@@ -593,42 +633,39 @@
 SMEM_SPEC = pl.BlockSpec(memory_space=pltpu.SMEM)
 
 
-def run_attention(count, idx, view, w_qkv, near, far, small):
+def run_attention(seq, idx, hat, w_qkv, near, far, small):
+    count = hat.shape[0]
     width = w_qkv.shape[1] // 3
     return pl.pallas_call(
-        attention_kernel,
+        partial(attention_kernel, seq),
         grid=(count // 2,),
         in_specs=[SMEM_SPEC, HBM_SPEC] + [VMEM_SPEC] * 4,
         out_specs=[
             per_pair(ROWS, 3 * width), per_pair(HEADS, ROWS, KEYS), per_pair(ROWS, width),
-            per_pair(ROWS, width), per_pair(ROWS, 128), VMEM_SPEC, VMEM_SPEC, VMEM_SPEC,
+            VMEM_SPEC, VMEM_SPEC, VMEM_SPEC,
         ],
         out_shape=[
             pltpu.HBM((count, ROWS, 3 * width), BF16),
             pltpu.HBM((count, HEADS, ROWS, KEYS), BF16),
             pltpu.HBM((count, ROWS, width), BF16),
-            pltpu.HBM((count, ROWS, width), BF16),
-            pltpu.HBM((count, ROWS, 128), F32),
             jax.ShapeDtypeStruct((width, 3 * width), BF16),
             jax.ShapeDtypeStruct((8, width), F32),
             jax.ShapeDtypeStruct((8, 2 * small.shape[1]), F32),
         ],
         scratch_shapes=[
-            pltpu.VMEM(view.shape, BF16),
-            pltpu.VMEM(view.shape, F32),
-            pltpu.VMEM((2 * ROWS, width), F32),
             pltpu.VMEM((2, KEYS, 2 * width), BF16),
             pltpu.VMEM((8, 3 * width), F32),
             pltpu.VMEM((2, 2, ROWS, KEYS), F32),
-            pltpu.SemaphoreType.DMA,
+            pltpu.VMEM((2, 2, ROWS, width), F32),
+            pltpu.SemaphoreType.DMA((1, 2)),
         ],
         compiler_params=pltpu.CompilerParams(vmem_limit_bytes=22 << 20),
         cost_estimate=pl.CostEstimate(flops=5 << 30, bytes_accessed=20 << 20, transcendentals=0),
         name="attention_fwd",
-    )(idx, *in_hbm(view), w_qkv, near, far, small)
-
-
-def run_mlp(idx, counts, view, cot, att, wo, w1, w2, near, far, vec, b1):
+    )(idx, *in_hbm(hat), w_qkv, near, far, small)
+
+
+def run_mlp(idx, counts, images, cot, att, wo, w1, w2, near, far, vec, b1):
     width = wo.shape[1]
     hidden = w1.shape[1]
     micro = counts.shape[0]
@@ -650,10 +687,6 @@
             jax.ShapeDtypeStruct((2, 2, packed, width), BF16),
         ],
         scratch_shapes=[
-            pltpu.VMEM(view.shape, F32),
-            pltpu.VMEM(view.shape, F32),
-            pltpu.VMEM((rows, width), F32),
-            pltpu.VMEM((rows, width), F32),
             pltpu.VMEM((rows, hidden), BF16),
             pltpu.VMEM((rows, hidden), BF16),
             pltpu.VMEM((2, rows, 256), F32),
@@ -669,14 +702,14 @@
             pltpu.VMEM((width, width), F32),
             pltpu.VMEM((4, 8, width), F32),
             pltpu.VMEM((2, 2, ROWS, width), BF16),
-            pltpu.VMEM((2, *view.shape), BF16),
-            pltpu.SemaphoreType.DMA((1, 2)),
-            pltpu.SemaphoreType.DMA((2,)),
+            pltpu.VMEM((2, 2, ROWS, width), BF16),
+            pltpu.VMEM((2, 2, ROWS, width), BF16),
+            pltpu.SemaphoreType.DMA((3, 2)),
         ],
         compiler_params=pltpu.CompilerParams(vmem_limit_bytes=40 << 20),
         cost_estimate=pl.CostEstimate(flops=12 << 30, bytes_accessed=20 << 20, transcendentals=0),
         name="mlp_fwd_bwd",
-    )(idx, counts, *in_hbm(view, cot, att), wo, w1, w2, near, far, vec, b1)
+    )(idx, counts, *in_hbm(images, cot, att), wo, w1, w2, near, far, vec, b1)
 
 
 def run_attention_back(begin, end, idx, hat, qkv, prob, att, datt, w_qkv, vec, carried):
@@ -703,7 +736,8 @@
             pltpu.VMEM((width, 2 * ROWS), BF16),
             pltpu.VMEM((2, 2, ROWS, KEYS), F32),
             pltpu.VMEM((2, 4, ROWS, KEYS), BF16),
-            two(ROWS, width), two(ROWS, width), two(ROWS, 3 * width), two(ROWS, width), two(HEADS, ROWS, KEYS),
+            pltpu.VMEM((2, 2, ROWS, width), F32),
+            two(ROWS, width), two(ROWS, 3 * width), two(ROWS, width), two(HEADS, ROWS, KEYS),
             pltpu.SemaphoreType.DMA((5, 2)),
         ],
         input_output_aliases={8: 0, 9: 1, 10: 2} if carried else {},
@@ -725,7 +759,7 @@
         scratch_shapes=[
             pltpu.VMEM(view_shape, F32),
             pltpu.VMEM((3 * width, width), BF16),
-            two(BF16, ROWS, width), two(F32, ROWS, 128), two(BF16, ROWS, 3 * width), two(BF16, ROWS, width),
+            two(F32, ROWS, width), two(F32, ROWS, 128), two(BF16, ROWS, 3 * width), two(BF16, ROWS, width),
             pltpu.SemaphoreType.DMA((4, 2)),
         ],
         compiler_params=pltpu.CompilerParams(vmem_limit_bytes=14 << 20),
@@ -903,6 +937,7 @@
     replica = lax.axis_index("replica")
     idx = jnp.stack([lax.axis_index("group"), replica & 1, (replica >> 1) & 1, (replica >> 2) & 1]).astype(jnp.int32)
     count = images.shape[0] * images.shape[1]
+    width = images.shape[3]
     vectors = (b_qv, b_out, b_fc1, b_fc2, gain_one, shift_one, gain_two, shift_two)
     first, small = run_pack_first(idx, w_qkv, vectors)
     second = run_pack_second(idx, w_out, w_fc1, w_fc2)
@@ -911,10 +946,15 @@
     far_first = flip(near_first, "replica", replicas, 1)
     far_second = flip(near_second, "replica", replicas, 1)
     view = interleaved(images)
-    qkv, prob, att, hat, rstd, w_all, vec, b1 = run_attention(count, idx, view, w_qkv, near_first, far_first, small)
+    image_rows, hat, rstd = run_prepare(
+        prepare_images_kernel, view, count, width, ((width, BF16), (width, F32), (128, F32))
+    )
+    (cot_rows,) = run_prepare(prepare_cotangent_kernel, interleaved(cotangent), count, width, ((width, BF16),))
+    qkv, prob, att, w_all, vec, b1 = run_attention(
+        images.shape[2], idx, hat, w_qkv, near_first, far_first, small
+    )
     act, middle, dx, datt, w_two, keep_b, send_b = run_mlp(
-        idx, image_count, view, interleaved(cotangent), att, w_out, w_fc1, w_fc2,
-        near_second, far_second, vec, b1,
+        idx, image_count, image_rows, cot_rows, att, w_out, w_fc1, w_fc2, near_second, far_second, vec, b1
     )
     carried = ()
     for begin, end in SPLITS:

time: 152 us -> 157 us (1.033)
  Pallas kernels: 86 us -> 92.4 us
    pallas_call x1 -> x3, Pallas kernels: 12.2 us -> 18.7 us  [the longest x1 11.3 us: run_attention(): pl.pallas_call(partial(attention_kernel, seq), grid=(count // 2,), in_spe...]
  transfers between devices with their start and end apart: 24 -> 24, of which waited for: 8 -> 7; matrix products, arithmetic and copies ran while one was open for 0% -> 0% of each run, Pallas kernels for 35% -> 38%
where the time goes in v5:
time: 157 us
  Pallas kernels  92.4 us (59%)
  waiting for transfers between devices  33.2 us (21%)
  starting transfers between devices  29.1 us (19%)
    ppermute x24, waiting for transfers between devices, flip(): return lax.ppermute(value, axis, [(i, i ^ bit) for i in range(size)])  33.2 us
    ppermute x24, starting transfers between devices, flip(): return lax.ppermute(value, axis, [(i, i ^ bit) for i in range(size)])  29.1 us
    pallas_call x1, Pallas kernels, run_mlp(): pl.pallas_call(mlp_kernel, grid=(micro,), in_specs=[SMEM_SPEC, SMEM_SPEC,...  26.9 us
    pallas_call x2, Pallas kernels, run_attention_back(): pl.pallas_call(partial(attention_back_kernel, begin, last), grid=(end - b...  19.9 us
    pallas_call x1, Pallas kernels, run_attention(): pl.pallas_call(partial(attention_kernel, seq), grid=(count // 2,), in_spe...  11.3 us
    pallas_call x2, Pallas kernels, run_prepare(): pl.pallas_call(kernel, grid=(count // 2,), in_specs=[HBM_SPEC], out_specs...  7.39 us
    pallas_call x1, Pallas kernels, run_outputs(): pl.pallas_call(outputs_kernel, grid=(count // 2,), in_specs=[SMEM_SPEC] +...  7.39 us
    pallas_call x1, Pallas kernels, run_input_grad(): pl.pallas_call(input_grad_kernel, grid=(count // 2,), in_specs=[HBM_SPEC]...  7.3 us
  transfers between devices with their start and end apart: 24, of which 7 were waited for; matrix products, arithmetic and copies ran while one was open for 0% of the time, Pallas kernels for 38%

profile of v5, /device:TPU:1, one launch (start us, length us, event | category | flops | bytes accessed | tf_op | source)
XLA Modules:
  0.0 156.5 jit_solution(12841732177900003337)
XLA Ops:
  1.3 2.6 %pack_second.1 = bf16[96,3456]{1,0:T(8,128)(2,1)} custom-call(s32[4]{0:T(128)} %pad_add_fusion.idx_ref, bf16[192,384]{1,0:T(8,128)(2,1)} %wo_ref.3, bf16[192,1536]{1,0:T(8,128)(2,1)} %w1_ref.3, bf16[768,384]{1,0:T(8,128)(2,1)} %w2_ref.3), custom_call_target="tpu_custom_call" | custom-call | tf_op jit(solution)/shard_map/pack_second/pallas_call | solution.py:172
  3.9 2.0 %collective-permute-start.2 = (bf16[96,3456]{1,0:T(8,128)(2,1)}, bf16[96,3456]{1,0:T(8,128)(2,1)S(1)}, u32[]{:S(2)}, u32[]{:S(2)}) collective-permute-start(bf16[96,3456]{1,0:T(8,128)(2,1)} %pack_second.1), channel_id=1, source_target_pairs={{0,16},{16,0},{1,17},{17,1},{2,18},{18,2},{3,19},{19,3},{4,20},{20... | collective-permute-start | bytes 1990664 | tf_op jit(solution)/shard_map/ppermute | solution.py:808
  5.9 2.4 %pack_first.1 = (bf16[112,1152]{1,0:T(8,128)(2,1)}, bf16[8,768]{1,0:T(8,128)(2,1)}) custom-call(s32[4]{0:T(128)} %pad_add_fusion.idx_ref, bf16[192,1152]{1,0:T(8,128)(2,1)} %w_ref.1, bf16[384]{0:T(512)(128)(2,1)} %refs_0_.1, bf16[192]{0:T(256)(128)(2,1)} %refs_1_.1, bf16[768]{0:T(1024)(128)(2,1)} %refs_2_.1, bf16[192]{0:T(256)(128)(2,1)} %refs_3_.1, ...), custom_call_target="tpu_custom_call" | custom-call | tf_op jit(solution)/shard_map/pack_first/pallas_call | solution.py:154
  8.4 17.9 %collective-permute-done.near_ref = bf16[112,1152]{1,0:T(8,128)(2,1)S(1)} collective-permute-done((bf16[112,1152]{1,0:T(8,128)(2,1)}, bf16[112,1152]{1,0:T(8,128)(2,1)S(1)}, u32[]{:S(2)}, u32[]{:S(2)}) %collective-permute-start) | collective-permute-done | bytes 258080 | tf_op jit(solution)/shard_map/ppermute | solution.py:808
  27.6 3.2 %shard_map.255.cot_hbm = bf16[8,208,384]{2,1,0:T(8,128)(2,1)} custom-call(bf16[4728,128]{1,0:T(8,128)(2,1)} %bitcast.33), custom_call_target="tpu_custom_call" | custom-call | flops 268435456 | bytes 8388608 | tf_op jit(solution)/shard_map/pallas_call | solution.py:227
  30.8 4.2 %shard_map.254 = (bf16[8,208,384]{2,1,0:T(8,128)(2,1)}, f32[8,208,384]{2,1,0:T(8,128)}, f32[8,208,128]{2,1,0:T(8,128)}) custom-call(bf16[4728,128]{1,0:T(8,128)(2,1)} %bitcast.32), custom_call_target="tpu_custom_call" | custom-call | flops 268435456 | bytes 8388608 | tf_op jit(solution)/shard_map/pallas_call | solution.py:227
  35.1 11.3 %attention_fwd.1 = (bf16[8,208,1152]{2,1,0:T(8,128)(2,1)}, bf16[8,6,208,256]{3,2,1,0:T(8,128)(2,1)}, bf16[8,208,384]{2,1,0:T(8,128)(2,1)}, bf16[384,1152]{1,0:T(...) custom-call(s32[4]{0:T(128)S(1)} %copy-done.4, f32[8,208,384]{2,1,0:T(8,128)} %get-tuple-element.61.hat_hbm, ...), custom_call_target="tpu_custom_call" | custom-call | flops 5368709120 | bytes 20971520 | tf_op jit(solution)/shard_map/attention_fwd/pallas_call | solution.py:639
  46.4 26.9 %mlp_fwd_bwd.1 = (bf16[8,208,1536]{2,1,0:T(8,128)(2,1)}, f32[8,208,384]{2,1,0:T(8,128)}, bf16[8,208,384]{2,1,0:T(8,128)(2,1)}, bf16[8,208,384]{2,1,0:T(8,128)(2,...) custom-call(s32[4]{0:T(128)S(1)} %copy-done.4, ...), custom_call_target="tpu_custom_call" | custom-call | flops 12884901888 | bytes 20971520 | tf_op jit(solution)/shard_map/mlp_fwd_bwd/pallas_call | solution.py:675
  73.9 6.3 %shard_map.256 = (bf16[8,208,1152]{2,1,0:T(8,128)(2,1)}, f32[384,1152]{1,0:T(8,128)S(1)}, f32[8,1152]{1,0:T(8,128)S(1)}) custom-call(s32[4]{0:T(128)S(1)} %copy-done.4, f32[8,208,384]{2,1,0:T(8,128)} %get-tuple-element.61.hat_hbm, bf16[8,208,1152]{2,1,0:T(8,128)(2,1)} %get-tuple-element.71.qkv_hbm, bf16[8,6,208,256]{3,2,1,0:T(8,128)(2,1)} %get-tuple-element.72.prob_hbm, ...), custom_call_target="tpu_custom_call" | custom-call | flops 2147483648 | bytes 20971520 | tf_op jit(solution)/shard_map/pallas_call | solution.py:722
  81.0 1.5 collective-permute-start.13
  82.5 13.6 %shard_map.257 = (bf16[8,208,1152]{2,1,0:T(8,128)(2,1)}, f32[384,1152]{1,0:T(8,128)S(1)}, f32[8,1152]{1,0:T(8,128)S(1)}, bf16[2,2,160,384]{3,2,1,0:T(8,128)(2,1)S(1)}, bf16[2,2,160,384]{3,2,1,0:T(8,128)(2,1)S(1)}) custom-call(s32[4]{0:T(128)S(1)} %copy-done.4, ...), custom_call_target="tpu_custom_call", output_to_operand_aliasing={{0}: (8, {}), {1}: (9, {}), {2}: (10, {})} | custom-call | flops 6442450944 | bytes 20971520 | tf_op jit(solution)/shard_map/pallas_call | solution.py:722
  98.7 1.6 collective-permute-start.14
  102.1 5.4 %collective-permute-done.14 = bf16[448,384]{1,0:T(8,128)(2,1)S(1)} collective-permute-done((bf16[448,384]{1,0:T(8,128)(2,1)S(1)}, bf16[448,384]{1,0:T(8,128)(2,1)S(1)}, u32[]{:S(2)}, u32[]{:S(2)}) %collective-permute-start.14) | collective-permute-done | bytes 344096 | tf_op jit(solution)/shard_map/ppermute | solution.py:808
  108.2 1.6 collective-permute-start.15
  112.6 2.5 %collective-permute-start.16 = (bf16[224,384]{1,0:T(8,128)(2,1)S(1)}, bf16[224,384]{1,0:T(8,128)(2,1)S(1)}, u32[]{:S(2)}, u32[]{:S(2)}) collective-permute-start(bf16[224,384]{1,0:T(8,128)(2,1)S(1)} %add.18), channel_id=1, source_target_pairs={{0,8},{1,9},{2,10},{3,11},{4,12},{5,13},{6,14},{7,15},{8,0},{9,1},... | collective-permute-start | bytes 516104 | tf_op jit(solution)/shard_map/ppermute | solution.py:808
  116.5 4.0 %collective-permute-done.16 = bf16[224,384]{1,0:T(8,128)(2,1)S(1)} collective-permute-done((bf16[224,384]{1,0:T(8,128)(2,1)S(1)}, bf16[224,384]{1,0:T(8,128)(2,1)S(1)}, u32[]{:S(2)}, u32[]{:S(2)}) %collective-permute-start.16) | collective-permute-done | bytes 172064 | tf_op jit(solution)/shard_map/ppermute | solution.py:808
  120.6 1.9 %collective-permute-start.17 = (bf16[224,384]{1,0:T(8,128)(2,1)S(1)}, bf16[224,384]{1,0:T(8,128)(2,1)S(1)}, u32[]{:S(2)}, u32[]{:S(2)}) collective-permute-start(bf16[224,384]{1,0:T(8,128)(2,1)S(1)} %add.19.refs_0_), channel_id=1, source_target_pairs={{0,4},{1,5},{2,6},{3,7},{4,0},{5,1},{6,2},{7,3},{8,12},{9,13},{10,... | collective-permute-start | bytes 516104 | tf_op jit(solution)/shard_map/ppermute | solution.py:808
  122.6 3.3 %collective-permute-start.8 = (bf16[160,384]{1,0:T(8,128)(2,1)S(1)}, bf16[160,384]{1,0:T(8,128)(2,1)S(1)}, u32[]{:S(2)}, u32[]{:S(2)}) collective-permute-start(bf16[160,384]{1,0:T(8,128)(2,1)S(1)} %add.16), channel_id=1, source_target_pairs={{0,8},{1,9},{2,10},{3,11},{4,12},{5,13},{6,14},{7,15},{8,0},{9,1},... | collective-permute-start | bytes 368648 | tf_op jit(solution)/shard_map/ppermute | solution.py:808
  125.9 2.9 %collective-permute-done.8 = bf16[160,384]{1,0:T(8,128)(2,1)S(1)} collective-permute-done((bf16[160,384]{1,0:T(8,128)(2,1)S(1)}, bf16[160,384]{1,0:T(8,128)(2,1)S(1)}, u32[]{:S(2)}, u32[]{:S(2)}) %collective-permute-start.8) | collective-permute-done | bytes 122912 | tf_op jit(solution)/shard_map/ppermute | solution.py:808
  128.8 3.3 %collective-permute-start.10 = (bf16[160,384]{1,0:T(8,128)(2,1)S(1)}, bf16[160,384]{1,0:T(8,128)(2,1)S(1)}, u32[]{:S(2)}, u32[]{:S(2)}) collective-permute-start(bf16[160,384]{1,0:T(8,128)(2,1)S(1)} %add.17.refs_0_), channel_id=1, source_target_pairs={{0,1},{1,0},{2,3},{3,2},{4,5},{5,4},{6,7},{7,6},{8,9},{9,8},{10,11... | collective-permute-start | bytes 368648 | tf_op jit(solution)/shard_map/ppermute | solution.py:808
  134.8 7.4 %layer_outputs.1 = bf16[4728,128]{1,0:T(8,128)(2,1)} custom-call(s32[4,1]{1,0:T(4,128)S(1)} %copy.33.count_ref, bf16[8,208,1536]{2,1,0:T(8,128)(2,1)} %get-tuple-element.67.act_hbm, f32[8,208,384]{2,1,0:T(8,128)} %get-tuple-element.68.middle_hbm, bf16[1536,384]{1,0:T(8,128)(2,1)S(1)} %get-tuple-element.69.w2_ref, f32[8,384]{1,0:T(8,128)S(1)} %get-tuple-element.65.vec.vec_ref), custom_call_target="tpu_custom_call" | custom-call | flops 2147483648 | bytes 20971520 | tf_op jit(solution)/shard_map/layer_outputs/pallas_call | solution.py:774
  145.2 7.3 %input_grad.1 = bf16[4728,128]{1,0:T(8,128)(2,1)} custom-call(f32[8,208,384]{2,1,0:T(8,128)} %get-tuple-element.61.hat_hbm, f32[8,208,128]{2,1,0:T(8,128)} %get-tuple-element.70.rstd_hbm, bf16[8,208,1152]{2,1,0:T(8,128)(2,1)} %get-tuple-element.78.dqkv_hbm, bf16[8,208,384]{2,1,0:T(8,128)(2,1)} %get-tuple-element.79.dx_hbm, ...), custom_call_target="tpu_custom_call" | custom-call | flops 2147483648 | bytes 20971520 | tf_op jit(solution)/shard_map/input_grad/pallas_call | solution.py:753
  152.5 1.6 %shard_map.260 = (f32[192,1152]{1,0:T(8,128)}, f32[384]{0:T(512)}, f32[192]{0:T(256)}, f32[192]{0:T(256)}) custom-call(s32[4]{0:T(128)S(1)} %copy-done.4, bf16[160,384]{1,0:T(8,128)(2,1)S(1)} %add.17.refs_0_, bf16[160,384]{1,0:T(8,128)(2,1)S(1)} %collective-permute-done.9.refs_1_, bf16[160,384]{1,0:T(8,128)(2,1)S(1)} %collective-permute-done.10.refs_2_, ...), custom_call_target="tpu_custom_call" | custom-call | tf_op jit(solution)/shard_map/pallas_call | solution.py:906
  154.1 2.4 %shard_map.264 = (f32[192,384]{1,0:T(8,128)}, f32[192]{0:T(256)}, f32[192,1536]{1,0:T(8,128)}, f32[768]{0:T(1024)}, f32[768,384]{1,0:T(8,128)}, /*index=5*/f32[192]{0:T(256)}, f32[192]{0:T(256)}, f32[192]{0:T(256)}) custom-call(s32[4]{0:T(128)S(1)} %copy-done.4, bf16[224,384]{1,0:T(8,128)(2,1)S(1)} %add.19.refs_0_, ...), custom_call_target="tpu_custom_call" | custom-call | tf_op jit(solution)/shard_map/pallas_call | solution.py:906
  (62 shorter events, 18.4 us)
Async XLA Ops:
  3.9 23.6 %collective-permute-start.2 = (bf16[96,3456]{1,0:T(8,128)(2,1)}, bf16[96,3456]{1,0:T(8,128)(2,1)S(1)}, u32[]{:S(2)}, u32[]{:S(2)}) collective-permute-start(bf16[96,3456]{1,0:T(8,128)(2,1)} %pack_second.1), channel_id=1, source_target_pairs={{0,16},{16,0},{1,17},{17,1},{2,18},{18,2},{3,19},{19,3},{4,20},{20... | collective-permute-start | bytes 1990664 | tf_op jit(solution)/shard_map/ppermute | solution.py:808
  8.4 17.9 %collective-permute-start = (bf16[112,1152]{1,0:T(8,128)(2,1)}, bf16[112,1152]{1,0:T(8,128)(2,1)S(1)}, u32[]{:S(2)}, u32[]{:S(2)}) collective-permute-start(bf16[112,1152]{1,0:T(8,128)(2,1)} %get-tuple-element.62), channel_id=1, source_target_pairs={{0,16},{16,0},{1,17},{17,1},{2,18},{18,2},{3,19},{19,3},{4,20},{20... | collective-permute-start | bytes 774152 | tf_op jit(solution)/shard_map/ppermute | solution.py:808
  26.3 8.8 %collective-permute-start.1 = (bf16[112,1152]{1,0:T(8,128)(2,1)S(1)}, bf16[112,1152]{1,0:T(8,128)(2,1)S(1)}, u32[]{:S(2)}, u32[]{:S(2)}) collective-permute-start(bf16[112,1152]{1,0:T(8,128)(2,1)S(1)} %collective-permute-done.near_ref), channel_id=1, source_target_pairs={{0,1},{1,0},{2,3},{3,2},{4,5},{5,4},{6,7},{7,6},{8,9},{9,8},{10,11... | collective-permute-start | bytes 774152 | tf_op jit(solution)/shard_map/ppermute | solution.py:808
  27.5 18.9 %collective-permute-start.3 = (bf16[96,3456]{1,0:T(8,128)(2,1)S(1)}, bf16[96,3456]{1,0:T(8,128)(2,1)S(1)}, u32[]{:S(2)}, u32[]{:S(2)}) collective-permute-start(bf16[96,3456]{1,0:T(8,128)(2,1)S(1)} %collective-permute-done.2.near_ref), channel_id=1, source_target_pairs={{0,1},{1,0},{2,3},{3,2},{4,5},{5,4},{6,7},{7,6},{8,9},{9,8},{10,11... | collective-permute-start | bytes 1990664 | tf_op jit(solution)/shard_map/ppermute | solution.py:808
  73.3 6.8 %collective-permute-start.12 = (bf16[2,2,448,384]{3,2,1,0:T(8,128)(2,1)S(1)}, bf16[2,2,448,384]{3,2,1,0:T(8,128)(2,1)S(1)}, u32[]{:S(2)}, u32[]{:S(2)}) collective-permute-start(bf16[2,2,448,384]{3,2,1,0:T(8,128)(2,1)S(1)} %get-tuple-element.89), channel_id=1, source_target_pairs={{0,1},{1,0},{2,3},{3,2},{4,5},{5,4},{6,7},{7,6},{8,9},{9,8},{10,11... | collective-permute-start | bytes 4128776 | tf_op jit(solution)/shard_map/ppermute | solution.py:808
  81.0 17.0 %collective-permute-start.13 = (bf16[2,448,384]{2,1,0:T(8,128)(2,1)S(1)}, bf16[2,448,384]{2,1,0:T(8,128)(2,1)S(1)}, u32[]{:S(2)}, u32[]{:S(2)}) collective-permute-start(bf16[2,448,384]{2,1,0:T(8,128)(2,1)S(1)} %get-tuple-element.91), channel_id=1, source_target_pairs={{0,16},{16,0},{1,17},{17,1},{2,18},{18,2},{3,19},{19,3},{4,20},{20... | collective-permute-start | bytes 2064392 | tf_op jit(solution)/shard_map/ppermute | solution.py:808
  96.2 4.1 %collective-permute-start.4 = (bf16[2,2,160,384]{3,2,1,0:T(8,128)(2,1)S(1)}, bf16[2,2,160,384]{3,2,1,0:T(8,128)(2,1)S(1)}, u32[]{:S(2)}, u32[]{:S(2)}) collective-permute-start(bf16[2,2,160,384]{3,2,1,0:T(8,128)(2,1)S(1)} %get-tuple-element.81), channel_id=1, source_target_pairs={{0,1},{1,0},{2,3},{3,2},{4,5},{5,4},{6,7},{7,6},{8,9},{9,8},{10,11... | collective-permute-start | bytes 1474568 | tf_op jit(solution)/shard_map/ppermute | solution.py:808
  98.7 8.9 %collective-permute-start.14 = (bf16[448,384]{1,0:T(8,128)(2,1)S(1)}, bf16[448,384]{1,0:T(8,128)(2,1)S(1)}, u32[]{:S(2)}, u32[]{:S(2)}) collective-permute-start(bf16[448,384]{1,0:T(8,128)(2,1)S(1)} %get-tuple-element.93), channel_id=1, source_target_pairs={{0,2},{1,3},{2,0},{3,1},{4,6},{5,7},{6,4},{7,5},{8,10},{9,11},{10,... | collective-permute-start | bytes 1032200 | tf_op jit(solution)/shard_map/ppermute | solution.py:808
  100.9 8.9 %collective-permute-start.5 = (bf16[2,160,384]{2,1,0:T(8,128)(2,1)S(1)}, bf16[2,160,384]{2,1,0:T(8,128)(2,1)S(1)}, u32[]{:S(2)}, u32[]{:S(2)}) collective-permute-start(bf16[2,160,384]{2,1,0:T(8,128)(2,1)S(1)} %get-tuple-element.83), channel_id=1, source_target_pairs={{0,16},{16,0},{1,17},{17,1},{2,18},{18,2},{3,19},{19,3},{4,20},{20... | collective-permute-start | bytes 737288 | tf_op jit(solution)/shard_map/ppermute | solution.py:808
  108.2 4.4 %collective-permute-start.15 = (bf16[224,384]{1,0:T(8,128)(2,1)S(1)}, bf16[224,384]{1,0:T(8,128)(2,1)S(1)}, u32[]{:S(2)}, u32[]{:S(2)}) collective-permute-start(bf16[224,384]{1,0:T(8,128)(2,1)S(1)} %get-tuple-element.95), channel_id=1, source_target_pairs={{0,4},{1,5},{2,6},{3,7},{4,0},{5,1},{6,2},{7,3},{8,12},{9,13},{10,... | collective-permute-start | bytes 516104 | tf_op jit(solution)/shard_map/ppermute | solution.py:808
  110.3 4.8 %collective-permute-start.6 = (bf16[160,384]{1,0:T(8,128)(2,1)S(1)}, bf16[160,384]{1,0:T(8,128)(2,1)S(1)}, u32[]{:S(2)}, u32[]{:S(2)}) collective-permute-start(bf16[160,384]{1,0:T(8,128)(2,1)S(1)} %get-tuple-element.85), channel_id=1, source_target_pairs={{0,2},{1,3},{2,0},{3,1},{4,6},{5,7},{6,4},{7,5},{8,10},{9,11},{10,... | collective-permute-start | bytes 368648 | tf_op jit(solution)/shard_map/ppermute | solution.py:808
  112.6 8.0 %collective-permute-start.16 = (bf16[224,384]{1,0:T(8,128)(2,1)S(1)}, bf16[224,384]{1,0:T(8,128)(2,1)S(1)}, u32[]{:S(2)}, u32[]{:S(2)}) collective-permute-start(bf16[224,384]{1,0:T(8,128)(2,1)S(1)} %add.18), channel_id=1, source_target_pairs={{0,8},{1,9},{2,10},{3,11},{4,12},{5,13},{6,14},{7,15},{8,0},{9,1},... | collective-permute-start | bytes 516104 | tf_op jit(solution)/shard_map/ppermute | solution.py:808
  115.1 7.4 %collective-permute-start.7 = (bf16[160,384]{1,0:T(8,128)(2,1)S(1)}, bf16[160,384]{1,0:T(8,128)(2,1)S(1)}, u32[]{:S(2)}, u32[]{:S(2)}) collective-permute-start(bf16[160,384]{1,0:T(8,128)(2,1)S(1)} %add.15), channel_id=1, source_target_pairs={{0,4},{1,5},{2,6},{3,7},{4,0},{5,1},{6,2},{7,3},{8,12},{9,13},{10,... | collective-permute-start | bytes 368648 | tf_op jit(solution)/shard_map/ppermute | solution.py:808
  120.6 13.0 %collective-permute-start.17 = (bf16[224,384]{1,0:T(8,128)(2,1)S(1)}, bf16[224,384]{1,0:T(8,128)(2,1)S(1)}, u32[]{:S(2)}, u32[]{:S(2)}) collective-permute-start(bf16[224,384]{1,0:T(8,128)(2,1)S(1)} %add.19.refs_0_), channel_id=1, source_target_pairs={{0,4},{1,5},{2,6},{3,7},{4,0},{5,1},{6,2},{7,3},{8,12},{9,13},{10,... | collective-permute-start | bytes 516104 | tf_op jit(solution)/shard_map/ppermute | solution.py:808
  122.6 6.2 %collective-permute-start.8 = (bf16[160,384]{1,0:T(8,128)(2,1)S(1)}, bf16[160,384]{1,0:T(8,128)(2,1)S(1)}, u32[]{:S(2)}, u32[]{:S(2)}) collective-permute-start(bf16[160,384]{1,0:T(8,128)(2,1)S(1)} %add.16), channel_id=1, source_target_pairs={{0,8},{1,9},{2,10},{3,11},{4,12},{5,13},{6,14},{7,15},{8,0},{9,1},... | collective-permute-start | bytes 368648 | tf_op jit(solution)/shard_map/ppermute | solution.py:808
  128.8 14.5 %collective-permute-start.10 = (bf16[160,384]{1,0:T(8,128)(2,1)S(1)}, bf16[160,384]{1,0:T(8,128)(2,1)S(1)}, u32[]{:S(2)}, u32[]{:S(2)}) collective-permute-start(bf16[160,384]{1,0:T(8,128)(2,1)S(1)} %add.17.refs_0_), channel_id=1, source_target_pairs={{0,1},{1,0},{2,3},{3,2},{4,5},{5,4},{6,7},{7,6},{8,9},{9,8},{10,11... | collective-permute-start | bytes 368648 | tf_op jit(solution)/shard_map/ppermute | solution.py:808
  132.1 10.1 %collective-permute-start.9 = (bf16[160,384]{1,0:T(8,128)(2,1)S(1)}, bf16[160,384]{1,0:T(8,128)(2,1)S(1)}, u32[]{:S(2)}, u32[]{:S(2)}) collective-permute-start(bf16[160,384]{1,0:T(8,128)(2,1)S(1)} %add.17.refs_0_), channel_id=1, source_target_pairs={{0,2},{1,3},{2,0},{3,1},{4,6},{5,7},{6,4},{7,5},{8,10},{9,11},{10,... | collective-permute-start | bytes 368648 | tf_op jit(solution)/shard_map/ppermute | solution.py:808
  133.4 10.4 %collective-permute-start.18 = (bf16[224,384]{1,0:T(8,128)(2,1)S(1)}, bf16[224,384]{1,0:T(8,128)(2,1)S(1)}, u32[]{:S(2)}, u32[]{:S(2)}) collective-permute-start(bf16[224,384]{1,0:T(8,128)(2,1)S(1)} %add.19.refs_0_), channel_id=1, source_target_pairs={{0,2},{1,3},{2,0},{3,1},{4,6},{5,7},{6,4},{7,5},{8,10},{9,11},{10,... | collective-permute-start | bytes 516104 | tf_op jit(solution)/shard_map/ppermute | solution.py:808
  133.6 10.7 %collective-permute-start.19 = (bf16[224,384]{1,0:T(8,128)(2,1)S(1)}, bf16[224,384]{1,0:T(8,128)(2,1)S(1)}, u32[]{:S(2)}, u32[]{:S(2)}) collective-permute-start(bf16[224,384]{1,0:T(8,128)(2,1)S(1)} %collective-permute-done.17.refs_1_), channel_id=1, source_target_pairs={{0,2},{1,3},{2,0},{3,1},{4,6},{5,7},{6,4},{7,5},{8,10},{9,11},{10,... | collective-permute-start | bytes 516104 | tf_op jit(solution)/shard_map/ppermute | solution.py:808
  142.2 10.3 %collective-permute-start.11 = (bf16[160,384]{1,0:T(8,128)(2,1)S(1)}, bf16[160,384]{1,0:T(8,128)(2,1)S(1)}, u32[]{:S(2)}, u32[]{:S(2)}) collective-permute-start(bf16[160,384]{1,0:T(8,128)(2,1)S(1)} %collective-permute-done.9.refs_1_), channel_id=1, source_target_pairs={{0,1},{1,0},{2,3},{3,2},{4,5},{5,4},{6,7},{7,6},{8,9},{9,8},{10,11... | collective-permute-start | bytes 368648 | tf_op jit(solution)/shard_map/ppermute | solution.py:808
  143.2 10.9 %collective-permute-start.20 = (bf16[224,384]{1,0:T(8,128)(2,1)S(1)}, bf16[224,384]{1,0:T(8,128)(2,1)S(1)}, u32[]{:S(2)}, u32[]{:S(2)}) collective-permute-start(bf16[224,384]{1,0:T(8,128)(2,1)S(1)} %add.19.refs_0_), channel_id=1, source_target_pairs={{0,1},{1,0},{2,3},{3,2},{4,5},{5,4},{6,7},{7,6},{8,9},{9,8},{10,11... | collective-permute-start | bytes 516104 | tf_op jit(solution)/shard_map/ppermute | solution.py:808
  143.3 10.8 %collective-permute-start.21 = (bf16[224,384]{1,0:T(8,128)(2,1)S(1)}, bf16[224,384]{1,0:T(8,128)(2,1)S(1)}, u32[]{:S(2)}, u32[]{:S(2)}) collective-permute-start(bf16[224,384]{1,0:T(8,128)(2,1)S(1)} %collective-permute-done.17.refs_1_), channel_id=1, source_target_pairs={{0,1},{1,0},{2,3},{3,2},{4,5},{5,4},{6,7},{7,6},{8,9},{9,8},{10,11... | collective-permute-start | bytes 516104 | tf_op jit(solution)/shard_map/ppermute | solution.py:808
  143.7 10.4 %collective-permute-start.22 = (bf16[224,384]{1,0:T(8,128)(2,1)S(1)}, bf16[224,384]{1,0:T(8,128)(2,1)S(1)}, u32[]{:S(2)}, u32[]{:S(2)}) collective-permute-start(bf16[224,384]{1,0:T(8,128)(2,1)S(1)} %collective-permute-done.18.refs_2_), channel_id=1, source_target_pairs={{0,1},{1,0},{2,3},{3,2},{4,5},{5,4},{6,7},{7,6},{8,9},{9,8},{10,11... | collective-permute-start | bytes 516104 | tf_op jit(solution)/shard_map/ppermute | solution.py:808
  144.3 9.9 %collective-permute-start.23 = (bf16[224,384]{1,0:T(8,128)(2,1)S(1)}, bf16[224,384]{1,0:T(8,128)(2,1)S(1)}, u32[]{:S(2)}, u32[]{:S(2)}) collective-permute-start(bf16[224,384]{1,0:T(8,128)(2,1)S(1)} %collective-permute-done.19.refs_3_), channel_id=1, source_target_pairs={{0,1},{1,0},{2,3},{3,2},{4,5},{5,4},{6,7},{7,6},{8,9},{9,8},{10,11... | collective-permute-start | bytes 516104 | tf_op jit(solution)/shard_map/ppermute | solution.py:808
  (7 other events, 83.1 us)

commit v6 on v5

--- a/solution.py
+++ b/solution.py
@@ -157,11 +157,12 @@
             num_scalar_prefetch=1,
             grid=(1,),
             in_specs=[own_rows(half // 2, wide)] + [pl.BlockSpec(v.shape, lambda i, idx: (0,)) for v in vectors],
-            out_specs=[pl.BlockSpec(s, lambda i, idx: (0, 0)) for s in shapes],
+            out_specs=[VMEM_SPEC] * 2,
         ),
         out_shape=[jax.ShapeDtypeStruct(s, BF16) for s in shapes],
+        compiler_params=pltpu.CompilerParams(vmem_limit_bytes=8 << 20),
         name="pack_first",
-    )(idx, w_qkv, *vectors)
+    )(idx, *in_hbm(w_qkv, *vectors))
 
 
 def run_pack_second(idx, w_out, w_fc1, w_fc2):
@@ -175,11 +176,12 @@
             num_scalar_prefetch=1,
             grid=(1,),
             in_specs=[own_rows(part, width), own_rows(part, hidden), own_rows(hidden // 4, width)],
-            out_specs=pl.BlockSpec(shape, lambda i, idx: (0, 0)),
+            out_specs=VMEM_SPEC,
         ),
         out_shape=jax.ShapeDtypeStruct(shape, BF16),
+        compiler_params=pltpu.CompilerParams(vmem_limit_bytes=8 << 20),
         name="pack_second",
-    )(idx, w_out, w_fc1, w_fc2)
+    )(idx, *in_hbm(w_out, w_fc1, w_fc2))
 
 
 def load_view(source, raw, view, sem):
@@ -423,7 +425,7 @@
     def _():
         quarter = half // 4
         wide = hidden // 8
-        gw2_t = gw2[...].T
+        gw2_t = gw2[...].astype(BF16).T
         small_rows = [jnp.sum(gsmall[k], axis=0, keepdims=True) for k in range(4)]
 
         def emit(group, quad, ref, side):
@@ -435,7 +437,7 @@
                 ].astype(BF16)
                 top += quarter
             start = group * (hidden // 2) + quad * wide
-            ref[group, side, top : top + wide, :] = gw2_t[start : start + wide].astype(BF16)
+            ref[group, side, top : top + wide, :] = gw2_t[start : start + wide]
             top += wide
             ref[group, side, top : top + quarter, :] = gwo[base : base + quarter, :].astype(BF16)
             top += quarter

time: 157 us -> 155 us (0.987)
  Pallas kernels: 92.4 us -> 90.3 us
where the time goes in v6:
time: 155 us
  Pallas kernels  90.3 us (58%)
  waiting for transfers between devices  33.8 us (22%)
  starting transfers between devices  29.2 us (19%)
    ppermute x24, waiting for transfers between devices, flip(): return lax.ppermute(value, axis, [(i, i ^ bit) for i in range(size)])  33.8 us
    ppermute x24, starting transfers between devices, flip(): return lax.ppermute(value, axis, [(i, i ^ bit) for i in range(size)])  29.2 us
    pallas_call x1, Pallas kernels, run_mlp(): pl.pallas_call(mlp_kernel, grid=(micro,), in_specs=[SMEM_SPEC, SMEM_SPEC,...  26.7 us
    pallas_call x2, Pallas kernels, run_attention_back(): pl.pallas_call(partial(attention_back_kernel, begin, last), grid=(end - b...  19.9 us
    pallas_call x1, Pallas kernels, run_attention(): pl.pallas_call(partial(attention_kernel, seq), grid=(count // 2,), in_spe...  11.2 us
    pallas_call x2, Pallas kernels, run_prepare(): pl.pallas_call(kernel, grid=(count // 2,), in_specs=[HBM_SPEC], out_specs...  7.39 us
    pallas_call x1, Pallas kernels, run_outputs(): pl.pallas_call(outputs_kernel, grid=(count // 2,), in_specs=[SMEM_SPEC] +...  7.38 us
    pallas_call x1, Pallas kernels, run_input_grad(): pl.pallas_call(input_grad_kernel, grid=(count // 2,), in_specs=[HBM_SPEC]...  7.3 us
  transfers between devices with their start and end apart: 24, of which 7 were waited for; matrix products, arithmetic and copies ran while one was open for 0% of the time, Pallas kernels for 38%

profile of v6, /device:TPU:1, one launch (start us, length us, event | category | flops | bytes accessed | tf_op | source)
XLA Modules:
  0.0 154.6 jit_solution(776102347776015506)
XLA Ops:
  0.7 1.7 %pack_second.1 = bf16[96,3456]{1,0:T(8,128)(2,1)S(1)} custom-call(s32[4]{0:T(128)S(1)} %pad_add_fusion.idx_ref, bf16[192,384]{1,0:T(8,128)(2,1)} %wo_ref.3, bf16[192,1536]{1,0:T(8,128)(2,1)} %w1_ref.3, bf16[768,384]{1,0:T(8,128)(2,1)} %w2_ref.3), custom_call_target="tpu_custom_call" | custom-call | tf_op jit(solution)/shard_map/pack_second/pallas_call | solution.py:173
  2.4 2.1 %collective-permute-start.2 = (bf16[96,3456]{1,0:T(8,128)(2,1)S(1)}, bf16[96,3456]{1,0:T(8,128)(2,1)S(1)}, u32[]{:S(2)}, u32[]{:S(2)}) collective-permute-start(bf16[96,3456]{1,0:T(8,128)(2,1)S(1)} %pack_second.1), channel_id=1, source_target_pairs={{0,16},{16,0},{1,17},{17,1},{2,18},{18,2},{3,19},{19,3},{4,20},{20... | collective-permute-start | bytes 1990664 | tf_op jit(solution)/shard_map/ppermute | solution.py:810
  4.5 1.6 %pack_first.1 = (bf16[112,1152]{1,0:T(8,128)(2,1)S(1)}, bf16[8,768]{1,0:T(8,128)(2,1)S(1)}) custom-call(s32[4]{0:T(128)S(1)} %pad_add_fusion.idx_ref, bf16[192,1152]{1,0:T(8,128)(2,1)} %w_ref.1, bf16[384]{0:T(512)(128)(2,1)} %refs_0_.1, bf16[192]{0:T(256)(128)(2,1)} %refs_1_.1, bf16[768]{0:T(1024)(128)(2,1)} %refs_2_.1, bf16[192]{0:T(256)(128)(2,1)} %refs_3_.1, ...), custom_call_target="tpu_custom_call" | custom-call | tf_op jit(solution)/shard_map/pack_first/pallas_call | solution.py:154
  6.2 18.4 %collective-permute-done.near_ref = bf16[112,1152]{1,0:T(8,128)(2,1)S(1)} collective-permute-done((bf16[112,1152]{1,0:T(8,128)(2,1)S(1)}, bf16[112,1152]{1,0:T(8,128)(2,1)S(1)}, u32[]{:S(2)}, u32[]{:S(2)}) %collective-permute-start) | collective-permute-done | bytes 258080 | tf_op jit(solution)/shard_map/ppermute | solution.py:810
  26.0 3.2 %shard_map.255.cot_hbm = bf16[8,208,384]{2,1,0:T(8,128)(2,1)} custom-call(bf16[4728,128]{1,0:T(8,128)(2,1)} %bitcast.33), custom_call_target="tpu_custom_call" | custom-call | flops 268435456 | bytes 8388608 | tf_op jit(solution)/shard_map/pallas_call | solution.py:229
  29.2 4.2 %shard_map.254 = (bf16[8,208,384]{2,1,0:T(8,128)(2,1)}, f32[8,208,384]{2,1,0:T(8,128)}, f32[8,208,128]{2,1,0:T(8,128)}) custom-call(bf16[4728,128]{1,0:T(8,128)(2,1)} %bitcast.32), custom_call_target="tpu_custom_call" | custom-call | flops 268435456 | bytes 8388608 | tf_op jit(solution)/shard_map/pallas_call | solution.py:229
  33.5 11.2 %attention_fwd.1 = (bf16[8,208,1152]{2,1,0:T(8,128)(2,1)}, bf16[8,6,208,256]{3,2,1,0:T(8,128)(2,1)}, bf16[8,208,384]{2,1,0:T(8,128)(2,1)}, bf16[384,1152]{1,0:T(...) custom-call(s32[4]{0:T(128)S(1)} %pad_add_fusion.idx_ref, f32[8,208,384]{2,1,0:T(8,128)} %get-tuple-element.61.hat_hbm, ...), custom_call_target="tpu_custom_call" | custom-call | flops 5368709120 | bytes 20971520 | tf_op jit(solution)/shard_map/attention_fwd/pallas_call | solution.py:641
  44.7 26.7 %mlp_fwd_bwd.1 = (bf16[8,208,1536]{2,1,0:T(8,128)(2,1)}, f32[8,208,384]{2,1,0:T(8,128)}, bf16[8,208,384]{2,1,0:T(8,128)(2,1)}, bf16[8,208,384]{2,1,0:T(8,128)(2,...) custom-call(s32[4]{0:T(128)S(1)} %pad_add_fusion.idx_ref, ...), custom_call_target="tpu_custom_call" | custom-call | flops 12884901888 | bytes 20971520 | tf_op jit(solution)/shard_map/mlp_fwd_bwd/pallas_call | solution.py:677
  72.1 6.3 %shard_map.256 = (bf16[8,208,1152]{2,1,0:T(8,128)(2,1)}, f32[384,1152]{1,0:T(8,128)S(1)}, f32[8,1152]{1,0:T(8,128)S(1)}) custom-call(s32[4]{0:T(128)S(1)} %pad_add_fusion.idx_ref, f32[8,208,384]{2,1,0:T(8,128)} %get-tuple-element.61.hat_hbm, bf16[8,208,1152]{2,1,0:T(8,128)(2,1)} %get-tuple-element.71.qkv_hbm, ...), custom_call_target="tpu_custom_call" | custom-call | flops 2147483648 | bytes 20971520 | tf_op jit(solution)/shard_map/pallas_call | solution.py:724
  80.6 13.6 %shard_map.257 = (bf16[8,208,1152]{2,1,0:T(8,128)(2,1)}, f32[384,1152]{1,0:T(8,128)S(1)}, f32[8,1152]{1,0:T(8,128)S(1)}, bf16[2,2,160,384]{3,2,1,0:T(8,128)(2,1)S(1)}, bf16[2,2,160,384]{3,2,1,0:T(8,128)(2,1)S(1)}) custom-call(s32[4]{0:T(128)S(1)} %pad_add_fusion.idx_ref, ...), custom_call_target="tpu_custom_call", output_to_operand_aliasing={{0}: (8, {}), {1}: (9, {}), {2}: (10, {})} | custom-call | flops 6442450944 | bytes 20971520 | tf_op jit(solution)/shard_map/pallas_call | solution.py:724
  94.6 1.6 %collective-permute-done.13.b_ref = bf16[2,448,384]{2,1,0:T(8,128)(2,1)S(1)} collective-permute-done((bf16[2,448,384]{2,1,0:T(8,128)(2,1)S(1)}, bf16[2,448,384]{2,1,0:T(8,128)(2,1)S(1)}, u32[]{:S(2)}, u32[]{:S(2)}) %collective-permute-start.13) | collective-permute-done | bytes 688160 | tf_op jit(solution)/shard_map/ppermute | solution.py:810
  96.8 1.5 collective-permute-start.14
  100.2 5.4 %collective-permute-done.14 = bf16[448,384]{1,0:T(8,128)(2,1)S(1)} collective-permute-done((bf16[448,384]{1,0:T(8,128)(2,1)S(1)}, bf16[448,384]{1,0:T(8,128)(2,1)S(1)}, u32[]{:S(2)}, u32[]{:S(2)}) %collective-permute-start.14) | collective-permute-done | bytes 344096 | tf_op jit(solution)/shard_map/ppermute | solution.py:810
  106.2 1.6 %collective-permute-start.15 = (bf16[224,384]{1,0:T(8,128)(2,1)S(1)}, bf16[224,384]{1,0:T(8,128)(2,1)S(1)}, u32[]{:S(2)}, u32[]{:S(2)}) collective-permute-start(bf16[224,384]{1,0:T(8,128)(2,1)S(1)} %get-tuple-element.95), channel_id=1, source_target_pairs={{0,4},{1,5},{2,6},{3,7},{4,0},{5,1},{6,2},{7,3},{8,12},{9,13},{10,... | collective-permute-start | bytes 516104 | tf_op jit(solution)/shard_map/ppermute | solution.py:810
  110.7 2.5 %collective-permute-start.16 = (bf16[224,384]{1,0:T(8,128)(2,1)S(1)}, bf16[224,384]{1,0:T(8,128)(2,1)S(1)}, u32[]{:S(2)}, u32[]{:S(2)}) collective-permute-start(bf16[224,384]{1,0:T(8,128)(2,1)S(1)} %add.18), channel_id=1, source_target_pairs={{0,8},{1,9},{2,10},{3,11},{4,12},{5,13},{6,14},{7,15},{8,0},{9,1},... | collective-permute-start | bytes 516104 | tf_op jit(solution)/shard_map/ppermute | solution.py:810
  114.6 4.1 %collective-permute-done.16 = bf16[224,384]{1,0:T(8,128)(2,1)S(1)} collective-permute-done((bf16[224,384]{1,0:T(8,128)(2,1)S(1)}, bf16[224,384]{1,0:T(8,128)(2,1)S(1)}, u32[]{:S(2)}, u32[]{:S(2)}) %collective-permute-start.16) | collective-permute-done | bytes 172064 | tf_op jit(solution)/shard_map/ppermute | solution.py:810
  118.7 1.9 %collective-permute-start.17 = (bf16[224,384]{1,0:T(8,128)(2,1)S(1)}, bf16[224,384]{1,0:T(8,128)(2,1)S(1)}, u32[]{:S(2)}, u32[]{:S(2)}) collective-permute-start(bf16[224,384]{1,0:T(8,128)(2,1)S(1)} %add.19.refs_0_), channel_id=1, source_target_pairs={{0,4},{1,5},{2,6},{3,7},{4,0},{5,1},{6,2},{7,3},{8,12},{9,13},{10,... | collective-permute-start | bytes 516104 | tf_op jit(solution)/shard_map/ppermute | solution.py:810
  120.7 3.3 %collective-permute-start.8 = (bf16[160,384]{1,0:T(8,128)(2,1)S(1)}, bf16[160,384]{1,0:T(8,128)(2,1)S(1)}, u32[]{:S(2)}, u32[]{:S(2)}) collective-permute-start(bf16[160,384]{1,0:T(8,128)(2,1)S(1)} %add.16), channel_id=1, source_target_pairs={{0,8},{1,9},{2,10},{3,11},{4,12},{5,13},{6,14},{7,15},{8,0},{9,1},... | collective-permute-start | bytes 368648 | tf_op jit(solution)/shard_map/ppermute | solution.py:810
  124.0 2.9 %collective-permute-done.8 = bf16[160,384]{1,0:T(8,128)(2,1)S(1)} collective-permute-done((bf16[160,384]{1,0:T(8,128)(2,1)S(1)}, bf16[160,384]{1,0:T(8,128)(2,1)S(1)}, u32[]{:S(2)}, u32[]{:S(2)}) %collective-permute-start.8) | collective-permute-done | bytes 122912 | tf_op jit(solution)/shard_map/ppermute | solution.py:810
  126.9 3.3 %collective-permute-start.10 = (bf16[160,384]{1,0:T(8,128)(2,1)S(1)}, bf16[160,384]{1,0:T(8,128)(2,1)S(1)}, u32[]{:S(2)}, u32[]{:S(2)}) collective-permute-start(bf16[160,384]{1,0:T(8,128)(2,1)S(1)} %add.17.refs_0_), channel_id=1, source_target_pairs={{0,1},{1,0},{2,3},{3,2},{4,5},{5,4},{6,7},{7,6},{8,9},{9,8},{10,11... | collective-permute-start | bytes 368648 | tf_op jit(solution)/shard_map/ppermute | solution.py:810
  132.9 7.4 %layer_outputs.1 = bf16[4728,128]{1,0:T(8,128)(2,1)} custom-call(s32[4,1]{1,0:T(4,128)S(1)} %copy.33.count_ref, bf16[8,208,1536]{2,1,0:T(8,128)(2,1)} %get-tuple-element.67.act_hbm, f32[8,208,384]{2,1,0:T(8,128)} %get-tuple-element.68.middle_hbm, bf16[1536,384]{1,0:T(8,128)(2,1)S(1)} %get-tuple-element.69.w2_ref, f32[8,384]{1,0:T(8,128)S(1)} %get-tuple-element.65.vec.vec_ref), custom_call_target="tpu_custom_call" | custom-call | flops 2147483648 | bytes 20971520 | tf_op jit(solution)/shard_map/layer_outputs/pallas_call | solution.py:776
  143.3 7.3 %input_grad.1 = bf16[4728,128]{1,0:T(8,128)(2,1)} custom-call(f32[8,208,384]{2,1,0:T(8,128)} %get-tuple-element.61.hat_hbm, f32[8,208,128]{2,1,0:T(8,128)} %get-tuple-element.70.rstd_hbm, bf16[8,208,1152]{2,1,0:T(8,128)(2,1)} %get-tuple-element.78.dqkv_hbm, bf16[8,208,384]{2,1,0:T(8,128)(2,1)} %get-tuple-element.79.dx_hbm, ...), custom_call_target="tpu_custom_call" | custom-call | flops 2147483648 | bytes 20971520 | tf_op jit(solution)/shard_map/input_grad/pallas_call | solution.py:755
  150.6 1.6 %shard_map.260 = (f32[192,1152]{1,0:T(8,128)}, f32[384]{0:T(512)}, f32[192]{0:T(256)}, f32[192]{0:T(256)}) custom-call(s32[4]{0:T(128)S(1)} %pad_add_fusion.idx_ref, bf16[160,384]{1,0:T(8,128)(2,1)S(1)} %add.17.refs_0_, bf16[160,384]{1,0:T(8,128)(2,1)S(1)} %collective-permute-done.9.refs_1_, bf16[160,384]{1,0:T(8,128)(2,1)S(1)} %collective-permute-done.10.refs_2_, ...), custom_call_target="tpu_custom_call" | custom-call | tf_op jit(solution)/shard_map/pallas_call | solution.py:908
  152.3 2.4 %shard_map.264 = (f32[192,384]{1,0:T(8,128)}, f32[192]{0:T(256)}, f32[192,1536]{1,0:T(8,128)}, f32[768]{0:T(1024)}, f32[768,384]{1,0:T(8,128)}, /*index=5*/f32[192]{0:T(256)}, f32[192]{0:T(256)}, f32[192]{0:T(256)}) custom-call(s32[4]{0:T(128)S(1)} %pad_add_fusion.idx_ref, bf16[224,384]{1,0:T(8,128)(2,1)S(1)} %add.19.refs_0_, ...), custom_call_target="tpu_custom_call" | custom-call | tf_op jit(solution)/shard_map/pallas_call | solution.py:908
  (58 shorter events, 17.9 us)
Async XLA Ops:
  2.4 23.5 %collective-permute-start.2 = (bf16[96,3456]{1,0:T(8,128)(2,1)S(1)}, bf16[96,3456]{1,0:T(8,128)(2,1)S(1)}, u32[]{:S(2)}, u32[]{:S(2)}) collective-permute-start(bf16[96,3456]{1,0:T(8,128)(2,1)S(1)} %pack_second.1), channel_id=1, source_target_pairs={{0,16},{16,0},{1,17},{17,1},{2,18},{18,2},{3,19},{19,3},{4,20},{20... | collective-permute-start | bytes 1990664 | tf_op jit(solution)/shard_map/ppermute | solution.py:810
  6.1 18.5 %collective-permute-start = (bf16[112,1152]{1,0:T(8,128)(2,1)S(1)}, bf16[112,1152]{1,0:T(8,128)(2,1)S(1)}, u32[]{:S(2)}, u32[]{:S(2)}) collective-permute-start(bf16[112,1152]{1,0:T(8,128)(2,1)S(1)} %get-tuple-element.62), channel_id=1, source_target_pairs={{0,16},{16,0},{1,17},{17,1},{2,18},{18,2},{3,19},{19,3},{4,20},{20... | collective-permute-start | bytes 774152 | tf_op jit(solution)/shard_map/ppermute | solution.py:810
  24.7 8.8 %collective-permute-start.1 = (bf16[112,1152]{1,0:T(8,128)(2,1)S(1)}, bf16[112,1152]{1,0:T(8,128)(2,1)S(1)}, u32[]{:S(2)}, u32[]{:S(2)}) collective-permute-start(bf16[112,1152]{1,0:T(8,128)(2,1)S(1)} %collective-permute-done.near_ref), channel_id=1, source_target_pairs={{0,1},{1,0},{2,3},{3,2},{4,5},{5,4},{6,7},{7,6},{8,9},{9,8},{10,11... | collective-permute-start | bytes 774152 | tf_op jit(solution)/shard_map/ppermute | solution.py:810
  25.9 18.8 %collective-permute-start.3 = (bf16[96,3456]{1,0:T(8,128)(2,1)S(1)}, bf16[96,3456]{1,0:T(8,128)(2,1)S(1)}, u32[]{:S(2)}, u32[]{:S(2)}) collective-permute-start(bf16[96,3456]{1,0:T(8,128)(2,1)S(1)} %collective-permute-done.2.near_ref), channel_id=1, source_target_pairs={{0,1},{1,0},{2,3},{3,2},{4,5},{5,4},{6,7},{7,6},{8,9},{9,8},{10,11... | collective-permute-start | bytes 1990664 | tf_op jit(solution)/shard_map/ppermute | solution.py:810
  71.5 6.8 %collective-permute-start.12 = (bf16[2,2,448,384]{3,2,1,0:T(8,128)(2,1)S(1)}, bf16[2,2,448,384]{3,2,1,0:T(8,128)(2,1)S(1)}, u32[]{:S(2)}, u32[]{:S(2)}) collective-permute-start(bf16[2,2,448,384]{3,2,1,0:T(8,128)(2,1)S(1)} %get-tuple-element.89), channel_id=1, source_target_pairs={{0,1},{1,0},{2,3},{3,2},{4,5},{5,4},{6,7},{7,6},{8,9},{9,8},{10,11... | collective-permute-start | bytes 4128776 | tf_op jit(solution)/shard_map/ppermute | solution.py:810
  79.1 17.1 %collective-permute-start.13 = (bf16[2,448,384]{2,1,0:T(8,128)(2,1)S(1)}, bf16[2,448,384]{2,1,0:T(8,128)(2,1)S(1)}, u32[]{:S(2)}, u32[]{:S(2)}) collective-permute-start(bf16[2,448,384]{2,1,0:T(8,128)(2,1)S(1)} %get-tuple-element.91), channel_id=1, source_target_pairs={{0,16},{16,0},{1,17},{17,1},{2,18},{18,2},{3,19},{19,3},{4,20},{20... | collective-permute-start | bytes 2064392 | tf_op jit(solution)/shard_map/ppermute | solution.py:810
  94.2 4.1 %collective-permute-start.4 = (bf16[2,2,160,384]{3,2,1,0:T(8,128)(2,1)S(1)}, bf16[2,2,160,384]{3,2,1,0:T(8,128)(2,1)S(1)}, u32[]{:S(2)}, u32[]{:S(2)}) collective-permute-start(bf16[2,2,160,384]{3,2,1,0:T(8,128)(2,1)S(1)} %get-tuple-element.81), channel_id=1, source_target_pairs={{0,1},{1,0},{2,3},{3,2},{4,5},{5,4},{6,7},{7,6},{8,9},{9,8},{10,11... | collective-permute-start | bytes 1474568 | tf_op jit(solution)/shard_map/ppermute | solution.py:810
  96.8 8.9 %collective-permute-start.14 = (bf16[448,384]{1,0:T(8,128)(2,1)S(1)}, bf16[448,384]{1,0:T(8,128)(2,1)S(1)}, u32[]{:S(2)}, u32[]{:S(2)}) collective-permute-start(bf16[448,384]{1,0:T(8,128)(2,1)S(1)} %get-tuple-element.93), channel_id=1, source_target_pairs={{0,2},{1,3},{2,0},{3,1},{4,6},{5,7},{6,4},{7,5},{8,10},{9,11},{10,... | collective-permute-start | bytes 1032200 | tf_op jit(solution)/shard_map/ppermute | solution.py:810
  99.0 8.9 %collective-permute-start.5 = (bf16[2,160,384]{2,1,0:T(8,128)(2,1)S(1)}, bf16[2,160,384]{2,1,0:T(8,128)(2,1)S(1)}, u32[]{:S(2)}, u32[]{:S(2)}) collective-permute-start(bf16[2,160,384]{2,1,0:T(8,128)(2,1)S(1)} %get-tuple-element.83), channel_id=1, source_target_pairs={{0,16},{16,0},{1,17},{17,1},{2,18},{18,2},{3,19},{19,3},{4,20},{20... | collective-permute-start | bytes 737288 | tf_op jit(solution)/shard_map/ppermute | solution.py:810
  106.2 4.4 %collective-permute-start.15 = (bf16[224,384]{1,0:T(8,128)(2,1)S(1)}, bf16[224,384]{1,0:T(8,128)(2,1)S(1)}, u32[]{:S(2)}, u32[]{:S(2)}) collective-permute-start(bf16[224,384]{1,0:T(8,128)(2,1)S(1)} %get-tuple-element.95), channel_id=1, source_target_pairs={{0,4},{1,5},{2,6},{3,7},{4,0},{5,1},{6,2},{7,3},{8,12},{9,13},{10,... | collective-permute-start | bytes 516104 | tf_op jit(solution)/shard_map/ppermute | solution.py:810
  108.4 4.8 %collective-permute-start.6 = (bf16[160,384]{1,0:T(8,128)(2,1)S(1)}, bf16[160,384]{1,0:T(8,128)(2,1)S(1)}, u32[]{:S(2)}, u32[]{:S(2)}) collective-permute-start(bf16[160,384]{1,0:T(8,128)(2,1)S(1)} %get-tuple-element.85), channel_id=1, source_target_pairs={{0,2},{1,3},{2,0},{3,1},{4,6},{5,7},{6,4},{7,5},{8,10},{9,11},{10,... | collective-permute-start | bytes 368648 | tf_op jit(solution)/shard_map/ppermute | solution.py:810
  110.7 8.0 %collective-permute-start.16 = (bf16[224,384]{1,0:T(8,128)(2,1)S(1)}, bf16[224,384]{1,0:T(8,128)(2,1)S(1)}, u32[]{:S(2)}, u32[]{:S(2)}) collective-permute-start(bf16[224,384]{1,0:T(8,128)(2,1)S(1)} %add.18), channel_id=1, source_target_pairs={{0,8},{1,9},{2,10},{3,11},{4,12},{5,13},{6,14},{7,15},{8,0},{9,1},... | collective-permute-start | bytes 516104 | tf_op jit(solution)/shard_map/ppermute | solution.py:810
  113.2 7.4 %collective-permute-start.7 = (bf16[160,384]{1,0:T(8,128)(2,1)S(1)}, bf16[160,384]{1,0:T(8,128)(2,1)S(1)}, u32[]{:S(2)}, u32[]{:S(2)}) collective-permute-start(bf16[160,384]{1,0:T(8,128)(2,1)S(1)} %add.15), channel_id=1, source_target_pairs={{0,4},{1,5},{2,6},{3,7},{4,0},{5,1},{6,2},{7,3},{8,12},{9,13},{10,... | collective-permute-start | bytes 368648 | tf_op jit(solution)/shard_map/ppermute | solution.py:810
  118.7 13.0 %collective-permute-start.17 = (bf16[224,384]{1,0:T(8,128)(2,1)S(1)}, bf16[224,384]{1,0:T(8,128)(2,1)S(1)}, u32[]{:S(2)}, u32[]{:S(2)}) collective-permute-start(bf16[224,384]{1,0:T(8,128)(2,1)S(1)} %add.19.refs_0_), channel_id=1, source_target_pairs={{0,4},{1,5},{2,6},{3,7},{4,0},{5,1},{6,2},{7,3},{8,12},{9,13},{10,... | collective-permute-start | bytes 516104 | tf_op jit(solution)/shard_map/ppermute | solution.py:810
  120.7 6.2 %collective-permute-start.8 = (bf16[160,384]{1,0:T(8,128)(2,1)S(1)}, bf16[160,384]{1,0:T(8,128)(2,1)S(1)}, u32[]{:S(2)}, u32[]{:S(2)}) collective-permute-start(bf16[160,384]{1,0:T(8,128)(2,1)S(1)} %add.16), channel_id=1, source_target_pairs={{0,8},{1,9},{2,10},{3,11},{4,12},{5,13},{6,14},{7,15},{8,0},{9,1},... | collective-permute-start | bytes 368648 | tf_op jit(solution)/shard_map/ppermute | solution.py:810
  126.9 14.5 %collective-permute-start.10 = (bf16[160,384]{1,0:T(8,128)(2,1)S(1)}, bf16[160,384]{1,0:T(8,128)(2,1)S(1)}, u32[]{:S(2)}, u32[]{:S(2)}) collective-permute-start(bf16[160,384]{1,0:T(8,128)(2,1)S(1)} %add.17.refs_0_), channel_id=1, source_target_pairs={{0,1},{1,0},{2,3},{3,2},{4,5},{5,4},{6,7},{7,6},{8,9},{9,8},{10,11... | collective-permute-start | bytes 368648 | tf_op jit(solution)/shard_map/ppermute | solution.py:810
  130.2 10.1 %collective-permute-start.9 = (bf16[160,384]{1,0:T(8,128)(2,1)S(1)}, bf16[160,384]{1,0:T(8,128)(2,1)S(1)}, u32[]{:S(2)}, u32[]{:S(2)}) collective-permute-start(bf16[160,384]{1,0:T(8,128)(2,1)S(1)} %add.17.refs_0_), channel_id=1, source_target_pairs={{0,2},{1,3},{2,0},{3,1},{4,6},{5,7},{6,4},{7,5},{8,10},{9,11},{10,... | collective-permute-start | bytes 368648 | tf_op jit(solution)/shard_map/ppermute | solution.py:810
  131.5 10.4 %collective-permute-start.18 = (bf16[224,384]{1,0:T(8,128)(2,1)S(1)}, bf16[224,384]{1,0:T(8,128)(2,1)S(1)}, u32[]{:S(2)}, u32[]{:S(2)}) collective-permute-start(bf16[224,384]{1,0:T(8,128)(2,1)S(1)} %add.19.refs_0_), channel_id=1, source_target_pairs={{0,2},{1,3},{2,0},{3,1},{4,6},{5,7},{6,4},{7,5},{8,10},{9,11},{10,... | collective-permute-start | bytes 516104 | tf_op jit(solution)/shard_map/ppermute | solution.py:810
  131.7 10.7 %collective-permute-start.19 = (bf16[224,384]{1,0:T(8,128)(2,1)S(1)}, bf16[224,384]{1,0:T(8,128)(2,1)S(1)}, u32[]{:S(2)}, u32[]{:S(2)}) collective-permute-start(bf16[224,384]{1,0:T(8,128)(2,1)S(1)} %collective-permute-done.17.refs_1_), channel_id=1, source_target_pairs={{0,2},{1,3},{2,0},{3,1},{4,6},{5,7},{6,4},{7,5},{8,10},{9,11},{10,... | collective-permute-start | bytes 516104 | tf_op jit(solution)/shard_map/ppermute | solution.py:810
  140.3 10.3 %collective-permute-start.11 = (bf16[160,384]{1,0:T(8,128)(2,1)S(1)}, bf16[160,384]{1,0:T(8,128)(2,1)S(1)}, u32[]{:S(2)}, u32[]{:S(2)}) collective-permute-start(bf16[160,384]{1,0:T(8,128)(2,1)S(1)} %collective-permute-done.9.refs_1_), channel_id=1, source_target_pairs={{0,1},{1,0},{2,3},{3,2},{4,5},{5,4},{6,7},{7,6},{8,9},{9,8},{10,11... | collective-permute-start | bytes 368648 | tf_op jit(solution)/shard_map/ppermute | solution.py:810
  141.3 10.9 %collective-permute-start.20 = (bf16[224,384]{1,0:T(8,128)(2,1)S(1)}, bf16[224,384]{1,0:T(8,128)(2,1)S(1)}, u32[]{:S(2)}, u32[]{:S(2)}) collective-permute-start(bf16[224,384]{1,0:T(8,128)(2,1)S(1)} %add.19.refs_0_), channel_id=1, source_target_pairs={{0,1},{1,0},{2,3},{3,2},{4,5},{5,4},{6,7},{7,6},{8,9},{9,8},{10,11... | collective-permute-start | bytes 516104 | tf_op jit(solution)/shard_map/ppermute | solution.py:810
  141.4 10.8 %collective-permute-start.21 = (bf16[224,384]{1,0:T(8,128)(2,1)S(1)}, bf16[224,384]{1,0:T(8,128)(2,1)S(1)}, u32[]{:S(2)}, u32[]{:S(2)}) collective-permute-start(bf16[224,384]{1,0:T(8,128)(2,1)S(1)} %collective-permute-done.17.refs_1_), channel_id=1, source_target_pairs={{0,1},{1,0},{2,3},{3,2},{4,5},{5,4},{6,7},{7,6},{8,9},{9,8},{10,11... | collective-permute-start | bytes 516104 | tf_op jit(solution)/shard_map/ppermute | solution.py:810
  141.8 10.4 %collective-permute-start.22 = (bf16[224,384]{1,0:T(8,128)(2,1)S(1)}, bf16[224,384]{1,0:T(8,128)(2,1)S(1)}, u32[]{:S(2)}, u32[]{:S(2)}) collective-permute-start(bf16[224,384]{1,0:T(8,128)(2,1)S(1)} %collective-permute-done.18.refs_2_), channel_id=1, source_target_pairs={{0,1},{1,0},{2,3},{3,2},{4,5},{5,4},{6,7},{7,6},{8,9},{9,8},{10,11... | collective-permute-start | bytes 516104 | tf_op jit(solution)/shard_map/ppermute | solution.py:810
  142.4 9.9 %collective-permute-start.23 = (bf16[224,384]{1,0:T(8,128)(2,1)S(1)}, bf16[224,384]{1,0:T(8,128)(2,1)S(1)}, u32[]{:S(2)}, u32[]{:S(2)}) collective-permute-start(bf16[224,384]{1,0:T(8,128)(2,1)S(1)} %collective-permute-done.19.refs_3_), channel_id=1, source_target_pairs={{0,1},{1,0},{2,3},{3,2},{4,5},{5,4},{6,7},{7,6},{8,9},{9,8},{10,11... | collective-permute-start | bytes 516104 | tf_op jit(solution)/shard_map/ppermute | solution.py:810
  (5 other events, 66.5 us)
